TPU v7x, 256 devices: a whole 4x4x8 slice. The times are simulated.
256 devices in a mesh: prompt: 8 (over y, z_hi), wide: 32 (over x, z_lo, core).
Axes of the slice: x: 4, y: 4, z: 8 (z_hi: 2, z_lo: 4; z = z_hi * 4 + z_lo), core: 2. Of those that a mesh axis runs over, the one named last changes fastest.
Arguments:
- candidate_hidden: bfloat16 [8, 4096, 4096], P('prompt', 'wide'), may hold values from -6 to 6
- frozen_query: bfloat16 [8, 4096, 4096], P('prompt', 'wide'), may hold values from -12 to 12
- candidate_key_value: bfloat16 [8, 4096, 2048], P('prompt', 'wide'), may hold values from -6 to 6
- prompt_key_value: bfloat16 [8, 2048, 2048], P('prompt', 'wide'), may hold values from -12 to 12
- candidate_adapter: int32 [8, 32], P('prompt'), may hold values from 0 to 15
- prompt_block_end: int32 [8, 32], P('prompt', 'wide'), may hold values from 1 to 16, as said below
- adapter_down: bfloat16 [16, 4, 16, 4096], P(None, None, None, 'wide'), may hold values from -0.09375 to 0.09375
- adapter_up: bfloat16 [16, 2, 16, 4096], P(None, None, None, 'wide'), may hold values from -0.625 to 0.625
- adapter_up_key_value: bfloat16 [16, 2, 16, 1024], P(None, None, None, 'wide'), may hold values from -0.625 to 0.625
- output_cotangent: bfloat16 [8, 4096, 4096], P('prompt', 'wide'), may hold values from -0.03125 to 0.03125
- context_cotangent: bfloat16 [8, 4096, 4096], P('prompt', 'wide'), may hold values from -0.03125 to 0.03125
Outputs:
- down_gradient: float32 [16, 4, 16, 4096], P(None, None, None, 'wide')
- up_gradient: float32 [16, 2, 16, 4096], P(None, None, None, 'wide')
- key_value_up_gradient: float32 [16, 2, 16, 1024], P(None, None, None, 'wide')
Inputs may be any that keep to these rules, and one draw needn't show every extreme that they name: `prompt_block_end`: the first block of every group sees the whole prompt.
All inputs are finite; a program needn't handle non-finite values.
Results may differ from a plain program's by a relative error of at most 0.02.
Values may be sent and summed in bfloat16 or wider, within the bound.
No kernel may reach another device: no remote copies, remote signals or barrier semaphores. Data moves between devices by JAX's collectives and lax.ppermute only.
A program may use at most 192 MiB of HBM per device.

v0:
```python
import jax
import jax.numpy as jnp
from jax import lax
from jax.sharding import PartitionSpec as P

HEADS = 32
KV_HEADS = 8
HEAD_DIM = 128
ADAPTER_COUNT = 16
BLOCK_TOKENS = 128


adapter_scale = 2.0
masked_score = -1e30


def split_heads(rows):
    return rows.reshape(rows.shape[0], KV_HEADS, HEADS // KV_HEADS, HEAD_DIM)


def score_rows(query_vectors, key_rows, visible):
    key_heads = key_rows.reshape(key_rows.shape[0], KV_HEADS, HEAD_DIM)
    scores = jnp.einsum(
        "bkgd,jkd->kgbj", split_heads(query_vectors), key_heads, preferred_element_type=jnp.float32
    ) * HEAD_DIM ** (-0.5)
    return jnp.where(visible, scores, masked_score)


def forward_update(row_peak, row_total, weighted, query_vectors, key_rows, value_rows, visible):
    scores = score_rows(query_vectors, key_rows, visible)
    new_peak = jnp.maximum(row_peak, jnp.max(scores, axis=-1))
    exponent = jnp.where(visible, jnp.exp(scores - new_peak[..., None]), 0.0)
    rescale = jnp.exp(row_peak - new_peak)
    value_heads = value_rows.reshape(value_rows.shape[0], KV_HEADS, HEAD_DIM)
    increment = jnp.einsum(
        "kgbj,jkd->bkgd",
        exponent.astype(jnp.bfloat16),
        value_heads,
        preferred_element_type=jnp.float32,
    )
    weighted = weighted * jnp.transpose(rescale, (2, 0, 1))[..., None] + increment
    row_total = row_total * rescale + jnp.sum(exponent, axis=-1)
    return (new_peak, row_total, weighted)


def backward_terms(
    query_vectors, key_rows, value_rows, visible, row_peak, row_total, context_grad, row_delta
):
    scores = score_rows(query_vectors, key_rows, visible)
    attention = (
        jnp.where(visible, jnp.exp(scores - row_peak[..., None]), 0.0) / row_total[..., None]
    )
    value_heads = value_rows.reshape(value_rows.shape[0], KV_HEADS, HEAD_DIM)
    attention_grad = jnp.einsum(
        "bkgd,jkd->kgbj", split_heads(context_grad), value_heads, preferred_element_type=jnp.float32
    )
    score_grad = (attention * (attention_grad - row_delta[..., None])).astype(jnp.bfloat16)
    return (attention, score_grad)


def body(
    candidate_hidden,
    frozen_query,
    candidate_key_value,
    prompt_key_value,
    candidate_adapter,
    prompt_block_end,
    adapter_down,
    adapter_up,
    adapter_up_key_value,
    output_cotangent,
    context_cotangent,
):
    position = lax.axis_index("wide")
    candidate_blocks = prompt_block_end.shape[1]
    model_width = candidate_hidden.shape[2]
    key_value_width = KV_HEADS * HEAD_DIM
    head_groups = HEADS // KV_HEADS
    inverse_root = HEAD_DIM ** (-0.5)
    group_ids = candidate_adapter[0]
    own_ids = lax.dynamic_slice_in_dim(group_ids, position * candidate_blocks, candidate_blocks)
    whole_a, whole_b, whole_pairs = (
        lax.all_gather(adapter_down, "wide", axis=3, tiled=True),
        lax.all_gather(adapter_up, "wide", axis=3, tiled=True),
        lax.all_gather(adapter_up_key_value, "wide", axis=3, tiled=True),
    )
    down_matrices = whole_a[own_ids]
    up_model_matrix = whole_b[own_ids]
    up_matrix_pairs = whole_pairs[own_ids]
    x_blocks = candidate_hidden[0].reshape(candidate_blocks, BLOCK_TOKENS, model_width)
    rank_projection = jnp.einsum(
        "cbd,cprd->cprb", x_blocks, down_matrices[:, :3], preferred_element_type=jnp.float32
    ).astype(jnp.bfloat16)
    query_adapter_delta = jnp.einsum(
        "crb,crd->cbd",
        rank_projection[:, 0],
        up_model_matrix[:, 0],
        preferred_element_type=jnp.float32,
    )
    query_vectors = (
        frozen_query[0].reshape(candidate_blocks, BLOCK_TOKENS, model_width).astype(jnp.float32)
        + adapter_scale * query_adapter_delta
    ).astype(jnp.bfloat16)
    key_value_delta = jnp.einsum(
        "cprb,cprd->cbpd",
        rank_projection[:, 1:],
        up_matrix_pairs,
        preferred_element_type=jnp.float32,
    ).reshape(candidate_blocks, BLOCK_TOKENS, 2 * key_value_width)
    candidate_own_key_value = (
        candidate_key_value[0]
        .reshape(candidate_blocks, BLOCK_TOKENS, 2 * key_value_width)
        .astype(jnp.float32)
        + adapter_scale * key_value_delta
    ).astype(jnp.bfloat16)
    limits = prompt_block_end[0] * BLOCK_TOKENS
    causal = jnp.arange(BLOCK_TOKENS)[None, :] <= jnp.arange(BLOCK_TOKENS)[:, None]
    start_state = (
        jnp.full(
            (candidate_blocks, KV_HEADS, head_groups, BLOCK_TOKENS), masked_score, jnp.float32
        ),
        jnp.zeros((candidate_blocks, KV_HEADS, head_groups, BLOCK_TOKENS), jnp.float32),
        jnp.zeros((candidate_blocks, BLOCK_TOKENS, KV_HEADS, head_groups, HEAD_DIM), jnp.float32),
    )
    gathered = lax.all_gather(prompt_key_value, "wide", axis=1, tiled=True)
    piece_rows = gathered[0]
    piece_len = piece_rows.shape[0]
    key_position = jnp.arange(piece_len)[None, :]
    peak_list = []
    total_list = []
    weighted_list = []
    block_index = 0
    visible = jnp.broadcast_to(key_position < limits[block_index], (BLOCK_TOKENS, piece_len))
    result = forward_update(
        start_state[0][block_index],
        start_state[1][block_index],
        start_state[2][block_index],
        query_vectors[block_index],
        piece_rows[:, :key_value_width],
        piece_rows[:, key_value_width:],
        visible,
    )
    peak_list.append(result[0])
    total_list.append(result[1])
    weighted_list.append(result[2])
    prompt_state = (jnp.stack(peak_list), jnp.stack(total_list), jnp.stack(weighted_list))
    peak_list, total_list, weighted_list = ([], [], [])
    block_index = 0
    result = forward_update(
        prompt_state[0][block_index],
        prompt_state[1][block_index],
        prompt_state[2][block_index],
        query_vectors[block_index],
        candidate_own_key_value[block_index][:, :key_value_width],
        candidate_own_key_value[block_index][:, key_value_width:],
        causal,
    )
    peak_list.append(result[0])
    total_list.append(result[1])
    weighted_list.append(result[2])
    final_peak = jnp.stack(peak_list)
    final_total = jnp.stack(total_list)
    weighted = jnp.stack(weighted_list)
    context = (
        (weighted / jnp.transpose(final_total, (0, 3, 1, 2))[..., None])
        .astype(jnp.bfloat16)
        .reshape(candidate_blocks, BLOCK_TOKENS, model_width)
    )
    output_gradients = output_cotangent[0].reshape(candidate_blocks, BLOCK_TOKENS, model_width)
    output_rank_rows = jnp.einsum(
        "cbd,crd->crb", context, down_matrices[:, 3], preferred_element_type=jnp.float32
    ).astype(jnp.bfloat16)
    up_output_matrix = (
        adapter_scale
        * jnp.einsum(
            "cbd,crd->crb",
            output_gradients,
            up_model_matrix[:, 1],
            preferred_element_type=jnp.float32,
        )
    ).astype(jnp.bfloat16)
    up_gradient_result = adapter_scale * jnp.einsum(
        "crb,cbd->crd", output_rank_rows, output_gradients, preferred_element_type=jnp.float32
    )
    grad_a_out = jnp.einsum(
        "crb,cbd->crd", up_output_matrix, context, preferred_element_type=jnp.float32
    )
    context_grad = (
        context_cotangent[0]
        .reshape(candidate_blocks, BLOCK_TOKENS, model_width)
        .astype(jnp.float32)
        + jnp.einsum(
            "crb,crd->cbd",
            up_output_matrix,
            down_matrices[:, 3],
            preferred_element_type=jnp.float32,
        )
    ).astype(jnp.bfloat16)
    head_shape = (candidate_blocks, BLOCK_TOKENS, KV_HEADS, head_groups, HEAD_DIM)
    row_delta = jnp.transpose(
        jnp.sum(
            context_grad.astype(jnp.float32).reshape(head_shape)
            * context.astype(jnp.float32).reshape(head_shape),
            axis=-1,
        ),
        (0, 2, 3, 1),
    )
    piece_rows = gathered[0]
    piece_len = piece_rows.shape[0]
    key_position = jnp.arange(piece_len)[None, :]
    key_heads = piece_rows[:, :key_value_width].reshape(piece_len, KV_HEADS, HEAD_DIM)
    block_index = 0
    visible = jnp.broadcast_to(key_position < limits[block_index], (BLOCK_TOKENS, piece_len))
    attention, score_grad = backward_terms(
        query_vectors[block_index],
        piece_rows[:, :key_value_width],
        piece_rows[:, key_value_width:],
        visible,
        final_peak[block_index],
        final_total[block_index],
        context_grad[block_index],
        row_delta[block_index],
    )
    updated = [
        jnp.einsum("kgbj,jkd->bkgd", score_grad, key_heads, preferred_element_type=jnp.float32)
        * inverse_root
    ]
    prompt_grads = jnp.stack(updated)
    query_list, pair_list = ([], [])
    block_index = 0
    own_keys = candidate_own_key_value[block_index][:, :key_value_width]
    attention, score_grad = backward_terms(
        query_vectors[block_index],
        own_keys,
        candidate_own_key_value[block_index][:, key_value_width:],
        causal,
        final_peak[block_index],
        final_total[block_index],
        context_grad[block_index],
        row_delta[block_index],
    )
    own_key_heads = own_keys.reshape(BLOCK_TOKENS, KV_HEADS, HEAD_DIM)
    query_full = (
        prompt_grads[block_index]
        + jnp.einsum(
            "kgbj,jkd->bkgd", score_grad, own_key_heads, preferred_element_type=jnp.float32
        )
        * inverse_root
    )
    query_list.append(query_full.reshape(BLOCK_TOKENS, model_width).astype(jnp.bfloat16))
    key_grad = (
        jnp.einsum(
            "kgbj,bkgd->jkd",
            score_grad,
            split_heads(query_vectors[block_index]),
            preferred_element_type=jnp.float32,
        )
        * inverse_root
    )
    value_grad = jnp.einsum(
        "kgbj,bkgd->jkd",
        attention.astype(jnp.bfloat16),
        split_heads(context_grad[block_index]),
        preferred_element_type=jnp.float32,
    )
    pair_list.append(
        jnp.stack(
            [
                key_grad.reshape(BLOCK_TOKENS, key_value_width),
                value_grad.reshape(BLOCK_TOKENS, key_value_width),
            ],
            axis=1,
        ).astype(jnp.bfloat16)
    )
    query_gradient = jnp.stack(query_list)
    key_value_gradient = jnp.stack(pair_list)
    up_query_matrix = (
        adapter_scale
        * jnp.einsum(
            "cbd,crd->crb",
            query_gradient,
            up_model_matrix[:, 0],
            preferred_element_type=jnp.float32,
        )
    ).astype(jnp.bfloat16)
    up_rank_key_value = (
        adapter_scale
        * jnp.einsum(
            "cbpd,cprd->cprb",
            key_value_gradient,
            up_matrix_pairs,
            preferred_element_type=jnp.float32,
        )
    ).astype(jnp.bfloat16)
    grad_a_qkv = jnp.einsum(
        "cprb,cbd->cprd",
        jnp.concatenate([up_query_matrix[:, None], up_rank_key_value], axis=1),
        x_blocks,
        preferred_element_type=jnp.float32,
    )
    down_gradient = jnp.concatenate([grad_a_qkv, grad_a_out[:, None]], axis=1)
    up_gradient = jnp.stack(
        [
            adapter_scale
            * jnp.einsum(
                "crb,cbd->crd",
                rank_projection[:, 0],
                query_gradient,
                preferred_element_type=jnp.float32,
            ),
            up_gradient_result,
        ],
        axis=1,
    )
    key_value_up_gradient = adapter_scale * jnp.einsum(
        "cprb,cbpd->cprd",
        rank_projection[:, 1:],
        key_value_gradient,
        preferred_element_type=jnp.float32,
    )
    back_a, back_b, back_pairs = (
        lax.all_to_all(
            down_gradient.astype(jnp.bfloat16), "wide", split_axis=3, concat_axis=0, tiled=True
        ).astype(down_gradient.dtype),
        lax.all_to_all(
            up_gradient.astype(jnp.bfloat16), "wide", split_axis=3, concat_axis=0, tiled=True
        ).astype(up_gradient.dtype),
        lax.all_to_all(
            key_value_up_gradient.astype(jnp.bfloat16),
            "wide",
            split_axis=3,
            concat_axis=0,
            tiled=True,
        ).astype(key_value_up_gradient.dtype),
    )
    owners = (group_ids[None, :] == jnp.arange(ADAPTER_COUNT)[:, None]).astype(jnp.float32)
    owned_a = jnp.einsum("ns,sprd->nprd", owners, back_a, precision=lax.Precision.HIGHEST)
    owned_b = jnp.einsum("ns,sprd->nprd", owners, back_b, precision=lax.Precision.HIGHEST)
    owned_pairs = jnp.einsum("ns,sprd->nprd", owners, back_pairs, precision=lax.Precision.HIGHEST)
    total_a, total_b, total_pairs = (
        lax.psum(owned_a.astype(jnp.bfloat16), "prompt").astype(jnp.float32),
        lax.psum(owned_b.astype(jnp.bfloat16), "prompt").astype(jnp.float32),
        lax.psum(owned_pairs.astype(jnp.bfloat16), "prompt").astype(jnp.float32),
    )
    return (total_a, total_b, total_pairs)


def solution(mesh):
    placed = (
        P("prompt", "wide", None),
        P("prompt", "wide", None),
        P("prompt", "wide", None),
        P("prompt", "wide", None),
        P("prompt", None),
        P("prompt", "wide"),
        P(None, None, None, "wide"),
        P(None, None, None, "wide"),
        P(None, None, None, "wide"),
        P("prompt", "wide", None),
        P("prompt", "wide", None),
    )
    return jax.shard_map(
        body,
        mesh=mesh,
        in_specs=placed,
        out_specs=(
            P(None, None, None, "wide"),
            P(None, None, None, "wide"),
            P(None, None, None, "wide"),
        ),
        check_vma=False,
    )
```

profile of v0, /device:TPU:4, one launch (start us, length us, event | category | flops | bytes accessed | tf_op | source)
XLA Modules:
  0.0 612.0 jit_solution(9639752189467336138)
XLA Ops:
  7.2 2.1 copy.89
  14.0 2.0 copy.88
  17.4 63.8 %all-gather.11.cloned.1.call-done = bf16[16,2,16,1024]{2,0,1,3:T(8,128)(2,1)} async-done(((bf16[16,2,16,32]{2,0,1,3:T(8,128)(2,1)}), bf16[16,2,16,1024]{2,0,1,3:T(8,128)(2,1)}) %all-gather.11.cloned.1.call-update) | async-done | bytes 1048592 | tf_op jit(solution)/shard_map/all_gather | solution.py:85
  81.2 3.3 constant_dynamic-slice_fusion
  85.6 66.9 %all-gather.5.cloned.1.call-done = bf16[16,2,16,4096]{3,2,1,0:T(8,128)(2,1)} async-done(((bf16[16,2,16,128]{3,2,1,0:T(8,128)(2,1)}), bf16[16,2,16,4096]{3,2,1,0:T(8,128)(2,1)}) %all-gather.5.cloned.1.call-update) | async-done | bytes 4194320 | tf_op jit(solution)/shard_map/all_gather | solution.py:84
  153.7 86.6 %all-gather.7.cloned.1.call-done = bf16[16,4,16,4096]{3,2,1,0:T(8,128)(2,1)} async-done(((bf16[16,4,16,128]{3,2,1,0:T(8,128)(2,1)}), bf16[16,4,16,4096]{3,2,1,0:T(8,128)(2,1)}) %all-gather.7.cloned.1.call-update) | async-done | bytes 8388624 | tf_op jit(solution)/shard_map/all_gather | solution.py:83
  246.1 63.8 %all-gather.9.cloned.1.call-done = bf16[1,2048,2048]{2,1,0:T(8,128)(2,1)} async-done(((bf16[1,64,2048]{2,1,0:T(8,128)(2,1)}), bf16[1,2048,2048]{2,1,0:T(8,128)(2,1)}) %all-gather.9.cloned.1.call-update) | async-done | bytes 8388624 | tf_op jit(solution)/shard_map/all_gather | solution.py:125
  309.9 12.3 %copy.85 = bf16[1,2048,2048]{1,2,0:T(8,128)(2,1)} copy(bf16[1,2048,2048]{2,1,0:T(8,128)(2,1)} %all-gather.9.cloned.1.call-done) | data formatting | bytes 16777216 | tf_op jit(solution)/shard_map/all_gather | solution.py:125
  322.1 5.3 fusion.100
  328.0 13.6 %bitcast_reduce_fusion = (f32[8,4,128]{2,1,0:T(4,128)S(1)}, f32[8,128,4,2048]{3,1,2,0:T(8,128)}) fusion(pred[2048]{0:T(1024)(128)(4,1)S(1)} %iota_compare_fusion.1, bf16[128,8,4,128]{0,3,2,1:T(8,128)(2,1)S(1)} %bitcast.309, bf16[2048,8,128,1]{0,2,3,1:T(8,128)(2,1)S(1)} %bitcast.311), kind=kOutput, calls=%fused_computation.5 | convolution fusion | flops 2172645376 | bytes 38815744 | tf_op jit(solution)/shard_map/bkgd,jkd->kgbj/dot_general | solution.py:23
  341.6 15.1 %fusion.8 = f32[8,4,128]{2,1,0:T(4,128)S(1)} fusion(f32[8,128,4,2048]{3,1,2,0:T(8,128)} %get-tuple-element.59, f32[8,4,128]{2,1,0:T(4,128)S(1)} %get-tuple-element.56, pred[2048]{0:T(1024)(128)(4,1)S(1)} %iota_compare_fusion.1), kind=kLoop, calls=%fused_computation.13 | loop fusion | flops 41938944 | bytes 33589248 | tf_op jit(solution)/shard_map/reduce_sum | solution.py:42
  357.4 2.0 fusion.51
  359.4 2.3 fusion.18
  361.7 2.3 copy.142
  364.0 2.8 fusion.36
  366.8 18.1 %multiply_reduce_fusion = (f32[128,8,4]{0,2,1:T(4,128)}, bf16[128,8,4,128]{0,3,2,1:T(8,128)(2,1)}) fusion(bf16[128,8,4,128]{0,3,2,1:T(8,128)(2,1)} %bitcast.328, f32[128,8,4]{0,2,1:T(4,128)S(1)} %fusion.63, f32[8,128,4,128]{3,1,2,0:T(8,128)} %fusion.51, f32[128,8,4]{0,2,1:T(4,128)S(1)} %get-tuple-element.55, bf16[2048,8,128,1]{0,2,3,1:T(8,128)(2,1)} %bitcast.319, ...), kind=kOutput, calls=%fused_computation.46 | convolution fusion | flops 2194141184 | bytes 42027008 | tf_op jit(solution)/shard_map/kgbj,jkd->bkgd/dot_general | solution.py:35
  384.9 2.2 fusion.27
  391.0 21.3 %fusion.25 = bf16[128,8,4,128]{0,3,2,1:T(8,128)(2,1)} fusion(f32[8,128,4,128]{3,1,2,0:T(8,128)} %fusion.102, bf16[2048,8,128,1]{0,2,3,1:T(8,128)(2,1)} %bitcast.312, f32[8,128,4,2048]{3,1,2,0:T(8,128)} %get-tuple-element.59, bf16[128,8,4,128]{0,3,2,1:T(8,128)(2,1)} %bitcast.330, bf16[2048,8,128,1]{0,2,3,1:T(8,128)(2,1)} %bitcast.320, ...), kind=kOutput, calls=%fused_computation.36 | convolution fusion | flops 4364173312 | bytes 46188544 | tf_op jit(solution)/shard_map/kgbj,jkd->bkgd/dot_general | solution.py:225
  414.9 2.1 fusion.23
  417.9 2.7 copy.108
  420.7 2.9 reshape.437
  423.6 6.5 %all-to-all-start.1 = ((bf16[32,2,2048]{2,1,0:T(2,128)(2,1)}), bf16[32,2,2048]{2,1,0:T(2,128)(2,1)S(1)}, u32[]{:S(2)}, u32[]{:S(2)}) async-start(bf16[32,2,2048]{2,1,0:T(2,128)(2,1)} %reshape.437), calls=%async_computation.1 | async-start | bytes 524288 | tf_op jit(solution)/shard_map/all_to_all | solution.py:325
  433.3 4.6 copy.106
  437.9 7.3 %reshape.435 = bf16[32,2,4096]{2,1,0:T(2,128)(2,1)} reshape(bf16[4096,1,4,16]{3,2,1,0:T(4,128)(2,1)} %bitcast.306) | data formatting | bytes 1048576
  445.2 7.9 %all-to-all-start = ((bf16[32,2,4096]{2,1,0:T(2,128)(2,1)}), bf16[32,2,4096]{2,1,0:T(2,128)(2,1)}, u32[]{:S(2)}, u32[]{:S(2)}) async-start(bf16[32,2,4096]{2,1,0:T(2,128)(2,1)} %reshape.435), calls=%async_computation | async-start | bytes 1048576 | tf_op jit(solution)/shard_map/all_to_all | solution.py:322
  458.3 8.9 %all-to-all-done = bf16[32,2,4096]{2,1,0:T(2,128)(2,1)} async-done(((bf16[32,2,4096]{2,1,0:T(2,128)(2,1)}), bf16[32,2,4096]{2,1,0:T(2,128)(2,1)}, u32[]{:S(2)}, u32[]{:S(2)}) %all-to-all-start) | async-done | bytes 524320 | tf_op jit(solution)/shard_map/all_to_all | solution.py:322
  467.2 6.4 %all-to-all-start.2 = ((bf16[32,2,512]{2,1,0:T(2,128)(2,1)}), bf16[32,2,512]{2,1,0:T(2,128)(2,1)S(1)}, u32[]{:S(2)}, u32[]{:S(2)}) async-start(bf16[32,2,512]{2,1,0:T(2,128)(2,1)} %reshape.439), calls=%async_computation.2 | async-start | bytes 131072 | tf_op jit(solution)/shard_map/all_to_all | solution.py:328
  473.6 8.3 %reshape.436 = bf16[4096,1,4,16]{3,2,1,0:T(4,128)(2,1)} reshape(bf16[32,2,4096]{2,1,0:T(2,128)(2,1)} %all-to-all-done) | data formatting | bytes 1048576
  482.0 4.6 copy.138
  488.5 59.5 %psum.23 = bf16[16,2,16,32]{3,0,2,1:T(8,128)(2,1)S(1)} all-reduce(bf16[16,2,16,32]{3,0,2,1:T(8,128)(2,1)S(1)} %convolution_convert_fusion.3), channel_id=1, replica_groups=mesh['prompt'=8,'wide'=32] {'prompt'}, use_global_device_ids=true, to_apply=%region_7.8 | all-reduce | flops 16384 | bytes 65536 | tf_op jit(solution)/shard_map/psum | solution.py:343
  548.8 53.2 %all-reduce.3.cloned.1.call-done = (bf16[16,4,16,128]{3,0,2,1:T(8,128)(2,1)}, bf16[16,2,16,128]{3,0,2,1:T(8,128)(2,1)}) async-done(((bf16[16,4,16,128]{3,0,2,1:T(8,128)(2,1)}, bf16[16,2,16,128]{3,0,2,1:T(8,128)(2,1)}), (bf16[16,4,16,128]{3,0,2,1:T(8,128)(2,1)}, bf16[16,2,16,128]{3,0,2,1:T(8,128)(2,1)})) %all-reduce.3.cloned.1.call-update) | async-done | bytes 393232 | tf_op jit(solution)/shard_map/psum | solution.py:341
  602.0 1.8 copy.112
  (86 shorter events, 32.9 us)
Async XLA Ops:
  7.2 233.2 %copy-start = (bf16[1,128,4096]{2,1,0:T(8,128)(2,1)S(1)}, bf16[1,128,4096]{2,1,0:T(8,128)(2,1)}, u32[]{:S(2)}) copy-start(bf16[1,128,4096]{2,1,0:T(8,128)(2,1)} %param.11) | copy-start | bytes 3145732
  7.2 145.3 %copy-start.4 = (bf16[1,128,4096]{2,1,0:T(8,128)(2,1)S(1)}, bf16[1,128,4096]{2,1,0:T(8,128)(2,1)}, u32[]{:S(2)}) copy-start(bf16[1,128,4096]{2,1,0:T(8,128)(2,1)} %param.20) | copy-start | bytes 3145732
  7.2 74.0 %all-gather.11.cloned.1.call-start = ((), (), s32[]{:S(2)}) async-start(), calls=%async_computation.6 | async-start | bytes 8650752 | tf_op jit(solution)/shard_map/all_gather | solution.py:85
  9.4 143.0 %all-gather.5.cloned.1.call-start = ((), (), s32[]{:S(2)}) async-start(), calls=%async_computation.3 | async-start | bytes 4325376 | tf_op jit(solution)/shard_map/all_gather | solution.py:84
  10.2 230.2 %all-gather.7.cloned.1.call-start = ((), (), s32[]{:S(2)}) async-start(), calls=%async_computation.4 | async-start | bytes 8650752 | tf_op jit(solution)/shard_map/all_gather | solution.py:83
  10.9 299.0 %all-gather.9.cloned.1.call-start = ((), (), s32[]{:S(2)}) async-start(), calls=%async_computation.5 | async-start | bytes 8650752 | tf_op jit(solution)/shard_map/all_gather | solution.py:125
  85.6 159.8 %copy-start.11 = (bf16[1,2,16,1024]{3,2,1,0:T(8,128)(2,1)}, bf16[1,2,16,1024]{3,2,1,0:T(8,128)(2,1)S(1)}, u32[]{:S(2)}) copy-start(bf16[1,2,16,1024]{3,2,1,0:T(8,128)(2,1)S(1)} %copy.90) | copy-start | bytes 196612
  153.7 91.5 %copy-start.7 = (bf16[1,128,2048]{1,2,0:T(8,128)(2,1)S(1)}, bf16[1,128,2048]{1,2,0:T(8,128)(2,1)}, u32[]{:S(2)}) copy-start(bf16[1,128,2048]{1,2,0:T(8,128)(2,1)} %copy.88) | copy-start | bytes 1572868
  322.1 5.3 copy-start.1
  327.5 14.1 %copy-start.3 = (bf16[2048,1024]{0,1:T(8,128)(2,1)}, bf16[2048,1024]{0,1:T(8,128)(2,1)S(1)}, u32[]{:S(2)}) copy-start(bf16[2048,1024]{0,1:T(8,128)(2,1)S(1)} %get-tuple-element.51) | copy-start | bytes 12582916
  341.6 15.7 %copy-start.9 = (bf16[128,1024]{0,1:T(8,128)(2,1)S(1)}, bf16[128,1024]{0,1:T(8,128)(2,1)}, u32[]{:S(2)}) copy-start(bf16[128,1024]{0,1:T(8,128)(2,1)} %get-tuple-element.53) | copy-start | bytes 786436
  356.7 2.7 copy-start.8
  384.8 2.2 copy-start.2
  387.1 3.1 copy-start.14
  387.1 3.9 copy-start.16
  391.0 22.9 %copy-start.6 = (bf16[128,8,4,128]{0,3,2,1:T(8,128)(2,1)S(1)}, bf16[128,8,4,128]{0,3,2,1:T(8,128)(2,1)}, u32[]{:S(2)}) copy-start(bf16[128,8,4,128]{0,3,2,1:T(8,128)(2,1)} %get-tuple-element.63) | copy-start | bytes 3145732
  391.0 23.9 %copy-start.5 = (bf16[1,128,4096]{2,1,0:T(8,128)(2,1)S(1)}, bf16[1,128,4096]{2,1,0:T(8,128)(2,1)}, u32[]{:S(2)}) copy-start(bf16[1,128,4096]{2,1,0:T(8,128)(2,1)} %param.20) | copy-start | bytes 3145732
  417.9 15.3 %copy-start.10 = (bf16[1,1,16,4096]{3,2,1,0:T(8,128)(2,1)S(1)}, bf16[1,1,16,4096]{3,2,1,0:T(8,128)(2,1)}, u32[]{:S(2)}) copy-start(bf16[1,1,16,4096]{3,2,1,0:T(8,128)(2,1)} %fusion.22) | copy-start | bytes 393220
  423.6 21.6 %all-to-all-start.1 = ((bf16[32,2,2048]{2,1,0:T(2,128)(2,1)}), bf16[32,2,2048]{2,1,0:T(2,128)(2,1)S(1)}, u32[]{:S(2)}, u32[]{:S(2)}) async-start(bf16[32,2,2048]{2,1,0:T(2,128)(2,1)} %reshape.437), calls=%async_computation.1 | async-start | bytes 524288 | tf_op jit(solution)/shard_map/all_to_all | solution.py:325
  433.3 19.8 %copy-start.12 = (bf16[128,1,1024]{2,0,1:T(8,128)(2,1)S(1)}, bf16[128,1,1024]{2,0,1:T(8,128)(2,1)}, u32[]{:S(2)}) copy-start(bf16[128,1,1024]{2,0,1:T(8,128)(2,1)} %copy.104) | copy-start | bytes 786436
  433.3 19.8 %copy-start.13 = (bf16[128,1,1024]{2,0,1:T(8,128)(2,1)S(1)}, bf16[128,1,1024]{2,0,1:T(8,128)(2,1)}, u32[]{:S(2)}) copy-start(bf16[128,1,1024]{2,0,1:T(8,128)(2,1)} %copy.105) | copy-start | bytes 786436
  445.2 12.3 %copy-start.15 = (s32[1,32]{1,0:T(1,128)S(1)}, s32[1,32]{1,0:T(1,128)}, u32[]{:S(2)}) copy-start(s32[1,32]{1,0:T(1,128)} %param.15) | copy-start | bytes 388
  445.2 22.0 %all-to-all-start = ((bf16[32,2,4096]{2,1,0:T(2,128)(2,1)}), bf16[32,2,4096]{2,1,0:T(2,128)(2,1)}, u32[]{:S(2)}, u32[]{:S(2)}) async-start(bf16[32,2,4096]{2,1,0:T(2,128)(2,1)} %reshape.435), calls=%async_computation | async-start | bytes 1048576 | tf_op jit(solution)/shard_map/all_to_all | solution.py:322
  467.2 20.3 %all-to-all-start.2 = ((bf16[32,2,512]{2,1,0:T(2,128)(2,1)}), bf16[32,2,512]{2,1,0:T(2,128)(2,1)S(1)}, u32[]{:S(2)}, u32[]{:S(2)}) async-start(bf16[32,2,512]{2,1,0:T(2,128)(2,1)} %reshape.439), calls=%async_computation.2 | async-start | bytes 131072 | tf_op jit(solution)/shard_map/all_to_all | solution.py:328
  473.6 128.4 %all-reduce.3.cloned.1.call-start = ((), (), s32[]{:S(2)}) async-start(), calls=%async_computation.7 | async-start | bytes 786432 | tf_op jit(solution)/shard_map/psum | solution.py:341
Sparse Core Ops, SparseCore 0:
  10.4 70.6 all-gather.10
  82.9 69.4 all-gather.4
  154.2 86.0 all-gather.6
  242.0 67.8 all-gather.8
  487.6 114.3 all-reduce.2
where the time goes:
time: 613 us; the launch traced here: 612 us
  waiting for transfers between devices  345 us (56%)
  matrix products  79.8 us (13%)
  local copies, waits for them, and re-layouts  73.2 us (12%)
  blocking collectives  59.5 us (10%)
  starting transfers between devices  20.9 us (3%)
  other arithmetic  16.8 us (3%)
  between operations  16.8 us (3%)
    all_gather x1, waiting for transfers between devices, body(): lax.all_gather(adapter_down, 'wide', axis=3, tiled=True)  86.6 us
    all_gather x1, waiting for transfers between devices, body(): lax.all_gather(adapter_up, 'wide', axis=3, tiled=True)  66.9 us
    all_gather x1, waiting for transfers between devices, body(): gathered = lax.all_gather(prompt_key_value, 'wide', axis=1, tiled=True)  63.8 us
    all_gather x1, waiting for transfers between devices, body(): lax.all_gather(adapter_up_key_value, 'wide', axis=3, tiled=True)  63.8 us
    psum x1, blocking collectives, body(): lax.psum(owned_pairs.astype(jnp.bfloat16), 'prompt').astype(jnp.float32)  59.5 us
    psum x1, waiting for transfers between devices, body(): lax.psum(owned_a.astype(jnp.bfloat16), 'prompt').astype(jnp.float32)  53.2 us
    unnamed x45, local copies, waits for them, and re-layouts  29.9 us
    dot_general x1, matrix products, body(): jnp.einsum('kgbj,jkd->bkgd', score_grad, key_heads, preferred_element_typ...  21.3 us
  transfers between devices with their start and end apart: 8, of which 6 were waited for; matrix products, arithmetic and copies ran while one was open for 8% of the time, Pallas kernels for 0%

commit v1 on v0

v1 whole, which is shorter than its diff:
```python
import functools

import jax
import jax.numpy as jnp
from jax import lax
from jax.experimental import pallas as pl
from jax.experimental.pallas import tpu as pltpu
from jax.sharding import PartitionSpec as P

HEADS = 32
KV_HEADS = 8
HEAD_DIM = 128
ADAPTERS = 16
RANK = 16
BLOCK = 128
WIDE = 32
ROWS = 104
ADAPTER_SCALE = 2.0
MASKED = -1e30
INVERSE_ROOT = HEAD_DIM ** (-0.5)
LOG2E = 1.4426950408889634
KEY_CHUNK = 256

BF16 = jnp.bfloat16
F32 = jnp.float32


def dot(a, b, dims):
    return lax.dot_general(a, b, (dims, ((), ())), preferred_element_type=F32)


NN = ((1,), (0,))
NT = ((1,), (1,))
TN = ((0,), (0,))


def vmem(n):
    return [pl.BlockSpec(memory_space=pltpu.VMEM)] * n


def smem():
    return pl.BlockSpec(memory_space=pltpu.SMEM)


def pack_kernel(ids_ref, down_ref, up_ref, pair_ref, out_ref):
    def step(n, carry):
        a = ids_ref[0, n]
        for p in range(4):
            out_ref[n, 16 * p : 16 * p + 16, :] = down_ref[a, p]
        for p in range(2):
            out_ref[n, 64 + 16 * p : 80 + 16 * p, :] = up_ref[a, p]
        pieces = []
        for p in range(2):
            pair = pair_ref[a, p].astype(F32)
            pieces += [pair[:8], pair[8:]]
        out_ref[n, 96:104, :] = jnp.concatenate(pieces, axis=1).astype(BF16)
        return carry

    lax.fori_loop(0, WIDE, step, 0)


def pack(ids, down, up, pairs):
    return pl.pallas_call(
        pack_kernel,
        out_shape=jax.ShapeDtypeStruct((WIDE, ROWS, 128), BF16),
        in_specs=[smem()] + vmem(3),
        out_specs=pl.BlockSpec(memory_space=pltpu.VMEM),
        name="pack",
    )(ids, down, up, pairs)


def wide_rows(ref, start, stop):
    return jnp.concatenate([ref[s, start:stop, :] for s in range(WIDE)], axis=1)


def pair_rows(ref):
    parts = []
    for g in range(4):
        pieces = []
        for s in range(WIDE):
            pieces.append(ref[s, 96:104, 32 * g : 32 * g + 32].astype(F32))
        parts.append(jnp.concatenate(pieces, axis=1))
    return jnp.concatenate(parts, axis=0).astype(BF16)


def prep_kernel(
    mine_ref, x_ref, fq_ref, ckv_ref, oc_ref, cc_ref,
    q_ref, own_ref, cg_ref, low_ref, upout_ref, pair_ref,
):
    low = dot(wide_rows(mine_ref, 0, 48), x_ref[0], NT).astype(BF16)
    low_ref[...] = low
    up_out = (ADAPTER_SCALE * dot(wide_rows(mine_ref, 80, 96), oc_ref[0], NT)).astype(BF16)
    upout_ref[...] = up_out
    pairs = pair_rows(mine_ref)
    pair_ref[...] = pairs
    for s in range(WIDE):
        cols = slice(128 * s, 128 * s + 128)
        delta = dot(low[:16], mine_ref[s, 64:80, :], TN)
        q_ref[:, cols] = (fq_ref[0, :, cols].astype(F32) + ADAPTER_SCALE * delta).astype(BF16)
        delta = dot(up_out, mine_ref[s, 48:64, :], TN)
        cg_ref[:, cols] = (cc_ref[0, :, cols].astype(F32) + delta).astype(BF16)
    for h in range(2):
        cols = slice(1024 * h, 1024 * h + 1024)
        delta = dot(low[16 + 16 * h : 32 + 16 * h], pairs[16 * h : 16 * h + 16], TN)
        own_ref[:, cols] = (ckv_ref[0, :, cols].astype(F32) + ADAPTER_SCALE * delta).astype(BF16)


def prep(mine, x, fq, ckv, oc, cc):
    return pl.pallas_call(
        prep_kernel,
        out_shape=(
            jax.ShapeDtypeStruct((BLOCK, 4096), BF16),
            jax.ShapeDtypeStruct((BLOCK, 2048), BF16),
            jax.ShapeDtypeStruct((BLOCK, 4096), BF16),
            jax.ShapeDtypeStruct((48, 128), BF16),
            jax.ShapeDtypeStruct((16, 128), BF16),
            jax.ShapeDtypeStruct((32, 1024), BF16),
        ),
        in_specs=vmem(6),
        out_specs=tuple(vmem(6)),
        name="prep",
    )(mine, x, fq, ckv, oc, cc)


def stack_heads(ref):
    return jnp.concatenate([ref[:, 128 * g : 128 * g + 128] for g in range(4)], axis=0)


def attention_kernel(
    end_ref, q_ref, cg_ref, k_ref, v_ref, ok_ref, ov_ref,
    ctx_ref, dq_ref, dk_ref, dv_ref, s_ref, p_ref,
):
    keys = k_ref.shape[0]
    chunks = keys // KEY_CHUNK
    factor = INVERSE_ROOT * LOG2E
    limit = end_ref[0, 0] * BLOCK
    q4 = stack_heads(q_ref)
    cg4 = stack_heads(cg_ref)
    own_k = ok_ref[...]
    own_v = ov_ref[...]
    row = lax.broadcasted_iota(jnp.int32, (512, BLOCK), 0) & (BLOCK - 1)
    col = lax.broadcasted_iota(jnp.int32, (512, BLOCK), 1)
    own_s = jnp.where(col <= row, dot(q4, own_k, NT), MASKED)
    peak = own_s
    for j in range(chunks):
        rows = slice(KEY_CHUNK * j, KEY_CHUNK * (j + 1))
        s = dot(q4, k_ref[rows, :], NT)
        position = lax.broadcasted_iota(jnp.int32, (1, KEY_CHUNK), 1) + KEY_CHUNK * j
        s = jnp.where(position < limit, s, MASKED)
        s_ref[:, rows] = s
        for t in range(KEY_CHUNK // 128):
            peak = jnp.maximum(peak, s[:, 128 * t : 128 * t + 128])
    peak = jnp.max(peak, axis=1, keepdims=True) * factor
    own_p = jnp.exp2(own_s * factor - peak)
    total = own_p
    weighted = dot(own_p.astype(BF16), own_v, NN)
    for j in range(chunks):
        rows = slice(KEY_CHUNK * j, KEY_CHUNK * (j + 1))
        p = jnp.exp2(s_ref[:, rows] * factor - peak)
        for t in range(KEY_CHUNK // 128):
            total = total + p[:, 128 * t : 128 * t + 128]
        p16 = p.astype(BF16)
        p_ref[:, rows] = p16
        weighted = weighted + dot(p16, v_ref[rows, :], NN)
    total = jnp.sum(total, axis=1, keepdims=True)
    context = (weighted / total).astype(BF16)
    delta = jnp.sum(cg4.astype(F32) * context.astype(F32), axis=1, keepdims=True)
    attention = own_p / total
    own_ds = (attention * (dot(cg4, own_v, NT) - delta)).astype(BF16)
    grad = jnp.zeros((512, 128), F32)
    for j in range(chunks):
        rows = slice(KEY_CHUNK * j, KEY_CHUNK * (j + 1))
        dp = dot(cg4, v_ref[rows, :], NT)
        ds = (p_ref[:, rows].astype(F32) * (dp - delta)).astype(BF16)
        grad = grad + dot(ds, k_ref[rows, :], NN)
    grad = (grad / total + dot(own_ds, own_k, NN)) * INVERSE_ROOT
    grad = grad.astype(BF16)
    for g in range(4):
        ctx_ref[:, 128 * g : 128 * g + 128] = context[128 * g : 128 * g + 128]
        dq_ref[:, 128 * g : 128 * g + 128] = grad[128 * g : 128 * g + 128]
    dk_ref[...] = (dot(own_ds, q4, TN) * INVERSE_ROOT).astype(BF16)
    dv_ref[...] = dot(attention.astype(BF16), cg4, TN).astype(BF16)


def attention_call(end, q, cg, kv, own):
    keys = kv.shape[0]
    heads = pl.BlockSpec((BLOCK, 512), lambda k: (0, k))
    head = pl.BlockSpec((BLOCK, 128), lambda k: (0, k))
    return pl.pallas_call(
        attention_kernel,
        grid=(KV_HEADS,),
        out_shape=(
            jax.ShapeDtypeStruct((BLOCK, 4096), BF16),
            jax.ShapeDtypeStruct((BLOCK, 4096), BF16),
            jax.ShapeDtypeStruct((BLOCK, 1024), BF16),
            jax.ShapeDtypeStruct((BLOCK, 1024), BF16),
        ),
        in_specs=[
            smem(),
            heads,
            heads,
            pl.BlockSpec((keys, 128), lambda k: (0, k)),
            pl.BlockSpec((keys, 128), lambda k: (0, k + KV_HEADS)),
            head,
            pl.BlockSpec((BLOCK, 128), lambda k: (0, k + KV_HEADS)),
        ],
        out_specs=(heads, heads, head, head),
        scratch_shapes=[
            pltpu.VMEM((512, keys), F32),
            pltpu.VMEM((512, keys), BF16),
        ],
        compiler_params=pltpu.CompilerParams(dimension_semantics=("arbitrary",)),
        name="attend",
    )(end, q, cg, kv, kv, own, own)


def grads_kernel(
    mine_ref, x_ref, oc_ref, low_ref, upout_ref, pair_ref,
    ctx_ref, dq_ref, dk_ref, dv_ref, out_ref,
):
    low = low_ref[...]
    context = ctx_ref[...]
    dq = dq_ref[...]
    dk = dk_ref[...]
    dv = dv_ref[...]
    out_low = dot(wide_rows(mine_ref, 48, 64), context, NT).astype(BF16)
    up_q = (ADAPTER_SCALE * dot(wide_rows(mine_ref, 64, 80), dq, NT)).astype(BF16)
    up_k = (ADAPTER_SCALE * dot(pair_ref[:16], dk, NT)).astype(BF16)
    up_v = (ADAPTER_SCALE * dot(pair_ref[16:], dv, NT)).astype(BF16)
    up_low = jnp.concatenate([up_q, up_k, up_v], axis=0)
    up_out = upout_ref[...]
    for s in range(WIDE):
        cols = slice(128 * s, 128 * s + 128)
        out_ref[s, 0:48, :] = dot(up_low, x_ref[0, :, cols], NN).astype(BF16)
        out_ref[s, 48:64, :] = dot(up_out, context[:, cols], NN).astype(BF16)
        out_ref[s, 64:80, :] = (ADAPTER_SCALE * dot(low[:16], dq[:, cols], NN)).astype(BF16)
        out_ref[s, 80:96, :] = (ADAPTER_SCALE * dot(out_low, oc_ref[0, :, cols], NN)).astype(BF16)
    pairs = [
        ADAPTER_SCALE * dot(low[16:32], dk, NN),
        ADAPTER_SCALE * dot(low[32:48], dv, NN),
    ]
    for s in range(WIDE):
        cols = slice(32 * s, 32 * s + 32)
        out_ref[s, 96:104, :] = jnp.concatenate(
            [pairs[0][:8, cols], pairs[0][8:, cols], pairs[1][:8, cols], pairs[1][8:, cols]], axis=1
        ).astype(BF16)


def grads(mine, x, oc, low, up_out, pairs, context, dq, dk, dv):
    return pl.pallas_call(
        grads_kernel,
        out_shape=jax.ShapeDtypeStruct((WIDE, ROWS, 128), BF16),
        in_specs=vmem(10),
        out_specs=pl.BlockSpec(memory_space=pltpu.VMEM),
        name="grads",
    )(mine, x, oc, low, up_out, pairs, context, dq, dk, dv)


def combine_kernel(ids_ref, lane_ref, back_ref, mine_ref, o1_ref, o2_ref, o3_ref, acc_ref):
    acc_ref[...] = jnp.zeros_like(acc_ref)

    def step(n, carry):
        a = ids_ref[0, n]
        acc_ref[a] += back_ref[n].astype(F32)
        return carry

    lax.fori_loop(0, WIDE, step, 0)
    y = lane_ref[0]
    mine_ref[...] = acc_ref[pl.ds(4 * y, 4)]
    for shift, ref in ((1, o1_ref), (2, o2_ref), (3, o3_ref)):
        ref[...] = acc_ref[pl.ds(4 * lax.rem(y + shift, 4), 4)].astype(BF16)


def combine(ids, place, back):
    quarter = (4, ROWS, 128)
    return pl.pallas_call(
        combine_kernel,
        out_shape=(
            jax.ShapeDtypeStruct(quarter, F32),
            jax.ShapeDtypeStruct(quarter, BF16),
            jax.ShapeDtypeStruct(quarter, BF16),
            jax.ShapeDtypeStruct(quarter, BF16),
        ),
        in_specs=[smem(), smem()] + vmem(1),
        out_specs=tuple(vmem(4)),
        scratch_shapes=[pltpu.VMEM((ADAPTERS, ROWS, 128), F32)],
        name="combine",
    )(ids, place, back)


def quarter_kernel(lane_ref, mine_ref, r1_ref, r2_ref, r3_ref, keep_ref, send_ref):
    z = lane_ref[1]
    for t in range(2):
        for out, start in ((keep_ref, 2 * z), (send_ref, 2 - 2 * z)):
            value = mine_ref[start + t]
            for ref in (r1_ref, r2_ref, r3_ref):
                value = value + ref[start + t].astype(F32)
            out[t] = value.astype(out.dtype)


def quarter_sum(place, mine, received):
    half = (2, ROWS, 128)
    return pl.pallas_call(
        quarter_kernel,
        out_shape=(jax.ShapeDtypeStruct(half, F32), jax.ShapeDtypeStruct(half, BF16)),
        in_specs=[smem()] + vmem(4),
        out_specs=tuple(vmem(2)),
        name="quarter",
    )(place, mine, *received)


def add_kernel(a_ref, b_ref, out_ref):
    out_ref[...] = (a_ref[...] + b_ref[...].astype(F32)).astype(BF16)


def add_half(a, b):
    return pl.pallas_call(
        add_kernel,
        out_shape=jax.ShapeDtypeStruct(a.shape, BF16),
        in_specs=vmem(2),
        out_specs=pl.BlockSpec(memory_space=pltpu.VMEM),
        name="halfsum",
    )(a, b)


def join_kernel(lane_ref, a_ref, b_ref, out_ref):
    z = lane_ref[1]
    out_ref[pl.ds(2 * z, 2)] = a_ref[...]
    out_ref[pl.ds(2 - 2 * z, 2)] = b_ref[...]


def join(place, a, b):
    return pl.pallas_call(
        join_kernel,
        out_shape=jax.ShapeDtypeStruct((4, ROWS, 128), BF16),
        in_specs=[smem()] + vmem(2),
        out_specs=pl.BlockSpec(memory_space=pltpu.VMEM),
        name="joined",
    )(place, a, b)


def unpack_kernel(lane_ref, q0_ref, q1_ref, q2_ref, q3_ref, down_ref, up_ref, pair_ref):
    y = lane_ref[0]
    for shift, ref in ((0, q0_ref), (1, q1_ref), (2, q2_ref), (3, q3_ref)):
        first = 4 * lax.rem(y + 4 - shift, 4)
        for t in range(4):
            a = first + t
            value = ref[t].astype(F32)
            for p in range(4):
                down_ref[a, p] = value[16 * p : 16 * p + 16]
            for p in range(2):
                up_ref[a, p] = value[64 + 16 * p : 80 + 16 * p]
                for h in range(2):
                    g = 2 * p + h
                    pair_ref[a, p, 8 * h : 8 * h + 8, :] = value[96:104, 32 * g : 32 * g + 32]


def unpack(place, quarters):
    return pl.pallas_call(
        unpack_kernel,
        out_shape=(
            jax.ShapeDtypeStruct((ADAPTERS, 4, RANK, 128), F32),
            jax.ShapeDtypeStruct((ADAPTERS, 2, RANK, 128), F32),
            jax.ShapeDtypeStruct((ADAPTERS, 2, RANK, 32), F32),
        ),
        in_specs=[smem()] + vmem(4),
        out_specs=tuple(vmem(3)),
        name="unpack",
    )(place, *quarters)


def y_shift(value, shift):
    pairs = [(2 * y + z, 2 * ((y + shift) % 4) + z) for y in range(4) for z in range(2)]
    return lax.ppermute(value, "prompt", pairs)


def z_swap(value):
    return lax.ppermute(value, "prompt", [(p, p ^ 1) for p in range(8)])


def body(
    candidate_hidden, frozen_query, candidate_key_value, prompt_key_value, candidate_adapter,
    prompt_block_end, adapter_down, adapter_up, adapter_up_key_value, output_cotangent,
    context_cotangent,
):
    group = lax.axis_index("prompt")
    place = jnp.stack([group // 2, group % 2]).astype(jnp.int32)
    gathered = lax.all_gather(prompt_key_value[0], "wide", axis=0, tiled=True)
    sent = pack(candidate_adapter, adapter_down, adapter_up, adapter_up_key_value)
    mine = lax.all_to_all(sent, "wide", 0, 0, tiled=True)
    q, own, cg, low, up_out, pairs = prep(
        mine, candidate_hidden, frozen_query, candidate_key_value, output_cotangent,
        context_cotangent,
    )
    context, dq, dk, dv = attention_call(prompt_block_end, q, cg, gathered, own)
    blocks = grads(mine, candidate_hidden, output_cotangent, low, up_out, pairs, context, dq, dk, dv)
    back = lax.all_to_all(blocks, "wide", 0, 0, tiled=True)
    total, *others = combine(candidate_adapter, place, back)
    received = [y_shift(other, shift) for shift, other in zip((1, 2, 3), others)]
    keep, send = quarter_sum(place, total, received)
    half = add_half(keep, z_swap(send))
    quarter = join(place, half, z_swap(half))
    quarters = [quarter] + [y_shift(quarter, shift) for shift in (1, 2, 3)]
    return unpack(place, quarters)


def solution(mesh):
    tokens = P("prompt", "wide", None)
    columns = P(None, None, None, "wide")
    placed = (
        tokens, tokens, tokens, tokens, P("prompt", None), P("prompt", "wide"),
        columns, columns, columns, tokens, tokens,
    )
    return jax.shard_map(
        body, mesh=mesh, in_specs=placed, out_specs=(columns, columns, columns), check_vma=False
    )
```

time: 613 us -> 217 us (0.35)
  waiting for transfers between devices: 345 us -> 101 us
  matrix products: 79.8 us -> 0 us
  local copies, waits for them, and re-layouts: 73.2 us -> 4.45 us
  blocking collectives: 59.5 us -> 0 us
  Pallas kernels: 0 us -> 58 us
  other arithmetic: 16.8 us -> 0.61 us
  starting transfers between devices: 20.9 us -> 35.5 us
    all_gather x4 -> x1, waiting for transfers between devices: 281 us -> 36.2 us  [body(): gathered = lax.all_gather(prompt_key_value[0], 'wide', axis=0, tiled=True)]
    dot_general x24 -> x0, matrix products: 79.8 us -> none  [the longest x1 21.3 us: body(): jnp.einsum('kgbj,jkd->bkgd', score_grad, key_heads, preferred_element_typ...]
    psum x1 -> x0, blocking collectives: 59.5 us -> none  [body(): lax.psum(owned_pairs.astype(jnp.bfloat16), 'prompt').astype(jnp.float32)]
    pallas_call x0 -> x9, Pallas kernels: none -> 58 us  [the longest x1 32.8 us: attention_call(): pl.pallas_call(attention_kernel, grid=(KV_HEADS,), out_shape=(jax.ShapeDt...]
    psum x1 -> x0, waiting for transfers between devices: 53.2 us -> none  [body(): lax.psum(owned_a.astype(jnp.bfloat16), 'prompt').astype(jnp.float32)]
    all_to_all x3 -> x2, waiting for transfers between devices: 8.92 us -> 48 us  [the longest x1 27.5 us: body(): mine = lax.all_to_all(sent, 'wide', 0, 0, tiled=True)]
    unnamed x45 -> x20, local copies, waits for them, and re-layouts: 29.9 us -> 4.45 us
    ppermute x0 -> x8, starting transfers between devices: none -> 19.6 us  [the longest x6 11.1 us: y_shift(): return lax.ppermute(value, 'prompt', pairs)]
  transfers between devices with their start and end apart: 8 -> 11, of which waited for: 6 -> 10; matrix products, arithmetic and copies ran while one was open for 8% -> 0% of each run, Pallas kernels for 0% -> 5%
where the time goes in v1:
time: 217 us; the launch traced here: 215 us
  waiting for transfers between devices  101 us (47%)
  Pallas kernels  58 us (27%)
  starting transfers between devices  35.5 us (16%)
  between operations  14.7 us (7%)
  local copies, waits for them, and re-layouts  4.45 us (2%)
    all_gather x1, waiting for transfers between devices, body(): gathered = lax.all_gather(prompt_key_value[0], 'wide', axis=0, tiled=True)  36.2 us
    pallas_call x1, Pallas kernels, attention_call(): pl.pallas_call(attention_kernel, grid=(KV_HEADS,), out_shape=(jax.ShapeDt...  32.8 us
    all_to_all x1, waiting for transfers between devices, body(): mine = lax.all_to_all(sent, 'wide', 0, 0, tiled=True)  27.5 us
    all_to_all x1, waiting for transfers between devices, body(): back = lax.all_to_all(blocks, 'wide', 0, 0, tiled=True)  20.5 us
    ppermute x6, starting transfers between devices, y_shift(): return lax.ppermute(value, 'prompt', pairs)  11.1 us
    all_to_all x1, starting transfers between devices, body(): mine = lax.all_to_all(sent, 'wide', 0, 0, tiled=True)  9.03 us
    ppermute x2, starting transfers between devices, z_swap(): return lax.ppermute(value, 'prompt', [(p, p ^ 1) for p in range(8)])  8.56 us
    ppermute x2, waiting for transfers between devices, z_swap(): return lax.ppermute(value, 'prompt', [(p, p ^ 1) for p in range(8)])  8.52 us
  transfers between devices with their start and end apart: 11, of which 10 were waited for; matrix products, arithmetic and copies ran while one was open for 0% of the time, Pallas kernels for 5%

profile of v1, /device:TPU:4, one launch (start us, length us, event | category | flops | bytes accessed | tf_op | source)
XLA Modules:
  0.0 214.8 jit_solution(9506013920364528813)
XLA Ops:
  7.2 0.7 all-gather.3.cloned.1.call-update
  7.9 4.4 %pack.1 = bf16[32,104,128]{2,1,0:T(8,128)(2,1)} custom-call(s32[1,32]{1,0:T(1,128)} %ids_ref.3, bf16[16,4,16,128]{3,2,1,0:T(8,128)(2,1)} %down_ref.1, bf16[16,2,16,128]{3,2,1,0:T(8,128)(2,1)} %up_ref.1, bf16[16,2,16,32]{3,2,1,0:T(8,128)(2,1)} %pair_ref.1), custom_call_target="tpu_custom_call" | custom-call | tf_op jit(solution)/shard_map/pack/pallas_call | solution.py:63
  12.3 9.0 %all-to-all-start = ((bf16[32,104,128]{2,1,0:T(8,128)(2,1)}), bf16[32,104,128]{2,1,0:T(8,128)(2,1)S(1)}, u32[]{:S(2)}, u32[]{:S(2)}) async-start(bf16[32,104,128]{2,1,0:T(8,128)(2,1)} %pack.1), calls=%async_computation | async-start | bytes 1703936 | tf_op jit(solution)/shard_map/all_to_all | solution.py:390
  22.0 27.5 %all-to-all-done.mine_ref = bf16[32,104,128]{2,1,0:T(8,128)(2,1)S(1)} async-done(((bf16[32,104,128]{2,1,0:T(8,128)(2,1)}), bf16[32,104,128]{2,1,0:T(8,128)(2,1)S(1)}, u32[]{:S(2)}, u32[]{:S(2)}) %all-to-all-start) | async-done | bytes 852000 | tf_op jit(solution)/shard_map/all_to_all | solution.py:390
  49.5 1.0 copy-done
  50.5 5.8 %prep.1 = (bf16[128,4096]{1,0:T(8,128)(2,1)}, bf16[128,2048]{1,0:T(8,128)(2,1)}, bf16[128,4096]{1,0:T(8,128)(2,1)}, bf16[48,128]{1,0:T(8,128)(2,1)}, bf16[16,128]{1,0:T(8,128)(2,1)}, /*index=5*/bf16[32,1024]{1,0:T(8,128)(2,1)}) custom-call(bf16[32,104,128]{2,1,0:T(8,128)(2,1)} %copy-done, bf16[1,128,4096]{2,1,0:T(8,128)(2,1)} %x_ref.3, ...), custom_call_target="tpu_custom_call" | custom-call | tf_op jit(solution)/shard_map/prep/pallas_call | solution.py:109
  56.3 36.2 %all-gather.3.cloned.1.call-done = bf16[1,2048,2048]{2,1,0:T(8,128)(2,1)} async-done(((bf16[1,64,2048]{2,1,0:T(8,128)(2,1)}), bf16[1,2048,2048]{2,1,0:T(8,128)(2,1)}) %all-gather.3.cloned.1.call-update) | async-done | bytes 8388624 | tf_op jit(solution)/shard_map/all_gather | solution.py:388
  92.5 32.8 %attend.1 = (bf16[128,4096]{1,0:T(8,128)(2,1)}, bf16[128,4096]{1,0:T(8,128)(2,1)}, bf16[128,1024]{1,0:T(8,128)(2,1)}, bf16[128,1024]{1,0:T(8,128)(2,1)}) custom-call(s32[1,1]{1,0:T(1,128)S(6)} %copy.14.end_ref, bf16[128,4096]{1,0:T(8,128)(2,1)} %get-tuple-element.22.q_ref, bf16[128,4096]{1,0:T(8,128)(2,1)} %get-tuple-element.23.cg_ref, ...), custom_call_target="tpu_custom_call" | custom-call | tf_op jit(solution)/shard_map/attend/pallas_call | solution.py:189
  125.4 5.6 %grads.1 = bf16[32,104,128]{2,1,0:T(8,128)(2,1)} custom-call(bf16[32,104,128]{2,1,0:T(8,128)(2,1)} %copy-done, bf16[1,128,4096]{2,1,0:T(8,128)(2,1)} %x_ref.3, bf16[1,128,4096]{2,1,0:T(8,128)(2,1)} %oc_ref.3, bf16[48,128]{1,0:T(8,128)(2,1)} %get-tuple-element.19.low_ref, bf16[16,128]{1,0:T(8,128)(2,1)} %get-tuple-element.20.upout_ref, ...), custom_call_target="tpu_custom_call" | custom-call | tf_op jit(solution)/shard_map/grads/pallas_call | solution.py:250
  131.0 6.8 %all-to-all-start.1 = ((bf16[32,104,128]{2,1,0:T(8,128)(2,1)}), bf16[32,104,128]{2,1,0:T(8,128)(2,1)S(1)}, u32[]{:S(2)}, u32[]{:S(2)}) async-start(bf16[32,104,128]{2,1,0:T(8,128)(2,1)} %grads.1), calls=%async_computation.1 | async-start | bytes 1703936 | tf_op jit(solution)/shard_map/all_to_all | solution.py:397
  138.5 20.5 %all-to-all-done.1.back_ref = bf16[32,104,128]{2,1,0:T(8,128)(2,1)S(1)} async-done(((bf16[32,104,128]{2,1,0:T(8,128)(2,1)}), bf16[32,104,128]{2,1,0:T(8,128)(2,1)S(1)}, u32[]{:S(2)}, u32[]{:S(2)}) %all-to-all-start.1) | async-done | bytes 852000 | tf_op jit(solution)/shard_map/all_to_all | solution.py:397
  159.0 0.9 copy-done.1
  159.9 2.4 %combine.1 = (f32[4,104,128]{2,1,0:T(8,128)}, bf16[4,104,128]{2,1,0:T(8,128)(2,1)}, bf16[4,104,128]{2,1,0:T(8,128)(2,1)}, bf16[4,104,128]{2,1,0:T(8,128)(2,1)}) custom-call(s32[1,32]{1,0:T(1,128)} %ids_ref.3, s32[2]{0:T(128)} %pad_add_fusion.lane_ref, bf16[32,104,128]{2,1,0:T(8,128)(2,1)} %copy-done.1), custom_call_target="tpu_custom_call" | custom-call | tf_op jit(solution)/shard_map/combine/pallas_call | solution.py:276
  162.3 1.6 collective-permute-start
  163.9 2.9 %collective-permute-start.1 = (bf16[4,104,128]{2,1,0:T(8,128)(2,1)}, bf16[4,104,128]{2,1,0:T(8,128)(2,1)S(1)}, u32[]{:S(2)}, u32[]{:S(2)}) collective-permute-start(bf16[4,104,128]{2,1,0:T(8,128)(2,1)} %get-tuple-element.31), channel_id=1, source_target_pairs={{0,128},{32,160},{64,192},{96,224},{128,0},{160,32},{192,64},{224,... | collective-permute-start | bytes 319496 | tf_op jit(solution)/shard_map/ppermute | solution.py:374
  166.8 1.5 collective-permute-start.2
  168.2 1.1 collective-permute-done.r1_ref
  169.3 3.6 %collective-permute-done.1.r2_ref = bf16[4,104,128]{2,1,0:T(8,128)(2,1)S(1)} collective-permute-done((bf16[4,104,128]{2,1,0:T(8,128)(2,1)}, bf16[4,104,128]{2,1,0:T(8,128)(2,1)S(1)}, u32[]{:S(2)}, u32[]{:S(2)}) %collective-permute-start.1) | collective-permute-done | bytes 106528 | tf_op jit(solution)/shard_map/ppermute | solution.py:374
  173.6 1.8 quarter.1
  175.4 4.6 %collective-permute-start.3 = (bf16[2,104,128]{2,1,0:T(8,128)(2,1)}, bf16[2,104,128]{2,1,0:T(8,128)(2,1)S(1)}, u32[]{:S(2)}, u32[]{:S(2)}) collective-permute-start(bf16[2,104,128]{2,1,0:T(8,128)(2,1)} %get-tuple-element.34), channel_id=1, source_target_pairs={{0,32},{32,0},{64,96},{96,64},{128,160},{160,128},{192,224},{224,1... | collective-permute-start | bytes 159752 | tf_op jit(solution)/shard_map/ppermute | solution.py:378
  180.0 4.3 %collective-permute-done.3.b_ref = bf16[2,104,128]{2,1,0:T(8,128)(2,1)S(1)} collective-permute-done((bf16[2,104,128]{2,1,0:T(8,128)(2,1)}, bf16[2,104,128]{2,1,0:T(8,128)(2,1)S(1)}, u32[]{:S(2)}, u32[]{:S(2)}) %collective-permute-start.3) | collective-permute-done | bytes 53280 | tf_op jit(solution)/shard_map/ppermute | solution.py:378
  184.9 1.5 halfsum.1.a_ref
  186.4 4.0 %collective-permute-start.4 = (bf16[2,104,128]{2,1,0:T(8,128)(2,1)}, bf16[2,104,128]{2,1,0:T(8,128)(2,1)S(1)}, u32[]{:S(2)}, u32[]{:S(2)}) collective-permute-start(bf16[2,104,128]{2,1,0:T(8,128)(2,1)} %halfsum.1.a_ref), channel_id=1, source_target_pairs={{0,32},{32,0},{64,96},{96,64},{128,160},{160,128},{192,224},{224,1... | collective-permute-start | bytes 159752 | tf_op jit(solution)/shard_map/ppermute | solution.py:378
  190.4 4.3 %collective-permute-done.4.b_ref = bf16[2,104,128]{2,1,0:T(8,128)(2,1)S(1)} collective-permute-done((bf16[2,104,128]{2,1,0:T(8,128)(2,1)}, bf16[2,104,128]{2,1,0:T(8,128)(2,1)S(1)}, u32[]{:S(2)}, u32[]{:S(2)}) %collective-permute-start.4) | collective-permute-done | bytes 53280 | tf_op jit(solution)/shard_map/ppermute | solution.py:378
  195.3 1.5 joined.1.q0_ref
  196.8 0.8 collective-permute-start.5
  197.6 2.7 %collective-permute-start.6 = (bf16[4,104,128]{2,1,0:T(8,128)(2,1)}, bf16[4,104,128]{2,1,0:T(8,128)(2,1)S(1)}, u32[]{:S(2)}, u32[]{:S(2)}) collective-permute-start(bf16[4,104,128]{2,1,0:T(8,128)(2,1)} %joined.1.q0_ref), channel_id=1, source_target_pairs={{0,128},{32,160},{64,192},{96,224},{128,0},{160,32},{192,64},{224,... | collective-permute-start | bytes 319496 | tf_op jit(solution)/shard_map/ppermute | solution.py:374
  200.3 1.6 collective-permute-start.7
  201.9 1.0 collective-permute-done.5.q1_ref
  202.9 1.4 collective-permute-done.6.q2_ref
  204.4 0.9 collective-permute-done.7.q3_ref
  205.9 2.1 unpack.1
  (21 shorter events, 3.2 us)
Async XLA Ops:
  7.2 85.4 %all-gather.3.cloned.1.call-start = ((), (), s32[]{:S(2)}) async-start(), calls=%async_computation.2 | async-start | bytes 8650752 | tf_op jit(solution)/shard_map/all_gather | solution.py:388
  12.3 37.2 %all-to-all-start = ((bf16[32,104,128]{2,1,0:T(8,128)(2,1)}), bf16[32,104,128]{2,1,0:T(8,128)(2,1)S(1)}, u32[]{:S(2)}, u32[]{:S(2)}) async-start(bf16[32,104,128]{2,1,0:T(8,128)(2,1)} %pack.1), calls=%async_computation | async-start | bytes 1703936 | tf_op jit(solution)/shard_map/all_to_all | solution.py:390
  49.5 1.0 copy-start
  131.0 28.0 %all-to-all-start.1 = ((bf16[32,104,128]{2,1,0:T(8,128)(2,1)}), bf16[32,104,128]{2,1,0:T(8,128)(2,1)S(1)}, u32[]{:S(2)}, u32[]{:S(2)}) async-start(bf16[32,104,128]{2,1,0:T(8,128)(2,1)} %grads.1), calls=%async_computation.1 | async-start | bytes 1703936 | tf_op jit(solution)/shard_map/all_to_all | solution.py:397
  158.9 0.9 copy-start.1
  162.3 7.1 %collective-permute-start = (bf16[4,104,128]{2,1,0:T(8,128)(2,1)}, bf16[4,104,128]{2,1,0:T(8,128)(2,1)S(1)}, u32[]{:S(2)}, u32[]{:S(2)}) collective-permute-start(bf16[4,104,128]{2,1,0:T(8,128)(2,1)} %get-tuple-element.30), channel_id=1, source_target_pairs={{0,64},{32,96},{64,128},{96,160},{128,192},{160,224},{192,0},{224,... | collective-permute-start | bytes 319496 | tf_op jit(solution)/shard_map/ppermute | solution.py:374
  163.9 9.1 %collective-permute-start.1 = (bf16[4,104,128]{2,1,0:T(8,128)(2,1)}, bf16[4,104,128]{2,1,0:T(8,128)(2,1)S(1)}, u32[]{:S(2)}, u32[]{:S(2)}) collective-permute-start(bf16[4,104,128]{2,1,0:T(8,128)(2,1)} %get-tuple-element.31), channel_id=1, source_target_pairs={{0,128},{32,160},{64,192},{96,224},{128,0},{160,32},{192,64},{224,... | collective-permute-start | bytes 319496 | tf_op jit(solution)/shard_map/ppermute | solution.py:374
  166.8 6.2 %collective-permute-start.2 = (bf16[4,104,128]{2,1,0:T(8,128)(2,1)}, bf16[4,104,128]{2,1,0:T(8,128)(2,1)S(1)}, u32[]{:S(2)}, u32[]{:S(2)}) collective-permute-start(bf16[4,104,128]{2,1,0:T(8,128)(2,1)} %get-tuple-element.32), channel_id=1, source_target_pairs={{0,192},{32,224},{64,0},{96,32},{128,64},{160,96},{192,128},{224,1... | collective-permute-start | bytes 319496 | tf_op jit(solution)/shard_map/ppermute | solution.py:374
  169.3 3.6 %copy-start.2 = (bf16[4,104,128]{2,1,0:T(8,128)(2,1)}, bf16[4,104,128]{2,1,0:T(8,128)(2,1)S(1)}, u32[]{:S(2)}) copy-start(bf16[4,104,128]{2,1,0:T(8,128)(2,1)S(1)} %collective-permute-done.r1_ref) | copy-start | bytes 319492
  173.0 0.6 copy-start.3
  173.0 0.7 copy-start.4
  175.4 8.8 %collective-permute-start.3 = (bf16[2,104,128]{2,1,0:T(8,128)(2,1)}, bf16[2,104,128]{2,1,0:T(8,128)(2,1)S(1)}, u32[]{:S(2)}, u32[]{:S(2)}) collective-permute-start(bf16[2,104,128]{2,1,0:T(8,128)(2,1)} %get-tuple-element.34), channel_id=1, source_target_pairs={{0,32},{32,0},{64,96},{96,64},{128,160},{160,128},{192,224},{224,1... | collective-permute-start | bytes 159752 | tf_op jit(solution)/shard_map/ppermute | solution.py:378
  184.3 0.6 copy-start.8
  186.4 8.3 %collective-permute-start.4 = (bf16[2,104,128]{2,1,0:T(8,128)(2,1)}, bf16[2,104,128]{2,1,0:T(8,128)(2,1)S(1)}, u32[]{:S(2)}, u32[]{:S(2)}) collective-permute-start(bf16[2,104,128]{2,1,0:T(8,128)(2,1)} %halfsum.1.a_ref), channel_id=1, source_target_pairs={{0,32},{32,0},{64,96},{96,64},{128,160},{160,128},{192,224},{224,1... | collective-permute-start | bytes 159752 | tf_op jit(solution)/shard_map/ppermute | solution.py:378
  194.7 0.6 copy-start.9
  196.8 6.1 %collective-permute-start.5 = (bf16[4,104,128]{2,1,0:T(8,128)(2,1)}, bf16[4,104,128]{2,1,0:T(8,128)(2,1)S(1)}, u32[]{:S(2)}, u32[]{:S(2)}) collective-permute-start(bf16[4,104,128]{2,1,0:T(8,128)(2,1)} %joined.1.q0_ref), channel_id=1, source_target_pairs={{0,64},{32,96},{64,128},{96,160},{128,192},{160,224},{192,0},{224,... | collective-permute-start | bytes 319496 | tf_op jit(solution)/shard_map/ppermute | solution.py:374
  197.6 6.8 %collective-permute-start.6 = (bf16[4,104,128]{2,1,0:T(8,128)(2,1)}, bf16[4,104,128]{2,1,0:T(8,128)(2,1)S(1)}, u32[]{:S(2)}, u32[]{:S(2)}) collective-permute-start(bf16[4,104,128]{2,1,0:T(8,128)(2,1)} %joined.1.q0_ref), channel_id=1, source_target_pairs={{0,128},{32,160},{64,192},{96,224},{128,0},{160,32},{192,64},{224,... | collective-permute-start | bytes 319496 | tf_op jit(solution)/shard_map/ppermute | solution.py:374
  200.3 4.9 %collective-permute-start.7 = (bf16[4,104,128]{2,1,0:T(8,128)(2,1)}, bf16[4,104,128]{2,1,0:T(8,128)(2,1)S(1)}, u32[]{:S(2)}, u32[]{:S(2)}) collective-permute-start(bf16[4,104,128]{2,1,0:T(8,128)(2,1)} %joined.1.q0_ref), channel_id=1, source_target_pairs={{0,192},{32,224},{64,0},{96,32},{128,64},{160,96},{192,128},{224,1... | collective-permute-start | bytes 319496 | tf_op jit(solution)/shard_map/ppermute | solution.py:374
  202.9 2.3 %copy-start.5 = (bf16[4,104,128]{2,1,0:T(8,128)(2,1)}, bf16[4,104,128]{2,1,0:T(8,128)(2,1)S(1)}, u32[]{:S(2)}) copy-start(bf16[4,104,128]{2,1,0:T(8,128)(2,1)S(1)} %collective-permute-done.5.q1_ref) | copy-start | bytes 319492
  204.4 0.9 copy-start.6
  205.3 0.6 copy-start.7
Sparse Core Ops, SparseCore 0:
  9.8 82.6 all-gather.2

commit v2 on v1

--- a/solution.py
+++ b/solution.py
@@ -1,5 +1,3 @@
-import functools
-
 import jax
 import jax.numpy as jnp
 from jax import lax
@@ -7,7 +5,7 @@
 from jax.experimental.pallas import tpu as pltpu
 from jax.sharding import PartitionSpec as P
 
-HEADS = 32
+
 KV_HEADS = 8
 HEAD_DIM = 128
 ADAPTERS = 16
@@ -20,6 +18,7 @@
 INVERSE_ROOT = HEAD_DIM ** (-0.5)
 LOG2E = 1.4426950408889634
 KEY_CHUNK = 256
+SHIFTS = (0, 1, 3, 2)
 
 BF16 = jnp.bfloat16
 F32 = jnp.float32
@@ -65,6 +64,7 @@
         out_shape=jax.ShapeDtypeStruct((WIDE, ROWS, 128), BF16),
         in_specs=[smem()] + vmem(3),
         out_specs=pl.BlockSpec(memory_space=pltpu.VMEM),
+        compiler_params=pltpu.CompilerParams(vmem_limit_bytes=4 << 20),
         name="pack",
     )(ids, down, up, pairs)
 
@@ -118,6 +118,7 @@
         ),
         in_specs=vmem(6),
         out_specs=tuple(vmem(6)),
+        compiler_params=pltpu.CompilerParams(vmem_limit_bytes=28 << 20),
         name="prep",
     )(mine, x, fq, ckv, oc, cc)
 
@@ -126,14 +127,23 @@
     return jnp.concatenate([ref[:, 128 * g : 128 * g + 128] for g in range(4)], axis=0)
 
 
+def piece_mask(limit_ref, shift, other):
+    x, z, core, end = (limit_ref[i] for i in range(4))
+    side = core ^ other
+    lane = lax.broadcasted_iota(jnp.int32, (1, KEY_CHUNK), 1)
+    origin = jnp.zeros((1, KEY_CHUNK), jnp.int32)
+    for t in range(4):
+        source = (lax.rem(x + 4 - shift, 4) * 4 + lax.rem(z + 4 - t, 4)) * 2 + side
+        origin = jnp.where(lane >= 64 * t, source, origin)
+    return origin < 2 * end
+
+
 def attention_kernel(
-    end_ref, q_ref, cg_ref, k_ref, v_ref, ok_ref, ov_ref,
-    ctx_ref, dq_ref, dk_ref, dv_ref, s_ref, p_ref,
+    limit_ref, q_ref, cg_ref, ok_ref, ov_ref, *refs,
 ):
-    keys = k_ref.shape[0]
-    chunks = keys // KEY_CHUNK
+    k_refs, v_refs = refs[:8], refs[8:16]
+    ctx_ref, dq_ref, dk_ref, dv_ref, s_ref, p_ref = refs[16:]
     factor = INVERSE_ROOT * LOG2E
-    limit = end_ref[0, 0] * BLOCK
     q4 = stack_heads(q_ref)
     cg4 = stack_heads(cg_ref)
     own_k = ok_ref[...]
@@ -142,11 +152,10 @@
     col = lax.broadcasted_iota(jnp.int32, (512, BLOCK), 1)
     own_s = jnp.where(col <= row, dot(q4, own_k, NT), MASKED)
     peak = own_s
-    for j in range(chunks):
+    for j in range(8):
         rows = slice(KEY_CHUNK * j, KEY_CHUNK * (j + 1))
-        s = dot(q4, k_ref[rows, :], NT)
-        position = lax.broadcasted_iota(jnp.int32, (1, KEY_CHUNK), 1) + KEY_CHUNK * j
-        s = jnp.where(position < limit, s, MASKED)
+        s = dot(q4, k_refs[j][...].reshape(KEY_CHUNK, 128), NT)
+        s = jnp.where(piece_mask(limit_ref, SHIFTS[j % 4], j // 4), s, MASKED)
         s_ref[:, rows] = s
         for t in range(KEY_CHUNK // 128):
             peak = jnp.maximum(peak, s[:, 128 * t : 128 * t + 128])
@@ -154,25 +163,25 @@
     own_p = jnp.exp2(own_s * factor - peak)
     total = own_p
     weighted = dot(own_p.astype(BF16), own_v, NN)
-    for j in range(chunks):
+    for j in range(8):
         rows = slice(KEY_CHUNK * j, KEY_CHUNK * (j + 1))
         p = jnp.exp2(s_ref[:, rows] * factor - peak)
         for t in range(KEY_CHUNK // 128):
             total = total + p[:, 128 * t : 128 * t + 128]
         p16 = p.astype(BF16)
         p_ref[:, rows] = p16
-        weighted = weighted + dot(p16, v_ref[rows, :], NN)
+        weighted = weighted + dot(p16, v_refs[j][...].reshape(KEY_CHUNK, 128), NN)
     total = jnp.sum(total, axis=1, keepdims=True)
     context = (weighted / total).astype(BF16)
     delta = jnp.sum(cg4.astype(F32) * context.astype(F32), axis=1, keepdims=True)
     attention = own_p / total
     own_ds = (attention * (dot(cg4, own_v, NT) - delta)).astype(BF16)
     grad = jnp.zeros((512, 128), F32)
-    for j in range(chunks):
+    for j in range(8):
         rows = slice(KEY_CHUNK * j, KEY_CHUNK * (j + 1))
-        dp = dot(cg4, v_ref[rows, :], NT)
+        dp = dot(cg4, v_refs[j][...].reshape(KEY_CHUNK, 128), NT)
         ds = (p_ref[:, rows].astype(F32) * (dp - delta)).astype(BF16)
-        grad = grad + dot(ds, k_ref[rows, :], NN)
+        grad = grad + dot(ds, k_refs[j][...].reshape(KEY_CHUNK, 128), NN)
     grad = (grad / total + dot(own_ds, own_k, NN)) * INVERSE_ROOT
     grad = grad.astype(BF16)
     for g in range(4):
@@ -182,47 +191,52 @@
     dv_ref[...] = dot(attention.astype(BF16), cg4, TN).astype(BF16)
 
 
-def attention_call(end, q, cg, kv, own):
-    keys = kv.shape[0]
+def attention_call(part, limits, q, cg, own, pieces):
+    first = 4 * part
+    heads_in = pl.BlockSpec((BLOCK, 512), lambda k: (0, k + first))
     heads = pl.BlockSpec((BLOCK, 512), lambda k: (0, k))
     head = pl.BlockSpec((BLOCK, 128), lambda k: (0, k))
     return pl.pallas_call(
         attention_kernel,
-        grid=(KV_HEADS,),
+        grid=(4,),
         out_shape=(
-            jax.ShapeDtypeStruct((BLOCK, 4096), BF16),
-            jax.ShapeDtypeStruct((BLOCK, 4096), BF16),
-            jax.ShapeDtypeStruct((BLOCK, 1024), BF16),
-            jax.ShapeDtypeStruct((BLOCK, 1024), BF16),
+            jax.ShapeDtypeStruct((BLOCK, 2048), BF16),
+            jax.ShapeDtypeStruct((BLOCK, 2048), BF16),
+            jax.ShapeDtypeStruct((BLOCK, 512), BF16),
+            jax.ShapeDtypeStruct((BLOCK, 512), BF16),
         ),
         in_specs=[
             smem(),
-            heads,
-            heads,
-            pl.BlockSpec((keys, 128), lambda k: (0, k)),
-            pl.BlockSpec((keys, 128), lambda k: (0, k + KV_HEADS)),
-            head,
-            pl.BlockSpec((BLOCK, 128), lambda k: (0, k + KV_HEADS)),
-        ],
+            heads_in,
+            heads_in,
+            pl.BlockSpec((BLOCK, 128), lambda k: (0, k + first)),
+            pl.BlockSpec((BLOCK, 128), lambda k: (0, k + first + KV_HEADS)),
+        ]
+        + [pl.BlockSpec((4, 64, 128), lambda k: (0, 0, k))] * 8
+        + [pl.BlockSpec((4, 64, 128), lambda k: (0, 0, k + 4))] * 8,
         out_specs=(heads, heads, head, head),
         scratch_shapes=[
-            pltpu.VMEM((512, keys), F32),
-            pltpu.VMEM((512, keys), BF16),
+            pltpu.VMEM((512, 2048), F32),
+            pltpu.VMEM((512, 2048), BF16),
         ],
-        compiler_params=pltpu.CompilerParams(dimension_semantics=("arbitrary",)),
-        name="attend",
-    )(end, q, cg, kv, kv, own, own)
+        compiler_params=pltpu.CompilerParams(
+            dimension_semantics=("arbitrary",), vmem_limit_bytes=24 << 20
+        ),
+        cost_estimate=pl.CostEstimate(
+            flops=12_000_000_000, bytes_accessed=8_000_000, transcendentals=4_000_000
+        ),
+    )(limits, q, cg, own, own, *pieces, *pieces)
 
 
 def grads_kernel(
     mine_ref, x_ref, oc_ref, low_ref, upout_ref, pair_ref,
-    ctx_ref, dq_ref, dk_ref, dv_ref, out_ref,
+    *refs,
 ):
+    out_ref = refs[8]
     low = low_ref[...]
-    context = ctx_ref[...]
-    dq = dq_ref[...]
-    dk = dk_ref[...]
-    dv = dv_ref[...]
+    context, dq, dk, dv = (
+        jnp.concatenate([refs[i][...], refs[i + 4][...]], axis=1) for i in range(4)
+    )
     out_low = dot(wide_rows(mine_ref, 48, 64), context, NT).astype(BF16)
     up_q = (ADAPTER_SCALE * dot(wide_rows(mine_ref, 64, 80), dq, NT)).astype(BF16)
     up_k = (ADAPTER_SCALE * dot(pair_ref[:16], dk, NT)).astype(BF16)
@@ -246,14 +260,15 @@
         ).astype(BF16)
 
 
-def grads(mine, x, oc, low, up_out, pairs, context, dq, dk, dv):
+def grads(mine, x, oc, low, up_out, pairs, *halves):
     return pl.pallas_call(
         grads_kernel,
         out_shape=jax.ShapeDtypeStruct((WIDE, ROWS, 128), BF16),
-        in_specs=vmem(10),
+        in_specs=vmem(14),
         out_specs=pl.BlockSpec(memory_space=pltpu.VMEM),
+        compiler_params=pltpu.CompilerParams(vmem_limit_bytes=28 << 20),
         name="grads",
-    )(mine, x, oc, low, up_out, pairs, context, dq, dk, dv)
+    )(mine, x, oc, low, up_out, pairs, *halves)
 
 
 def combine_kernel(ids_ref, lane_ref, back_ref, mine_ref, o1_ref, o2_ref, o3_ref, acc_ref):
@@ -284,59 +299,30 @@
         in_specs=[smem(), smem()] + vmem(1),
         out_specs=tuple(vmem(4)),
         scratch_shapes=[pltpu.VMEM((ADAPTERS, ROWS, 128), F32)],
+        compiler_params=pltpu.CompilerParams(vmem_limit_bytes=8 << 20),
         name="combine",
     )(ids, place, back)
 
 
-def quarter_kernel(lane_ref, mine_ref, r1_ref, r2_ref, r3_ref, keep_ref, send_ref):
-    z = lane_ref[1]
-    for t in range(2):
-        for out, start in ((keep_ref, 2 * z), (send_ref, 2 - 2 * z)):
-            value = mine_ref[start + t]
-            for ref in (r1_ref, r2_ref, r3_ref):
-                value = value + ref[start + t].astype(F32)
-            out[t] = value.astype(out.dtype)
-
-
-def quarter_sum(place, mine, received):
-    half = (2, ROWS, 128)
-    return pl.pallas_call(
-        quarter_kernel,
-        out_shape=(jax.ShapeDtypeStruct(half, F32), jax.ShapeDtypeStruct(half, BF16)),
-        in_specs=[smem()] + vmem(4),
-        out_specs=tuple(vmem(2)),
-        name="quarter",
-    )(place, mine, *received)
+def quarter_kernel(mine_ref, r1_ref, r2_ref, r3_ref, out_ref):
+    value = mine_ref[...]
+    for ref in (r1_ref, r2_ref, r3_ref):
+        value = value + ref[...].astype(F32)
+    out_ref[...] = value.astype(BF16)
 
 
 def add_kernel(a_ref, b_ref, out_ref):
-    out_ref[...] = (a_ref[...] + b_ref[...].astype(F32)).astype(BF16)
-
-
-def add_half(a, b):
-    return pl.pallas_call(
-        add_kernel,
-        out_shape=jax.ShapeDtypeStruct(a.shape, BF16),
-        in_specs=vmem(2),
+    out_ref[...] = (a_ref[...].astype(F32) + b_ref[...].astype(F32)).astype(BF16)
+
+
+def summed(kernel, *terms):
+    return pl.pallas_call(
+        kernel,
+        out_shape=jax.ShapeDtypeStruct(terms[0].shape, BF16),
+        in_specs=vmem(len(terms)),
         out_specs=pl.BlockSpec(memory_space=pltpu.VMEM),
-        name="halfsum",
-    )(a, b)
-
-
-def join_kernel(lane_ref, a_ref, b_ref, out_ref):
-    z = lane_ref[1]
-    out_ref[pl.ds(2 * z, 2)] = a_ref[...]
-    out_ref[pl.ds(2 - 2 * z, 2)] = b_ref[...]
-
-
-def join(place, a, b):
-    return pl.pallas_call(
-        join_kernel,
-        out_shape=jax.ShapeDtypeStruct((4, ROWS, 128), BF16),
-        in_specs=[smem()] + vmem(2),
-        out_specs=pl.BlockSpec(memory_space=pltpu.VMEM),
-        name="joined",
-    )(place, a, b)
+        compiler_params=pltpu.CompilerParams(vmem_limit_bytes=4 << 20),
+    )(*terms)
 
 
 def unpack_kernel(lane_ref, q0_ref, q1_ref, q2_ref, q3_ref, down_ref, up_ref, pair_ref):
@@ -365,6 +351,7 @@
         ),
         in_specs=[smem()] + vmem(4),
         out_specs=tuple(vmem(3)),
+        compiler_params=pltpu.CompilerParams(vmem_limit_bytes=8 << 20),
         name="unpack",
     )(place, *quarters)
 
@@ -378,28 +365,55 @@
     return lax.ppermute(value, "prompt", [(p, p ^ 1) for p in range(8)])
 
 
-def body(
+def wide_index(x, z, core):
+    return (4 * (x % 4) + z % 4) * 2 + core
+
+
+def wide_move(value, dx, dz, dcore):
+    pairs = [
+        (wide_index(x, z, c), wide_index(x + dx, z + dz, c ^ dcore))
+        for x in range(4) for z in range(4) for c in range(2)
+    ]
+    return lax.ppermute(value, "wide", pairs)
+
+
+def gather_part(prompt, part):
+    keys = prompt[:, 512 * part : 512 * part + 512]
+    values = prompt[:, 1024 + 512 * part : 1536 + 512 * part]
+    mine = jnp.concatenate([keys, values], axis=1)
+    moved = [wide_move(mine, 0, s, 0) for s in (1, 2, 3)]
+    column = jnp.stack([mine] + moved)
+    return [column] + [wide_move(column, s, 0, 0) for s in (1, 3, 2)]
+
+
+def step(
     candidate_hidden, frozen_query, candidate_key_value, prompt_key_value, candidate_adapter,
     prompt_block_end, adapter_down, adapter_up, adapter_up_key_value, output_cotangent,
     context_cotangent,
 ):
     group = lax.axis_index("prompt")
     place = jnp.stack([group // 2, group % 2]).astype(jnp.int32)
-    gathered = lax.all_gather(prompt_key_value[0], "wide", axis=0, tiled=True)
+    lane = lax.axis_index("wide")
+    limits = jnp.stack([lane // 8, lane // 2 % 4, lane % 2, prompt_block_end[0, 0]]).astype(jnp.int32)
     sent = pack(candidate_adapter, adapter_down, adapter_up, adapter_up_key_value)
     mine = lax.all_to_all(sent, "wide", 0, 0, tiled=True)
+    parts = []
+    for part in range(2):
+        pieces = gather_part(prompt_key_value[0], part)
+        parts.append(pieces + [wide_move(piece, 0, 0, 1) for piece in pieces])
     q, own, cg, low, up_out, pairs = prep(
         mine, candidate_hidden, frozen_query, candidate_key_value, output_cotangent,
         context_cotangent,
     )
-    context, dq, dk, dv = attention_call(prompt_block_end, q, cg, gathered, own)
-    blocks = grads(mine, candidate_hidden, output_cotangent, low, up_out, pairs, context, dq, dk, dv)
+    halves = []
+    for part in range(2):
+        halves += attention_call(part, limits, q, cg, own, parts[part])
+    blocks = grads(mine, candidate_hidden, output_cotangent, low, up_out, pairs, *halves)
     back = lax.all_to_all(blocks, "wide", 0, 0, tiled=True)
     total, *others = combine(candidate_adapter, place, back)
     received = [y_shift(other, shift) for shift, other in zip((1, 2, 3), others)]
-    keep, send = quarter_sum(place, total, received)
-    half = add_half(keep, z_swap(send))
-    quarter = join(place, half, z_swap(half))
+    quarter = summed(quarter_kernel, total, *received)
+    quarter = summed(add_kernel, quarter, z_swap(quarter))
     quarters = [quarter] + [y_shift(quarter, shift) for shift in (1, 2, 3)]
     return unpack(place, quarters)
 
@@ -412,5 +426,5 @@
         columns, columns, columns, tokens, tokens,
     )
     return jax.shard_map(
-        body, mesh=mesh, in_specs=placed, out_specs=(columns, columns, columns), check_vma=False
+        step, mesh=mesh, in_specs=placed, out_specs=(columns, columns, columns), check_vma=False
     )

time: 217 us -> 204 us (0.940)
  starting transfers between devices: 35.5 us -> 67 us
  waiting for transfers between devices: 101 us -> 79.2 us
  Pallas kernels: 58 us -> 44.7 us
  between operations: 14.7 us -> 1.54 us
  local copies, waits for them, and re-layouts: 4.45 us -> 8.63 us
    ppermute x0 -> x20, waiting for transfers between devices: none -> 43.6 us  [wide_move(): return lax.ppermute(value, 'wide', pairs)]
    all_gather x1 -> x0, waiting for transfers between devices: 36.2 us -> none  [body(): gathered = lax.all_gather(prompt_key_value[0], 'wide', axis=0, tiled=True)]
    ppermute x0 -> x20, starting transfers between devices: none -> 35.1 us  [wide_move(): return lax.ppermute(value, 'wide', pairs)]
    all_to_all x2, waiting for transfers between devices: 48 us -> 21 us  [the longest x1 21 us: step(): back = lax.all_to_all(blocks, 'wide', 0, 0, tiled=True)]
    unnamed x20 -> x28, local copies, waits for them, and re-layouts: 4.45 us -> 8.61 us
    pallas_call x1, Pallas kernels: 5.81 us -> 1.75 us  [prep(): pl.pallas_call(prep_kernel, out_shape=(jax.ShapeDtypeStruct((BLOCK, 4096)...]
    ppermute x2 -> x1, starting transfers between devices: 8.56 us -> 4.58 us  [z_swap(): return lax.ppermute(value, 'prompt', [(p, p ^ 1) for p in range(8)])]
    pallas_call x1, Pallas kernels: 5.63 us -> 2.13 us  [grads(): pl.pallas_call(grads_kernel, out_shape=jax.ShapeDtypeStruct((WIDE, ROWS,...]
  transfers between devices with their start and end apart: 11 -> 29, of which waited for: 10 -> 13; matrix products, arithmetic and copies ran while one was open for 0% -> 1% of each run, Pallas kernels for 5% -> 9%
where the time goes in v2:
time: 204 us; the launch traced here: 202 us
  waiting for transfers between devices  79.2 us (39%)
  starting transfers between devices  67 us (33%)
  Pallas kernels  44.7 us (22%)
  local copies, waits for them, and re-layouts  8.63 us (4%)
    ppermute x20, waiting for transfers between devices, wide_move(): return lax.ppermute(value, 'wide', pairs)  43.6 us
    ppermute x20, starting transfers between devices, wide_move(): return lax.ppermute(value, 'wide', pairs)  35.1 us
    pallas_call x2, Pallas kernels, attention_call(): pl.pallas_call(attention_kernel, grid=(4,), out_shape=(jax.ShapeDtypeStru...  34.4 us
    all_to_all x1, waiting for transfers between devices, step(): back = lax.all_to_all(blocks, 'wide', 0, 0, tiled=True)  21 us
    ppermute x6, starting transfers between devices, y_shift(): return lax.ppermute(value, 'prompt', pairs)  11.2 us
    all_to_all x1, starting transfers between devices, step(): mine = lax.all_to_all(sent, 'wide', 0, 0, tiled=True)  9.16 us
    unnamed x28, local copies, waits for them, and re-layouts  8.61 us
    ppermute x6, waiting for transfers between devices, y_shift(): return lax.ppermute(value, 'prompt', pairs)  7.97 us
  transfers between devices with their start and end apart: 29, of which 13 were waited for; matrix products, arithmetic and copies ran while one was open for 1% of the time, Pallas kernels for 9%

profile of v2, /device:TPU:4, one launch (start us, length us, event | category | flops | bytes accessed | tf_op | source)
XLA Modules:
  0.0 202.2 jit_solution(4639435126820356094)
XLA Ops:
  4.0 3.9 %pack.1 = bf16[32,104,128]{2,1,0:T(8,128)(2,1)} custom-call(s32[1,32]{1,0:T(1,128)S(1)} %copy-done.9, bf16[16,4,16,128]{3,2,1,0:T(8,128)(2,1)S(1)} %copy-done.6, bf16[16,2,16,128]{3,2,1,0:T(8,128)(2,1)S(1)} %copy-done.7, bf16[16,2,16,32]{3,2,1,0:T(8,128)(2,1)S(1)} %copy-done.8), custom_call_target="tpu_custom_call" | custom-call | tf_op jit(solution)/shard_map/pack/pallas_call | solution.py:62
  7.9 9.2 %all-to-all-start = ((bf16[32,104,128]{2,1,0:T(8,128)(2,1)}), bf16[32,104,128]{2,1,0:T(8,128)(2,1)S(1)}, u32[]{:S(2)}, u32[]{:S(2)}) async-start(bf16[32,104,128]{2,1,0:T(8,128)(2,1)} %pack.1), calls=%async_computation | async-start | bytes 1703936 | tf_op jit(solution)/shard_map/all_to_all | solution.py:399
  17.1 3.4 %collective-permute-start.2 = (bf16[64,1024]{1,0:T(8,128)(2,1)S(1)}, bf16[64,1024]{1,0:T(8,128)(2,1)S(1)}, u32[]{:S(2)}, u32[]{:S(2)}) collective-permute-start(bf16[64,1024]{1,0:T(8,128)(2,1)S(1)} %get-tuple-element.46), channel_id=1, source_target_pairs={{0,6},{1,7},{2,0},{3,1},{4,2},{5,3},{6,4},{7,5},{8,14},{9,15},{10,... | collective-permute-start | bytes 393224 | tf_op jit(solution)/shard_map/ppermute | solution.py:377
  21.6 2.8 %collective-permute-start.12 = (bf16[64,1024]{1,0:T(8,128)(2,1)S(1)}, bf16[64,1024]{1,0:T(8,128)(2,1)S(1)}, u32[]{:S(2)}, u32[]{:S(2)}) collective-permute-start(bf16[64,1024]{1,0:T(8,128)(2,1)S(1)} %get-tuple-element.44), channel_id=1, source_target_pairs={{0,6},{1,7},{2,0},{3,1},{4,2},{5,3},{6,4},{7,5},{8,14},{9,15},{10,... | collective-permute-start | bytes 393224 | tf_op jit(solution)/shard_map/ppermute | solution.py:377
  25.6 9.2 %collective-permute-done.2 = bf16[64,1024]{1,0:T(8,128)(2,1)S(1)} collective-permute-done((bf16[64,1024]{1,0:T(8,128)(2,1)S(1)}, bf16[64,1024]{1,0:T(8,128)(2,1)S(1)}, u32[]{:S(2)}, u32[]{:S(2)}) %collective-permute-start.2) | collective-permute-done | bytes 131104 | tf_op jit(solution)/shard_map/ppermute | solution.py:377
  34.8 19.1 %collective-permute-start.10 = (bf16[64,1024]{1,0:T(8,128)(2,1)S(1)}, bf16[64,1024]{1,0:T(8,128)(2,1)S(1)}, u32[]{:S(2)}, u32[]{:S(2)}) collective-permute-start(bf16[64,1024]{1,0:T(8,128)(2,1)S(1)} %get-tuple-element.44), channel_id=1, source_target_pairs={{0,2},{1,3},{2,4},{3,5},{4,6},{5,7},{6,0},{7,1},{8,10},{9,11},{10,... | collective-permute-start | bytes 393224 | tf_op jit(solution)/shard_map/ppermute | solution.py:377
  53.9 2.2 %collective-permute-done.1 = bf16[64,1024]{1,0:T(8,128)(2,1)S(1)} collective-permute-done((bf16[64,1024]{1,0:T(8,128)(2,1)S(1)}, bf16[64,1024]{1,0:T(8,128)(2,1)S(1)}, u32[]{:S(2)}, u32[]{:S(2)}) %collective-permute-start.1) | collective-permute-done | bytes 131104 | tf_op jit(solution)/shard_map/ppermute | solution.py:377
  56.3 1.3 collective-permute-start.3
  58.4 1.8 collective-permute-start.5
  62.1 1.2 collective-permute-start.13
  63.3 19.1 %collective-permute-done.3.refs_1_.refs_9_ = bf16[4,64,1024]{2,1,0:T(8,128)(2,1)} collective-permute-done((bf16[4,64,1024]{2,1,0:T(8,128)(2,1)S(1)}, bf16[4,64,1024]{2,1,0:T(8,128)(2,1)}, u32[]{:S(2)}, u32[]{:S(2)}) %collective-permute-start.3) | collective-permute-done | bytes 524320 | tf_op jit(solution)/shard_map/ppermute | solution.py:377
  84.5 9.2 %collective-permute-done.13.refs_1_.refs_9_ = bf16[4,64,1024]{2,1,0:T(8,128)(2,1)} collective-permute-done((bf16[4,64,1024]{2,1,0:T(8,128)(2,1)}, bf16[4,64,1024]{2,1,0:T(8,128)(2,1)}, u32[]{:S(2)}, u32[]{:S(2)}) %collective-permute-start.13) | collective-permute-done | bytes 524320 | tf_op jit(solution)/shard_map/ppermute | solution.py:377
  94.5 1.2 copy-done.3
  95.7 1.2 copy-done.4
  98.0 1.7 prep.1
  100.3 2.7 %collective-permute-done.15.refs_3_.refs_11_ = bf16[4,64,1024]{2,1,0:T(8,128)(2,1)} collective-permute-done((bf16[4,64,1024]{2,1,0:T(8,128)(2,1)}, bf16[4,64,1024]{2,1,0:T(8,128)(2,1)}, u32[]{:S(2)}, u32[]{:S(2)}) %collective-permute-start.15) | collective-permute-done | bytes 524320 | tf_op jit(solution)/shard_map/ppermute | solution.py:377
  103.6 17.2 %shard_map.130 = (bf16[128,2048]{1,0:T(8,128)(2,1)S(1)}, bf16[128,2048]{1,0:T(8,128)(2,1)S(1)}, bf16[128,512]{1,0:T(8,128)(2,1)S(1)}, bf16[128,512]{1,0:T(8,128)(2,1)S(1)}) custom-call(s32[4]{0:T(128)S(1)} %pad_add_fusion.1.limit_ref, bf16[128,4096]{1,0:T(8,128)(2,1)S(1)} %get-tuple-element.24.q_ref, bf16[128,4096]{1,0:T(8,128)(2,1)S(1)} %get-tuple-element.25.cg_ref, ...), custom_call_target="tpu_custom_call" | custom-call | flops 12000000000 | bytes 8000000 | tf_op jit(solution)/shard_map/pallas_call | solution.py:199
  120.8 17.2 %shard_map.131 = (bf16[128,2048]{1,0:T(8,128)(2,1)S(1)}, bf16[128,2048]{1,0:T(8,128)(2,1)S(1)}, bf16[128,512]{1,0:T(8,128)(2,1)S(1)}, bf16[128,512]{1,0:T(8,128)(2,1)S(1)}) custom-call(s32[4]{0:T(128)S(1)} %pad_add_fusion.1.limit_ref, bf16[128,4096]{1,0:T(8,128)(2,1)S(1)} %get-tuple-element.24.q_ref, bf16[128,4096]{1,0:T(8,128)(2,1)S(1)} %get-tuple-element.25.cg_ref, ...), custom_call_target="tpu_custom_call" | custom-call | flops 12000000000 | bytes 8000000 | tf_op jit(solution)/shard_map/pallas_call | solution.py:199
  138.0 2.1 %grads.1 = bf16[32,104,128]{2,1,0:T(8,128)(2,1)S(1)} custom-call(bf16[32,104,128]{2,1,0:T(8,128)(2,1)S(1)} %all-to-all-done.mine_ref, bf16[1,128,4096]{2,1,0:T(8,128)(2,1)S(1)} %copy-done, bf16[1,128,4096]{2,1,0:T(8,128)(2,1)S(1)} %copy-done.1, bf16[48,128]{1,0:T(8,128)(2,1)S(1)} %get-tuple-element.21.low_ref, ...), custom_call_target="tpu_custom_call" | custom-call | tf_op jit(solution)/shard_map/grads/pallas_call | solution.py:264
  141.1 7.0 %all-to-all-start.1 = ((bf16[32,104,128]{2,1,0:T(8,128)(2,1)}), bf16[32,104,128]{2,1,0:T(8,128)(2,1)S(1)}, u32[]{:S(2)}, u32[]{:S(2)}) async-start(bf16[32,104,128]{2,1,0:T(8,128)(2,1)} %copy-done.2), calls=%async_computation.1 | async-start | bytes 1703936 | tf_op jit(solution)/shard_map/all_to_all | solution.py:412
  148.1 21.0 %all-to-all-done.1.back_ref = bf16[32,104,128]{2,1,0:T(8,128)(2,1)S(1)} async-done(((bf16[32,104,128]{2,1,0:T(8,128)(2,1)}), bf16[32,104,128]{2,1,0:T(8,128)(2,1)S(1)}, u32[]{:S(2)}, u32[]{:S(2)}) %all-to-all-start.1) | async-done | bytes 852000 | tf_op jit(solution)/shard_map/all_to_all | solution.py:412
  170.1 1.7 collective-permute-start.20
  171.8 2.9 %collective-permute-start.21 = (bf16[4,104,128]{2,1,0:T(8,128)(2,1)S(1)}, bf16[4,104,128]{2,1,0:T(8,128)(2,1)S(1)}, u32[]{:S(2)}, u32[]{:S(2)}) collective-permute-start(bf16[4,104,128]{2,1,0:T(8,128)(2,1)S(1)} %get-tuple-element.37), channel_id=1, source_target_pairs={{0,128},{32,160},{64,192},{96,224},{128,0},{160,32},{192,64},{224,... | collective-permute-start | bytes 319496 | tf_op jit(solution)/shard_map/ppermute | solution.py:361
  174.7 1.3 collective-permute-start.22
  177.1 3.6 %collective-permute-done.21.r2_ref = bf16[4,104,128]{2,1,0:T(8,128)(2,1)S(1)} collective-permute-done((bf16[4,104,128]{2,1,0:T(8,128)(2,1)S(1)}, bf16[4,104,128]{2,1,0:T(8,128)(2,1)S(1)}, u32[]{:S(2)}, u32[]{:S(2)}) %collective-permute-start.21) | collective-permute-done | bytes 106528 | tf_op jit(solution)/shard_map/ppermute | solution.py:361
  180.7 4.6 %collective-permute-start.23 = (bf16[4,104,128]{2,1,0:T(8,128)(2,1)S(1)}, bf16[4,104,128]{2,1,0:T(8,128)(2,1)S(1)}, u32[]{:S(2)}, u32[]{:S(2)}) collective-permute-start(bf16[4,104,128]{2,1,0:T(8,128)(2,1)S(1)} %shard_map.132.a_ref), channel_id=1, source_target_pairs={{0,32},{32,0},{64,96},{96,64},{128,160},{160,128},{192,224},{224,1... | collective-permute-start | bytes 319496 | tf_op jit(solution)/shard_map/ppermute | solution.py:365
  185.3 6.7 %collective-permute-done.23.b_ref = bf16[4,104,128]{2,1,0:T(8,128)(2,1)S(1)} collective-permute-done((bf16[4,104,128]{2,1,0:T(8,128)(2,1)S(1)}, bf16[4,104,128]{2,1,0:T(8,128)(2,1)S(1)}, u32[]{:S(2)}, u32[]{:S(2)}) %collective-permute-start.23) | collective-permute-done | bytes 106528 | tf_op jit(solution)/shard_map/ppermute | solution.py:365
  192.0 1.2 collective-permute-start.24
  193.3 2.6 %collective-permute-start.25 = (bf16[4,104,128]{2,1,0:T(8,128)(2,1)S(1)}, bf16[4,104,128]{2,1,0:T(8,128)(2,1)S(1)}, u32[]{:S(2)}, u32[]{:S(2)}) collective-permute-start(bf16[4,104,128]{2,1,0:T(8,128)(2,1)S(1)} %shard_map.133.q0_ref), channel_id=1, source_target_pairs={{0,128},{32,160},{64,192},{96,224},{128,0},{160,32},{192,64},{224,... | collective-permute-start | bytes 319496 | tf_op jit(solution)/shard_map/ppermute | solution.py:361
  195.9 1.4 collective-permute-start.26
  197.4 1.8 collective-permute-done.24.q1_ref
  200.7 1.5 unpack.1
  (70 shorter events, 17.6 us)
Async XLA Ops:
  7.9 86.6 %all-to-all-start = ((bf16[32,104,128]{2,1,0:T(8,128)(2,1)}), bf16[32,104,128]{2,1,0:T(8,128)(2,1)S(1)}, u32[]{:S(2)}, u32[]{:S(2)}) async-start(bf16[32,104,128]{2,1,0:T(8,128)(2,1)} %pack.1), calls=%async_computation | async-start | bytes 1703936 | tf_op jit(solution)/shard_map/all_to_all | solution.py:399
  17.1 17.7 %collective-permute-start.2 = (bf16[64,1024]{1,0:T(8,128)(2,1)S(1)}, bf16[64,1024]{1,0:T(8,128)(2,1)S(1)}, u32[]{:S(2)}, u32[]{:S(2)}) collective-permute-start(bf16[64,1024]{1,0:T(8,128)(2,1)S(1)} %get-tuple-element.46), channel_id=1, source_target_pairs={{0,6},{1,7},{2,0},{3,1},{4,2},{5,3},{6,4},{7,5},{8,14},{9,15},{10,... | collective-permute-start | bytes 393224 | tf_op jit(solution)/shard_map/ppermute | solution.py:377
  20.5 35.7 %collective-permute-start.1 = (bf16[64,1024]{1,0:T(8,128)(2,1)S(1)}, bf16[64,1024]{1,0:T(8,128)(2,1)S(1)}, u32[]{:S(2)}, u32[]{:S(2)}) collective-permute-start(bf16[64,1024]{1,0:T(8,128)(2,1)S(1)} %get-tuple-element.46), channel_id=1, source_target_pairs={{0,4},{1,5},{2,6},{3,7},{4,0},{5,1},{6,2},{7,3},{8,12},{9,13},{10,... | collective-permute-start | bytes 393224 | tf_op jit(solution)/shard_map/ppermute | solution.py:377
  20.5 35.7 %collective-permute-start = (bf16[64,1024]{1,0:T(8,128)(2,1)S(1)}, bf16[64,1024]{1,0:T(8,128)(2,1)S(1)}, u32[]{:S(2)}, u32[]{:S(2)}) collective-permute-start(bf16[64,1024]{1,0:T(8,128)(2,1)S(1)} %get-tuple-element.46), channel_id=1, source_target_pairs={{0,2},{1,3},{2,4},{3,5},{4,6},{5,7},{6,0},{7,1},{8,10},{9,11},{10,... | collective-permute-start | bytes 393224 | tf_op jit(solution)/shard_map/ppermute | solution.py:377
  21.6 36.7 %collective-permute-start.12 = (bf16[64,1024]{1,0:T(8,128)(2,1)S(1)}, bf16[64,1024]{1,0:T(8,128)(2,1)S(1)}, u32[]{:S(2)}, u32[]{:S(2)}) collective-permute-start(bf16[64,1024]{1,0:T(8,128)(2,1)S(1)} %get-tuple-element.44), channel_id=1, source_target_pairs={{0,6},{1,7},{2,0},{3,1},{4,2},{5,3},{6,4},{7,5},{8,14},{9,15},{10,... | collective-permute-start | bytes 393224 | tf_op jit(solution)/shard_map/ppermute | solution.py:377
  24.4 36.8 %collective-permute-start.11 = (bf16[64,1024]{1,0:T(8,128)(2,1)S(1)}, bf16[64,1024]{1,0:T(8,128)(2,1)S(1)}, u32[]{:S(2)}, u32[]{:S(2)}) collective-permute-start(bf16[64,1024]{1,0:T(8,128)(2,1)S(1)} %get-tuple-element.44), channel_id=1, source_target_pairs={{0,4},{1,5},{2,6},{3,7},{4,0},{5,1},{6,2},{7,3},{8,12},{9,13},{10,... | collective-permute-start | bytes 393224 | tf_op jit(solution)/shard_map/ppermute | solution.py:377
  34.8 26.5 %collective-permute-start.10 = (bf16[64,1024]{1,0:T(8,128)(2,1)S(1)}, bf16[64,1024]{1,0:T(8,128)(2,1)S(1)}, u32[]{:S(2)}, u32[]{:S(2)}) collective-permute-start(bf16[64,1024]{1,0:T(8,128)(2,1)S(1)} %get-tuple-element.44), channel_id=1, source_target_pairs={{0,2},{1,3},{2,4},{3,5},{4,6},{5,7},{6,0},{7,1},{8,10},{9,11},{10,... | collective-permute-start | bytes 393224 | tf_op jit(solution)/shard_map/ppermute | solution.py:377
  56.2 38.3 %copy-start = (bf16[1,128,4096]{2,1,0:T(8,128)(2,1)S(1)}, bf16[1,128,4096]{2,1,0:T(8,128)(2,1)}, u32[]{:S(2)}) copy-start(bf16[1,128,4096]{2,1,0:T(8,128)(2,1)} %x_ref.3) | copy-start | bytes 3145732
  56.2 38.3 %copy-start.1 = (bf16[1,128,4096]{2,1,0:T(8,128)(2,1)S(1)}, bf16[1,128,4096]{2,1,0:T(8,128)(2,1)}, u32[]{:S(2)}) copy-start(bf16[1,128,4096]{2,1,0:T(8,128)(2,1)} %oc_ref.3) | copy-start | bytes 3145732
  56.3 26.2 %collective-permute-start.3 = (bf16[4,64,1024]{2,1,0:T(8,128)(2,1)S(1)}, bf16[4,64,1024]{2,1,0:T(8,128)(2,1)}, u32[]{:S(2)}, u32[]{:S(2)}) collective-permute-start(bf16[4,64,1024]{2,1,0:T(8,128)(2,1)S(1)} %pad_maximum_fusion.refs_0_.refs_8_), channel_id=1, source_target_pairs={{0,8},{1,9},{2,10},{3,11},{4,12},{5,13},{6,14},{7,15},{8,16},{9,17... | collective-permute-start | bytes 1572872 | tf_op jit(solution)/shard_map/ppermute | solution.py:377
  57.6 24.9 %collective-permute-start.4 = (bf16[4,64,1024]{2,1,0:T(8,128)(2,1)S(1)}, bf16[4,64,1024]{2,1,0:T(8,128)(2,1)}, u32[]{:S(2)}, u32[]{:S(2)}) collective-permute-start(bf16[4,64,1024]{2,1,0:T(8,128)(2,1)S(1)} %pad_maximum_fusion.refs_0_.refs_8_), channel_id=1, source_target_pairs={{0,24},{1,25},{2,26},{3,27},{4,28},{5,29},{6,30},{7,31},{8,0},{9,1... | collective-permute-start | bytes 1572872 | tf_op jit(solution)/shard_map/ppermute | solution.py:377
  58.4 24.8 %collective-permute-start.5 = (bf16[4,64,1024]{2,1,0:T(8,128)(2,1)S(1)}, bf16[4,64,1024]{2,1,0:T(8,128)(2,1)}, u32[]{:S(2)}, u32[]{:S(2)}) collective-permute-start(bf16[4,64,1024]{2,1,0:T(8,128)(2,1)S(1)} %pad_maximum_fusion.refs_0_.refs_8_), channel_id=1, source_target_pairs={{0,16},{1,17},{2,18},{3,19},{4,20},{5,21},{6,22},{7,23},{8,24},{9,... | collective-permute-start | bytes 1572872 | tf_op jit(solution)/shard_map/ppermute | solution.py:377
  61.2 22.0 %collective-permute-start.6 = (bf16[4,64,1024]{2,1,0:T(8,128)(2,1)S(1)}, bf16[4,64,1024]{2,1,0:T(8,128)(2,1)S(1)}, u32[]{:S(2)}, u32[]{:S(2)}) collective-permute-start(bf16[4,64,1024]{2,1,0:T(8,128)(2,1)S(1)} %pad_maximum_fusion.refs_0_.refs_8_), channel_id=1, source_target_pairs={{0,1},{1,0},{2,3},{3,2},{4,5},{5,4},{6,7},{7,6},{8,9},{9,8},{10,11... | collective-permute-start | bytes 1572872 | tf_op jit(solution)/shard_map/ppermute | solution.py:377
  62.1 31.6 %collective-permute-start.13 = (bf16[4,64,1024]{2,1,0:T(8,128)(2,1)}, bf16[4,64,1024]{2,1,0:T(8,128)(2,1)}, u32[]{:S(2)}, u32[]{:S(2)}) collective-permute-start(bf16[4,64,1024]{2,1,0:T(8,128)(2,1)} %pad_maximum_fusion.1.refs_0_.refs_8_), channel_id=1, source_target_pairs={{0,8},{1,9},{2,10},{3,11},{4,12},{5,13},{6,14},{7,15},{8,16},{9,17... | collective-permute-start | bytes 1572872 | tf_op jit(solution)/shard_map/ppermute | solution.py:377
  82.4 17.3 %collective-permute-start.14 = (bf16[4,64,1024]{2,1,0:T(8,128)(2,1)}, bf16[4,64,1024]{2,1,0:T(8,128)(2,1)}, u32[]{:S(2)}, u32[]{:S(2)}) collective-permute-start(bf16[4,64,1024]{2,1,0:T(8,128)(2,1)} %pad_maximum_fusion.1.refs_0_.refs_8_), channel_id=1, source_target_pairs={{0,24},{1,25},{2,26},{3,27},{4,28},{5,29},{6,30},{7,31},{8,0},{9,1... | collective-permute-start | bytes 1572872 | tf_op jit(solution)/shard_map/ppermute | solution.py:377
  82.4 20.5 %collective-permute-start.15 = (bf16[4,64,1024]{2,1,0:T(8,128)(2,1)}, bf16[4,64,1024]{2,1,0:T(8,128)(2,1)}, u32[]{:S(2)}, u32[]{:S(2)}) collective-permute-start(bf16[4,64,1024]{2,1,0:T(8,128)(2,1)} %pad_maximum_fusion.1.refs_0_.refs_8_), channel_id=1, source_target_pairs={{0,16},{1,17},{2,18},{3,19},{4,20},{5,21},{6,22},{7,23},{8,24},{9,... | collective-permute-start | bytes 1572872 | tf_op jit(solution)/shard_map/ppermute | solution.py:377
  83.2 19.8 %collective-permute-start.7 = (bf16[4,64,1024]{2,1,0:T(8,128)(2,1)}, bf16[4,64,1024]{2,1,0:T(8,128)(2,1)}, u32[]{:S(2)}, u32[]{:S(2)}) collective-permute-start(bf16[4,64,1024]{2,1,0:T(8,128)(2,1)} %collective-permute-done.3.refs_1_.refs_9_), channel_id=1, source_target_pairs={{0,1},{1,0},{2,3},{3,2},{4,5},{5,4},{6,7},{7,6},{8,9},{9,8},{10,11... | collective-permute-start | bytes 1572872 | tf_op jit(solution)/shard_map/ppermute | solution.py:377
  84.0 19.5 %collective-permute-start.8 = (bf16[4,64,1024]{2,1,0:T(8,128)(2,1)}, bf16[4,64,1024]{2,1,0:T(8,128)(2,1)}, u32[]{:S(2)}, u32[]{:S(2)}) collective-permute-start(bf16[4,64,1024]{2,1,0:T(8,128)(2,1)} %collective-permute-done.4.refs_2_.refs_10_), channel_id=1, source_target_pairs={{0,1},{1,0},{2,3},{3,2},{4,5},{5,4},{6,7},{7,6},{8,9},{9,8},{10,11... | collective-permute-start | bytes 1572872 | tf_op jit(solution)/shard_map/ppermute | solution.py:377
  93.7 9.9 %collective-permute-start.9 = (bf16[4,64,1024]{2,1,0:T(8,128)(2,1)}, bf16[4,64,1024]{2,1,0:T(8,128)(2,1)}, u32[]{:S(2)}, u32[]{:S(2)}) collective-permute-start(bf16[4,64,1024]{2,1,0:T(8,128)(2,1)} %collective-permute-done.5.refs_3_.refs_11_), channel_id=1, source_target_pairs={{0,1},{1,0},{2,3},{3,2},{4,5},{5,4},{6,7},{7,6},{8,9},{9,8},{10,11... | collective-permute-start | bytes 1572872 | tf_op jit(solution)/shard_map/ppermute | solution.py:377
  99.7 21.0 %collective-permute-start.16 = (bf16[4,64,1024]{2,1,0:T(8,128)(2,1)}, bf16[4,64,1024]{2,1,0:T(8,128)(2,1)S(1)}, u32[]{:S(2)}, u32[]{:S(2)}) collective-permute-start(bf16[4,64,1024]{2,1,0:T(8,128)(2,1)} %pad_maximum_fusion.1.refs_0_.refs_8_), channel_id=1, source_target_pairs={{0,1},{1,0},{2,3},{3,2},{4,5},{5,4},{6,7},{7,6},{8,9},{9,8},{10,11... | collective-permute-start | bytes 1572872 | tf_op jit(solution)/shard_map/ppermute | solution.py:377
  103.0 17.8 %collective-permute-start.17 = (bf16[4,64,1024]{2,1,0:T(8,128)(2,1)}, bf16[4,64,1024]{2,1,0:T(8,128)(2,1)S(1)}, u32[]{:S(2)}, u32[]{:S(2)}) collective-permute-start(bf16[4,64,1024]{2,1,0:T(8,128)(2,1)} %collective-permute-done.13.refs_1_.refs_9_), channel_id=1, source_target_pairs={{0,1},{1,0},{2,3},{3,2},{4,5},{5,4},{6,7},{7,6},{8,9},{9,8},{10,11... | collective-permute-start | bytes 1572872 | tf_op jit(solution)/shard_map/ppermute | solution.py:377
  103.0 17.8 %collective-permute-start.18 = (bf16[4,64,1024]{2,1,0:T(8,128)(2,1)}, bf16[4,64,1024]{2,1,0:T(8,128)(2,1)S(1)}, u32[]{:S(2)}, u32[]{:S(2)}) collective-permute-start(bf16[4,64,1024]{2,1,0:T(8,128)(2,1)} %collective-permute-done.14.refs_2_.refs_10_), channel_id=1, source_target_pairs={{0,1},{1,0},{2,3},{3,2},{4,5},{5,4},{6,7},{7,6},{8,9},{9,8},{10,11... | collective-permute-start | bytes 1572872 | tf_op jit(solution)/shard_map/ppermute | solution.py:377
  103.5 17.3 %collective-permute-start.19 = (bf16[4,64,1024]{2,1,0:T(8,128)(2,1)}, bf16[4,64,1024]{2,1,0:T(8,128)(2,1)S(1)}, u32[]{:S(2)}, u32[]{:S(2)}) collective-permute-start(bf16[4,64,1024]{2,1,0:T(8,128)(2,1)} %collective-permute-done.15.refs_3_.refs_11_), channel_id=1, source_target_pairs={{0,1},{1,0},{2,3},{3,2},{4,5},{5,4},{6,7},{7,6},{8,9},{9,8},{10,11... | collective-permute-start | bytes 1572872 | tf_op jit(solution)/shard_map/ppermute | solution.py:377
  141.1 28.1 %all-to-all-start.1 = ((bf16[32,104,128]{2,1,0:T(8,128)(2,1)}), bf16[32,104,128]{2,1,0:T(8,128)(2,1)S(1)}, u32[]{:S(2)}, u32[]{:S(2)}) async-start(bf16[32,104,128]{2,1,0:T(8,128)(2,1)} %copy-done.2), calls=%async_computation.1 | async-start | bytes 1703936 | tf_op jit(solution)/shard_map/all_to_all | solution.py:412
  148.1 21.1 %copy-start.10 = (s32[1,32]{1,0:T(1,128)S(1)}, s32[1,32]{1,0:T(1,128)}, u32[]{:S(2)}) copy-start(s32[1,32]{1,0:T(1,128)} %ids_ref.3) | copy-start | bytes 388
  170.1 7.0 %collective-permute-start.20 = (bf16[4,104,128]{2,1,0:T(8,128)(2,1)S(1)}, bf16[4,104,128]{2,1,0:T(8,128)(2,1)S(1)}, u32[]{:S(2)}, u32[]{:S(2)}) collective-permute-start(bf16[4,104,128]{2,1,0:T(8,128)(2,1)S(1)} %get-tuple-element.36), channel_id=1, source_target_pairs={{0,64},{32,96},{64,128},{96,160},{128,192},{160,224},{192,0},{224,... | collective-permute-start | bytes 319496 | tf_op jit(solution)/shard_map/ppermute | solution.py:361
  171.8 8.9 %collective-permute-start.21 = (bf16[4,104,128]{2,1,0:T(8,128)(2,1)S(1)}, bf16[4,104,128]{2,1,0:T(8,128)(2,1)S(1)}, u32[]{:S(2)}, u32[]{:S(2)}) collective-permute-start(bf16[4,104,128]{2,1,0:T(8,128)(2,1)S(1)} %get-tuple-element.37), channel_id=1, source_target_pairs={{0,128},{32,160},{64,192},{96,224},{128,0},{160,32},{192,64},{224,... | collective-permute-start | bytes 319496 | tf_op jit(solution)/shard_map/ppermute | solution.py:361
  174.7 6.0 %collective-permute-start.22 = (bf16[4,104,128]{2,1,0:T(8,128)(2,1)S(1)}, bf16[4,104,128]{2,1,0:T(8,128)(2,1)S(1)}, u32[]{:S(2)}, u32[]{:S(2)}) collective-permute-start(bf16[4,104,128]{2,1,0:T(8,128)(2,1)S(1)} %get-tuple-element.38), channel_id=1, source_target_pairs={{0,192},{32,224},{64,0},{96,32},{128,64},{160,96},{192,128},{224,1... | collective-permute-start | bytes 319496 | tf_op jit(solution)/shard_map/ppermute | solution.py:361
  180.7 11.3 %collective-permute-start.23 = (bf16[4,104,128]{2,1,0:T(8,128)(2,1)S(1)}, bf16[4,104,128]{2,1,0:T(8,128)(2,1)S(1)}, u32[]{:S(2)}, u32[]{:S(2)}) collective-permute-start(bf16[4,104,128]{2,1,0:T(8,128)(2,1)S(1)} %shard_map.132.a_ref), channel_id=1, source_target_pairs={{0,32},{32,0},{64,96},{96,64},{128,160},{160,128},{192,224},{224,1... | collective-permute-start | bytes 319496 | tf_op jit(solution)/shard_map/ppermute | solution.py:365
  192.0 7.1 %collective-permute-start.24 = (bf16[4,104,128]{2,1,0:T(8,128)(2,1)S(1)}, bf16[4,104,128]{2,1,0:T(8,128)(2,1)S(1)}, u32[]{:S(2)}, u32[]{:S(2)}) collective-permute-start(bf16[4,104,128]{2,1,0:T(8,128)(2,1)S(1)} %shard_map.133.q0_ref), channel_id=1, source_target_pairs={{0,64},{32,96},{64,128},{96,160},{128,192},{160,224},{192,0},{224,... | collective-permute-start | bytes 319496 | tf_op jit(solution)/shard_map/ppermute | solution.py:361
  193.3 7.1 %collective-permute-start.25 = (bf16[4,104,128]{2,1,0:T(8,128)(2,1)S(1)}, bf16[4,104,128]{2,1,0:T(8,128)(2,1)S(1)}, u32[]{:S(2)}, u32[]{:S(2)}) collective-permute-start(bf16[4,104,128]{2,1,0:T(8,128)(2,1)S(1)} %shard_map.133.q0_ref), channel_id=1, source_target_pairs={{0,128},{32,160},{64,192},{96,224},{128,0},{160,32},{192,64},{224,... | collective-permute-start | bytes 319496 | tf_op jit(solution)/shard_map/ppermute | solution.py:361
  195.9 4.8 %collective-permute-start.26 = (bf16[4,104,128]{2,1,0:T(8,128)(2,1)S(1)}, bf16[4,104,128]{2,1,0:T(8,128)(2,1)S(1)}, u32[]{:S(2)}, u32[]{:S(2)}) collective-permute-start(bf16[4,104,128]{2,1,0:T(8,128)(2,1)S(1)} %shard_map.133.q0_ref), channel_id=1, source_target_pairs={{0,192},{32,224},{64,0},{96,32},{128,64},{160,96},{192,128},{224,1... | collective-permute-start | bytes 319496 | tf_op jit(solution)/shard_map/ppermute | solution.py:361
  (11 other events, 23.4 us)

commit v3 on v2

--- a/solution.py
+++ b/solution.py
@@ -19,6 +19,7 @@
 LOG2E = 1.4426950408889634
 KEY_CHUNK = 256
 SHIFTS = (0, 1, 3, 2)
+HALVES = (slice(0, 256), slice(256, 512))
 
 BF16 = jnp.bfloat16
 F32 = jnp.float32
@@ -41,7 +42,13 @@
     return pl.BlockSpec(memory_space=pltpu.SMEM)
 
 
-def pack_kernel(ids_ref, down_ref, up_ref, pair_ref, out_ref):
+def pack_kernel(ids_ref, end_ref, down_ref, up_ref, pair_ref, out_ref, place_ref):
+    lane = lax.axis_index("wide")
+    group = lax.axis_index("prompt")
+    numbers = (lane // 8, lax.rem(lane // 2, 4), lax.rem(lane, 2), end_ref[0, 0])
+    for i, value in enumerate(numbers + (group // 2, lax.rem(group, 2))):
+        place_ref[i] = value
+
     def step(n, carry):
         a = ids_ref[0, n]
         for p in range(4):
@@ -58,15 +65,52 @@
     lax.fori_loop(0, WIDE, step, 0)
 
 
-def pack(ids, down, up, pairs):
+def pack(ids, end, down, up, pairs):
     return pl.pallas_call(
         pack_kernel,
-        out_shape=jax.ShapeDtypeStruct((WIDE, ROWS, 128), BF16),
-        in_specs=[smem()] + vmem(3),
+        out_shape=(
+            jax.ShapeDtypeStruct((WIDE, ROWS, 128), BF16),
+            jax.ShapeDtypeStruct((8,), jnp.int32),
+        ),
+        in_specs=[smem(), smem()] + vmem(3),
+        out_specs=(pl.BlockSpec(memory_space=pltpu.VMEM), smem()),
+        compiler_params=pltpu.CompilerParams(vmem_limit_bytes=4 << 20),
+        name="pack",
+    )(ids, end, down, up, pairs)
+
+
+def split_kernel(prompt_ref, first_ref, second_ref):
+    for part, ref in enumerate((first_ref, second_ref)):
+        ref[:, :512] = prompt_ref[0, :, 512 * part : 512 * part + 512]
+        ref[:, 512:] = prompt_ref[0, :, 1024 + 512 * part : 1536 + 512 * part]
+
+
+def split_prompt(prompt):
+    half = jax.ShapeDtypeStruct((64, 1024), BF16)
+    return pl.pallas_call(
+        split_kernel,
+        out_shape=(half, half),
+        in_specs=vmem(1),
+        out_specs=tuple(vmem(2)),
+        compiler_params=pltpu.CompilerParams(vmem_limit_bytes=2 << 20),
+        name="split",
+    )(prompt)
+
+
+def column_kernel(a_ref, b_ref, c_ref, d_ref, out_ref):
+    for i, ref in enumerate((a_ref, b_ref, c_ref, d_ref)):
+        out_ref[i] = ref[...]
+
+
+def column_of(pieces):
+    return pl.pallas_call(
+        column_kernel,
+        out_shape=jax.ShapeDtypeStruct((4, 64, 1024), BF16),
+        in_specs=vmem(4),
         out_specs=pl.BlockSpec(memory_space=pltpu.VMEM),
         compiler_params=pltpu.CompilerParams(vmem_limit_bytes=4 << 20),
-        name="pack",
-    )(ids, down, up, pairs)
+        name="column",
+    )(*pieces)
 
 
 def wide_rows(ref, start, stop):
@@ -118,7 +162,7 @@
         ),
         in_specs=vmem(6),
         out_specs=tuple(vmem(6)),
-        compiler_params=pltpu.CompilerParams(vmem_limit_bytes=28 << 20),
+        compiler_params=pltpu.CompilerParams(vmem_limit_bytes=12 << 20),
         name="prep",
     )(mine, x, fq, ckv, oc, cc)
 
@@ -162,7 +206,8 @@
     peak = jnp.max(peak, axis=1, keepdims=True) * factor
     own_p = jnp.exp2(own_s * factor - peak)
     total = own_p
-    weighted = dot(own_p.astype(BF16), own_v, NN)
+    own_p16 = own_p.astype(BF16)
+    weighted = [dot(own_p16[r], own_v, NN) for r in HALVES]
     for j in range(8):
         rows = slice(KEY_CHUNK * j, KEY_CHUNK * (j + 1))
         p = jnp.exp2(s_ref[:, rows] * factor - peak)
@@ -170,19 +215,21 @@
             total = total + p[:, 128 * t : 128 * t + 128]
         p16 = p.astype(BF16)
         p_ref[:, rows] = p16
-        weighted = weighted + dot(p16, v_refs[j][...].reshape(KEY_CHUNK, 128), NN)
+        value = v_refs[j][...].reshape(KEY_CHUNK, 128)
+        weighted = [w + dot(p16[r], value, NN) for w, r in zip(weighted, HALVES)]
     total = jnp.sum(total, axis=1, keepdims=True)
-    context = (weighted / total).astype(BF16)
+    context = (jnp.concatenate(weighted, axis=0) / total).astype(BF16)
     delta = jnp.sum(cg4.astype(F32) * context.astype(F32), axis=1, keepdims=True)
     attention = own_p / total
     own_ds = (attention * (dot(cg4, own_v, NT) - delta)).astype(BF16)
-    grad = jnp.zeros((512, 128), F32)
+    grad = [jnp.zeros((256, 128), F32)] * 2
     for j in range(8):
         rows = slice(KEY_CHUNK * j, KEY_CHUNK * (j + 1))
         dp = dot(cg4, v_refs[j][...].reshape(KEY_CHUNK, 128), NT)
         ds = (p_ref[:, rows].astype(F32) * (dp - delta)).astype(BF16)
-        grad = grad + dot(ds, k_refs[j][...].reshape(KEY_CHUNK, 128), NN)
-    grad = (grad / total + dot(own_ds, own_k, NN)) * INVERSE_ROOT
+        key = k_refs[j][...].reshape(KEY_CHUNK, 128)
+        grad = [w + dot(ds[r], key, NN) for w, r in zip(grad, HALVES)]
+    grad = (jnp.concatenate(grad, axis=0) / total + dot(own_ds, own_k, NN)) * INVERSE_ROOT
     grad = grad.astype(BF16)
     for g in range(4):
         ctx_ref[:, 128 * g : 128 * g + 128] = context[128 * g : 128 * g + 128]
@@ -191,7 +238,7 @@
     dv_ref[...] = dot(attention.astype(BF16), cg4, TN).astype(BF16)
 
 
-def attention_call(part, limits, q, cg, own, pieces):
+def attention_call(part, place, q, cg, own, pieces):
     first = 4 * part
     heads_in = pl.BlockSpec((BLOCK, 512), lambda k: (0, k + first))
     heads = pl.BlockSpec((BLOCK, 512), lambda k: (0, k))
@@ -220,12 +267,12 @@
             pltpu.VMEM((512, 2048), BF16),
         ],
         compiler_params=pltpu.CompilerParams(
-            dimension_semantics=("arbitrary",), vmem_limit_bytes=24 << 20
+            dimension_semantics=("arbitrary",), vmem_limit_bytes=18 << 20
         ),
         cost_estimate=pl.CostEstimate(
             flops=12_000_000_000, bytes_accessed=8_000_000, transcendentals=4_000_000
         ),
-    )(limits, q, cg, own, own, *pieces, *pieces)
+    )(place, q, cg, own, own, *pieces, *pieces)
 
 
 def grads_kernel(
@@ -266,7 +313,7 @@
         out_shape=jax.ShapeDtypeStruct((WIDE, ROWS, 128), BF16),
         in_specs=vmem(14),
         out_specs=pl.BlockSpec(memory_space=pltpu.VMEM),
-        compiler_params=pltpu.CompilerParams(vmem_limit_bytes=28 << 20),
+        compiler_params=pltpu.CompilerParams(vmem_limit_bytes=12 << 20),
         name="grads",
     )(mine, x, oc, low, up_out, pairs, *halves)
 
@@ -280,7 +327,7 @@
         return carry
 
     lax.fori_loop(0, WIDE, step, 0)
-    y = lane_ref[0]
+    y = lane_ref[4]
     mine_ref[...] = acc_ref[pl.ds(4 * y, 4)]
     for shift, ref in ((1, o1_ref), (2, o2_ref), (3, o3_ref)):
         ref[...] = acc_ref[pl.ds(4 * lax.rem(y + shift, 4), 4)].astype(BF16)
@@ -326,7 +373,7 @@
 
 
 def unpack_kernel(lane_ref, q0_ref, q1_ref, q2_ref, q3_ref, down_ref, up_ref, pair_ref):
-    y = lane_ref[0]
+    y = lane_ref[4]
     for shift, ref in ((0, q0_ref), (1, q1_ref), (2, q2_ref), (3, q3_ref)):
         first = 4 * lax.rem(y + 4 - shift, 4)
         for t in range(4):
@@ -377,12 +424,9 @@
     return lax.ppermute(value, "wide", pairs)
 
 
-def gather_part(prompt, part):
-    keys = prompt[:, 512 * part : 512 * part + 512]
-    values = prompt[:, 1024 + 512 * part : 1536 + 512 * part]
-    mine = jnp.concatenate([keys, values], axis=1)
+def gather_part(mine):
     moved = [wide_move(mine, 0, s, 0) for s in (1, 2, 3)]
-    column = jnp.stack([mine] + moved)
+    column = column_of([mine] + moved)
     return [column] + [wide_move(column, s, 0, 0) for s in (1, 3, 2)]
 
 
@@ -391,15 +435,14 @@
     prompt_block_end, adapter_down, adapter_up, adapter_up_key_value, output_cotangent,
     context_cotangent,
 ):
-    group = lax.axis_index("prompt")
-    place = jnp.stack([group // 2, group % 2]).astype(jnp.int32)
-    lane = lax.axis_index("wide")
-    limits = jnp.stack([lane // 8, lane // 2 % 4, lane % 2, prompt_block_end[0, 0]]).astype(jnp.int32)
-    sent = pack(candidate_adapter, adapter_down, adapter_up, adapter_up_key_value)
+    prompts = split_prompt(prompt_key_value)
+    sent, place = pack(
+        candidate_adapter, prompt_block_end, adapter_down, adapter_up, adapter_up_key_value
+    )
     mine = lax.all_to_all(sent, "wide", 0, 0, tiled=True)
     parts = []
     for part in range(2):
-        pieces = gather_part(prompt_key_value[0], part)
+        pieces = gather_part(prompts[part])
         parts.append(pieces + [wide_move(piece, 0, 0, 1) for piece in pieces])
     q, own, cg, low, up_out, pairs = prep(
         mine, candidate_hidden, frozen_query, candidate_key_value, output_cotangent,
@@ -407,7 +450,7 @@
     )
     halves = []
     for part in range(2):
-        halves += attention_call(part, limits, q, cg, own, parts[part])
+        halves += attention_call(part, place, q, cg, own, parts[part])
     blocks = grads(mine, candidate_hidden, output_cotangent, low, up_out, pairs, *halves)
     back = lax.all_to_all(blocks, "wide", 0, 0, tiled=True)
     total, *others = combine(candidate_adapter, place, back)

time: 204 us -> 199 us (0.975)
  blocking collectives: 0 us -> 31.6 us
  starting transfers between devices: 67 us -> 39 us
  Pallas kernels: 44.7 us -> 40.8 us
  waiting for transfers between devices: 79.2 us -> 76.5 us
    all_to_all x0 -> x1, blocking collectives: none -> 31.6 us  [step(): back = lax.all_to_all(blocks, 'wide', 0, 0, tiled=True)]
    ppermute x20, starting transfers between devices: 35.1 us -> 14.1 us  [wide_move(): return lax.ppermute(value, 'wide', pairs)]
    all_to_all x1 -> x0, waiting for transfers between devices: 21 us -> none  [step(): back = lax.all_to_all(blocks, 'wide', 0, 0, tiled=True)]
    ppermute x20, waiting for transfers between devices: 43.6 us -> 61.8 us  [wide_move(): return lax.ppermute(value, 'wide', pairs)]
    all_to_all x1 -> x0, starting transfers between devices: 6.95 us -> none  [step(): back = lax.all_to_all(blocks, 'wide', 0, 0, tiled=True)]
    pallas_call x2, Pallas kernels: 34.4 us -> 29.6 us  [attention_call(): pl.pallas_call(attention_kernel, grid=(4,), out_shape=(jax.ShapeDtypeStru...]
    pallas_call x1 -> x4, Pallas kernels: 3.85 us -> 4.75 us  [the longest x1 3.88 us: pack(): pl.pallas_call(pack_kernel, out_shape=(jax.ShapeDtypeStruct((WIDE, ROWS,...]
  transfers between devices with their start and end apart: 29 -> 28, of which waited for: 13 -> 12; matrix products, arithmetic and copies ran while one was open for 1% -> 0% of each run, Pallas kernels for 9% -> 9%
where the time goes in v3:
time: 199 us; the launch traced here: 197 us
  waiting for transfers between devices  76.5 us (38%)
  Pallas kernels  40.8 us (21%)
  starting transfers between devices  39 us (20%)
  blocking collectives  31.6 us (16%)
  local copies, waits for them, and re-layouts  7.86 us (4%)
    ppermute x20, waiting for transfers between devices, wide_move(): return lax.ppermute(value, 'wide', pairs)  61.8 us
    all_to_all x1, blocking collectives, step(): back = lax.all_to_all(blocks, 'wide', 0, 0, tiled=True)  31.6 us
    pallas_call x2, Pallas kernels, attention_call(): pl.pallas_call(attention_kernel, grid=(4,), out_shape=(jax.ShapeDtypeStru...  29.6 us
    ppermute x20, starting transfers between devices, wide_move(): return lax.ppermute(value, 'wide', pairs)  14.1 us
    ppermute x6, starting transfers between devices, y_shift(): return lax.ppermute(value, 'prompt', pairs)  11.2 us
    all_to_all x1, starting transfers between devices, step(): mine = lax.all_to_all(sent, 'wide', 0, 0, tiled=True)  9.17 us
    ppermute x6, waiting for transfers between devices, y_shift(): return lax.ppermute(value, 'prompt', pairs)  7.97 us
    unnamed x28, local copies, waits for them, and re-layouts  7.86 us
  transfers between devices with their start and end apart: 28, of which 12 were waited for; matrix products, arithmetic and copies ran while one was open for 0% of the time, Pallas kernels for 9%

profile of v3, /device:TPU:4, one launch (start us, length us, event | category | flops | bytes accessed | tf_op | source)
XLA Modules:
  0.0 197.3 jit_solution(5694340188757301288)
XLA Ops:
  4.1 3.9 %pack.1 = (bf16[32,104,128]{2,1,0:T(8,128)(2,1)}, s32[8]{0:T(128)S(1)}) custom-call(s32[1,32]{1,0:T(1,128)S(1)} %copy-done.9, s32[1,1]{1,0:T(1,128)S(6)} %copy.14.end_ref, bf16[16,4,16,128]{3,2,1,0:T(8,128)(2,1)S(1)} %copy-done.5, bf16[16,2,16,128]{3,2,1,0:T(8,128)(2,1)S(1)} %copy-done.7, bf16[16,2,16,32]{3,2,1,0:T(8,128)(2,1)S(1)} %copy-done.8), custom_call_target="tpu_custom_call" | custom-call | tf_op jit(solution)/shard_map/pack/pallas_call | solution.py:69
  8.0 9.2 %all-to-all-start = ((bf16[32,104,128]{2,1,0:T(8,128)(2,1)}), bf16[32,104,128]{2,1,0:T(8,128)(2,1)S(1)}, u32[]{:S(2)}, u32[]{:S(2)}) async-start(bf16[32,104,128]{2,1,0:T(8,128)(2,1)} %get-tuple-element.26), calls=%async_computation | async-start | bytes 1703936 | tf_op jit(solution)/shard_map/all_to_all | solution.py:442
  17.2 1.5 collective-permute-start
  18.7 2.4 %collective-permute-start.1 = (bf16[64,1024]{1,0:T(8,128)(2,1)S(1)}, bf16[64,1024]{1,0:T(8,128)(2,1)S(1)}, u32[]{:S(2)}, u32[]{:S(2)}) collective-permute-start(bf16[64,1024]{1,0:T(8,128)(2,1)S(1)} %get-tuple-element.33.a_ref), channel_id=1, source_target_pairs={{0,4},{1,5},{2,6},{3,7},{4,0},{5,1},{6,2},{7,3},{8,12},{9,13},{10,... | collective-permute-start | bytes 393224 | tf_op jit(solution)/shard_map/ppermute | solution.py:424
  21.1 1.4 collective-permute-start.2
  23.7 14.9 %collective-permute-done.b_ref = bf16[64,1024]{1,0:T(8,128)(2,1)S(1)} collective-permute-done((bf16[64,1024]{1,0:T(8,128)(2,1)S(1)}, bf16[64,1024]{1,0:T(8,128)(2,1)S(1)}, u32[]{:S(2)}, u32[]{:S(2)}) %collective-permute-start) | collective-permute-done | bytes 131104 | tf_op jit(solution)/shard_map/ppermute | solution.py:424
  38.6 14.9 %collective-permute-done.1.c_ref = bf16[64,1024]{1,0:T(8,128)(2,1)S(1)} collective-permute-done((bf16[64,1024]{1,0:T(8,128)(2,1)S(1)}, bf16[64,1024]{1,0:T(8,128)(2,1)S(1)}, u32[]{:S(2)}, u32[]{:S(2)}) %collective-permute-start.1) | collective-permute-done | bytes 131104 | tf_op jit(solution)/shard_map/ppermute | solution.py:424
  53.5 1.3 collective-permute-start.3
  55.6 1.8 collective-permute-start.5
  57.4 1.7 collective-permute-done.11.c_ref
  59.9 1.2 collective-permute-start.13
  61.1 18.5 %collective-permute-done.3.refs_1_.refs_9_ = bf16[4,64,1024]{2,1,0:T(8,128)(2,1)} collective-permute-done((bf16[4,64,1024]{2,1,0:T(8,128)(2,1)S(1)}, bf16[4,64,1024]{2,1,0:T(8,128)(2,1)}, u32[]{:S(2)}, u32[]{:S(2)}) %collective-permute-start.3) | collective-permute-done | bytes 524320 | tf_op jit(solution)/shard_map/ppermute | solution.py:424
  81.8 9.1 %collective-permute-done.13.refs_1_.refs_9_ = bf16[4,64,1024]{2,1,0:T(8,128)(2,1)S(1)} collective-permute-done((bf16[4,64,1024]{2,1,0:T(8,128)(2,1)}, bf16[4,64,1024]{2,1,0:T(8,128)(2,1)S(1)}, u32[]{:S(2)}, u32[]{:S(2)}) %collective-permute-start.13) | collective-permute-done | bytes 524320 | tf_op jit(solution)/shard_map/ppermute | solution.py:424
  91.7 1.2 copy-done.2
  92.9 1.2 copy-done.3
  95.2 1.8 prep.1
  97.5 2.7 %collective-permute-done.15.refs_3_.refs_11_ = bf16[4,64,1024]{2,1,0:T(8,128)(2,1)} collective-permute-done((bf16[4,64,1024]{2,1,0:T(8,128)(2,1)}, bf16[4,64,1024]{2,1,0:T(8,128)(2,1)}, u32[]{:S(2)}, u32[]{:S(2)}) %collective-permute-start.15) | collective-permute-done | bytes 524320 | tf_op jit(solution)/shard_map/ppermute | solution.py:424
  100.8 14.8 %shard_map.130 = (bf16[128,2048]{1,0:T(8,128)(2,1)S(1)}, bf16[128,2048]{1,0:T(8,128)(2,1)S(1)}, bf16[128,512]{1,0:T(8,128)(2,1)S(1)}, bf16[128,512]{1,0:T(8,128)(2,1)S(1)}) custom-call(s32[8]{0:T(128)S(1)} %get-tuple-element.25.limit_ref.lane_ref, bf16[128,4096]{1,0:T(8,128)(2,1)S(1)} %get-tuple-element.30.q_ref, ...), custom_call_target="tpu_custom_call" | custom-call | flops 12000000000 | bytes 8000000 | tf_op jit(solution)/shard_map/pallas_call | solution.py:246
  115.7 14.8 %shard_map.131 = (bf16[128,2048]{1,0:T(8,128)(2,1)S(1)}, bf16[128,2048]{1,0:T(8,128)(2,1)S(1)}, bf16[128,512]{1,0:T(8,128)(2,1)S(1)}, bf16[128,512]{1,0:T(8,128)(2,1)S(1)}) custom-call(s32[8]{0:T(128)S(1)} %get-tuple-element.25.limit_ref.lane_ref, bf16[128,4096]{1,0:T(8,128)(2,1)S(1)} %get-tuple-element.30.q_ref, ...), custom_call_target="tpu_custom_call" | custom-call | flops 12000000000 | bytes 8000000 | tf_op jit(solution)/shard_map/pallas_call | solution.py:246
  130.5 2.1 %grads.1 = bf16[32,104,128]{2,1,0:T(8,128)(2,1)S(1)} custom-call(bf16[32,104,128]{2,1,0:T(8,128)(2,1)S(1)} %all-to-all-done.mine_ref, bf16[1,128,4096]{2,1,0:T(8,128)(2,1)S(1)} %copy-done, bf16[1,128,4096]{2,1,0:T(8,128)(2,1)S(1)} %copy-done.1, bf16[48,128]{1,0:T(8,128)(2,1)S(1)} %get-tuple-element.27.low_ref, ...), custom_call_target="tpu_custom_call" | custom-call | tf_op jit(solution)/shard_map/grads/pallas_call | solution.py:311
  132.6 31.6 %all_to_all.10.back_ref = bf16[32,104,128]{2,1,0:T(8,128)(2,1)S(1)} all-to-all(bf16[32,104,128]{2,1,0:T(8,128)(2,1)S(1)} %grads.1), channel_id=1, replica_groups=mesh['prompt'=8,'wide'=32] {'wide'}, dimensions={0} | all-to-all | bytes 1703936 | tf_op jit(solution)/shard_map/all_to_all | solution.py:455
  165.2 1.7 collective-permute-start.20
  166.8 2.9 %collective-permute-start.21 = (bf16[4,104,128]{2,1,0:T(8,128)(2,1)S(1)}, bf16[4,104,128]{2,1,0:T(8,128)(2,1)S(1)}, u32[]{:S(2)}, u32[]{:S(2)}) collective-permute-start(bf16[4,104,128]{2,1,0:T(8,128)(2,1)S(1)} %get-tuple-element.45), channel_id=1, source_target_pairs={{0,128},{32,160},{64,192},{96,224},{128,0},{160,32},{192,64},{224,... | collective-permute-start | bytes 319496 | tf_op jit(solution)/shard_map/ppermute | solution.py:408
  169.7 1.3 collective-permute-start.22
  172.1 3.6 %collective-permute-done.21.r2_ref = bf16[4,104,128]{2,1,0:T(8,128)(2,1)S(1)} collective-permute-done((bf16[4,104,128]{2,1,0:T(8,128)(2,1)S(1)}, bf16[4,104,128]{2,1,0:T(8,128)(2,1)S(1)}, u32[]{:S(2)}, u32[]{:S(2)}) %collective-permute-start.21) | collective-permute-done | bytes 106528 | tf_op jit(solution)/shard_map/ppermute | solution.py:408
  175.8 4.6 %collective-permute-start.23 = (bf16[4,104,128]{2,1,0:T(8,128)(2,1)S(1)}, bf16[4,104,128]{2,1,0:T(8,128)(2,1)S(1)}, u32[]{:S(2)}, u32[]{:S(2)}) collective-permute-start(bf16[4,104,128]{2,1,0:T(8,128)(2,1)S(1)} %shard_map.132.a_ref), channel_id=1, source_target_pairs={{0,32},{32,0},{64,96},{96,64},{128,160},{160,128},{192,224},{224,1... | collective-permute-start | bytes 319496 | tf_op jit(solution)/shard_map/ppermute | solution.py:412
  180.3 6.7 %collective-permute-done.23.b_ref = bf16[4,104,128]{2,1,0:T(8,128)(2,1)S(1)} collective-permute-done((bf16[4,104,128]{2,1,0:T(8,128)(2,1)S(1)}, bf16[4,104,128]{2,1,0:T(8,128)(2,1)S(1)}, u32[]{:S(2)}, u32[]{:S(2)}) %collective-permute-start.23) | collective-permute-done | bytes 106528 | tf_op jit(solution)/shard_map/ppermute | solution.py:412
  187.1 1.2 collective-permute-start.24
  188.3 2.7 %collective-permute-start.25 = (bf16[4,104,128]{2,1,0:T(8,128)(2,1)S(1)}, bf16[4,104,128]{2,1,0:T(8,128)(2,1)S(1)}, u32[]{:S(2)}, u32[]{:S(2)}) collective-permute-start(bf16[4,104,128]{2,1,0:T(8,128)(2,1)S(1)} %shard_map.133.q0_ref), channel_id=1, source_target_pairs={{0,128},{32,160},{64,192},{96,224},{128,0},{160,32},{192,64},{224,... | collective-permute-start | bytes 319496 | tf_op jit(solution)/shard_map/ppermute | solution.py:408
  190.9 1.4 collective-permute-start.26
  192.4 1.8 collective-permute-done.24.q1_ref
  195.7 1.5 unpack.1
  (65 shorter events, 14.4 us)
Async XLA Ops:
  8.0 9.2 %copy-start.6 = (bf16[1,64,2048]{2,1,0:T(8,128)(2,1)S(1)}, bf16[1,64,2048]{2,1,0:T(8,128)(2,1)}, u32[]{:S(2)}) copy-start(bf16[1,64,2048]{2,1,0:T(8,128)(2,1)} %prompt_ref.1) | copy-start | bytes 786436
  8.0 83.7 %all-to-all-start = ((bf16[32,104,128]{2,1,0:T(8,128)(2,1)}), bf16[32,104,128]{2,1,0:T(8,128)(2,1)S(1)}, u32[]{:S(2)}, u32[]{:S(2)}) async-start(bf16[32,104,128]{2,1,0:T(8,128)(2,1)} %get-tuple-element.26), calls=%async_computation | async-start | bytes 1703936 | tf_op jit(solution)/shard_map/all_to_all | solution.py:442
  17.2 21.4 %collective-permute-start = (bf16[64,1024]{1,0:T(8,128)(2,1)S(1)}, bf16[64,1024]{1,0:T(8,128)(2,1)S(1)}, u32[]{:S(2)}, u32[]{:S(2)}) collective-permute-start(bf16[64,1024]{1,0:T(8,128)(2,1)S(1)} %get-tuple-element.33.a_ref), channel_id=1, source_target_pairs={{0,2},{1,3},{2,4},{3,5},{4,6},{5,7},{6,0},{7,1},{8,10},{9,11},{10,... | collective-permute-start | bytes 393224 | tf_op jit(solution)/shard_map/ppermute | solution.py:424
  18.7 34.7 %collective-permute-start.1 = (bf16[64,1024]{1,0:T(8,128)(2,1)S(1)}, bf16[64,1024]{1,0:T(8,128)(2,1)S(1)}, u32[]{:S(2)}, u32[]{:S(2)}) collective-permute-start(bf16[64,1024]{1,0:T(8,128)(2,1)S(1)} %get-tuple-element.33.a_ref), channel_id=1, source_target_pairs={{0,4},{1,5},{2,6},{3,7},{4,0},{5,1},{6,2},{7,3},{8,12},{9,13},{10,... | collective-permute-start | bytes 393224 | tf_op jit(solution)/shard_map/ppermute | solution.py:424
  21.1 32.3 %collective-permute-start.2 = (bf16[64,1024]{1,0:T(8,128)(2,1)S(1)}, bf16[64,1024]{1,0:T(8,128)(2,1)S(1)}, u32[]{:S(2)}, u32[]{:S(2)}) collective-permute-start(bf16[64,1024]{1,0:T(8,128)(2,1)S(1)} %get-tuple-element.33.a_ref), channel_id=1, source_target_pairs={{0,6},{1,7},{2,0},{3,1},{4,2},{5,3},{6,4},{7,5},{8,14},{9,15},{10,... | collective-permute-start | bytes 393224 | tf_op jit(solution)/shard_map/ppermute | solution.py:424
  22.6 69.1 %copy-start = (bf16[1,128,4096]{2,1,0:T(8,128)(2,1)S(1)}, bf16[1,128,4096]{2,1,0:T(8,128)(2,1)}, u32[]{:S(2)}) copy-start(bf16[1,128,4096]{2,1,0:T(8,128)(2,1)} %x_ref.3) | copy-start | bytes 3145732
  22.6 69.1 %copy-start.1 = (bf16[1,128,4096]{2,1,0:T(8,128)(2,1)S(1)}, bf16[1,128,4096]{2,1,0:T(8,128)(2,1)}, u32[]{:S(2)}) copy-start(bf16[1,128,4096]{2,1,0:T(8,128)(2,1)} %oc_ref.3) | copy-start | bytes 3145732
  22.6 33.0 %collective-permute-start.10 = (bf16[64,1024]{1,0:T(8,128)(2,1)S(1)}, bf16[64,1024]{1,0:T(8,128)(2,1)S(1)}, u32[]{:S(2)}, u32[]{:S(2)}) collective-permute-start(bf16[64,1024]{1,0:T(8,128)(2,1)S(1)} %get-tuple-element.38.a_ref), channel_id=1, source_target_pairs={{0,2},{1,3},{2,4},{3,5},{4,6},{5,7},{6,0},{7,1},{8,10},{9,11},{10,... | collective-permute-start | bytes 393224 | tf_op jit(solution)/shard_map/ppermute | solution.py:424
  23.1 35.9 %collective-permute-start.11 = (bf16[64,1024]{1,0:T(8,128)(2,1)S(1)}, bf16[64,1024]{1,0:T(8,128)(2,1)S(1)}, u32[]{:S(2)}, u32[]{:S(2)}) collective-permute-start(bf16[64,1024]{1,0:T(8,128)(2,1)S(1)} %get-tuple-element.38.a_ref), channel_id=1, source_target_pairs={{0,4},{1,5},{2,6},{3,7},{4,0},{5,1},{6,2},{7,3},{8,12},{9,13},{10,... | collective-permute-start | bytes 393224 | tf_op jit(solution)/shard_map/ppermute | solution.py:424
  38.6 20.5 %collective-permute-start.12 = (bf16[64,1024]{1,0:T(8,128)(2,1)S(1)}, bf16[64,1024]{1,0:T(8,128)(2,1)S(1)}, u32[]{:S(2)}, u32[]{:S(2)}) collective-permute-start(bf16[64,1024]{1,0:T(8,128)(2,1)S(1)} %get-tuple-element.38.a_ref), channel_id=1, source_target_pairs={{0,6},{1,7},{2,0},{3,1},{4,2},{5,3},{6,4},{7,5},{8,14},{9,15},{10,... | collective-permute-start | bytes 393224 | tf_op jit(solution)/shard_map/ppermute | solution.py:424
  53.5 26.2 %collective-permute-start.3 = (bf16[4,64,1024]{2,1,0:T(8,128)(2,1)S(1)}, bf16[4,64,1024]{2,1,0:T(8,128)(2,1)}, u32[]{:S(2)}, u32[]{:S(2)}) collective-permute-start(bf16[4,64,1024]{2,1,0:T(8,128)(2,1)S(1)} %column.2.refs_0_.refs_8_), channel_id=1, source_target_pairs={{0,8},{1,9},{2,10},{3,11},{4,12},{5,13},{6,14},{7,15},{8,16},{9,17... | collective-permute-start | bytes 1572872 | tf_op jit(solution)/shard_map/ppermute | solution.py:424
  54.8 24.9 %collective-permute-start.4 = (bf16[4,64,1024]{2,1,0:T(8,128)(2,1)S(1)}, bf16[4,64,1024]{2,1,0:T(8,128)(2,1)}, u32[]{:S(2)}, u32[]{:S(2)}) collective-permute-start(bf16[4,64,1024]{2,1,0:T(8,128)(2,1)S(1)} %column.2.refs_0_.refs_8_), channel_id=1, source_target_pairs={{0,24},{1,25},{2,26},{3,27},{4,28},{5,29},{6,30},{7,31},{8,0},{9,1... | collective-permute-start | bytes 1572872 | tf_op jit(solution)/shard_map/ppermute | solution.py:424
  55.6 24.8 %collective-permute-start.5 = (bf16[4,64,1024]{2,1,0:T(8,128)(2,1)S(1)}, bf16[4,64,1024]{2,1,0:T(8,128)(2,1)}, u32[]{:S(2)}, u32[]{:S(2)}) collective-permute-start(bf16[4,64,1024]{2,1,0:T(8,128)(2,1)S(1)} %column.2.refs_0_.refs_8_), channel_id=1, source_target_pairs={{0,16},{1,17},{2,18},{3,19},{4,20},{5,21},{6,22},{7,23},{8,24},{9,... | collective-permute-start | bytes 1572872 | tf_op jit(solution)/shard_map/ppermute | solution.py:424
  59.1 21.4 %collective-permute-start.6 = (bf16[4,64,1024]{2,1,0:T(8,128)(2,1)S(1)}, bf16[4,64,1024]{2,1,0:T(8,128)(2,1)S(1)}, u32[]{:S(2)}, u32[]{:S(2)}) collective-permute-start(bf16[4,64,1024]{2,1,0:T(8,128)(2,1)S(1)} %column.2.refs_0_.refs_8_), channel_id=1, source_target_pairs={{0,1},{1,0},{2,3},{3,2},{4,5},{5,4},{6,7},{7,6},{8,9},{9,8},{10,11... | collective-permute-start | bytes 1572872 | tf_op jit(solution)/shard_map/ppermute | solution.py:424
  59.9 30.9 %collective-permute-start.13 = (bf16[4,64,1024]{2,1,0:T(8,128)(2,1)}, bf16[4,64,1024]{2,1,0:T(8,128)(2,1)S(1)}, u32[]{:S(2)}, u32[]{:S(2)}) collective-permute-start(bf16[4,64,1024]{2,1,0:T(8,128)(2,1)} %column.3.refs_0_.refs_8_), channel_id=1, source_target_pairs={{0,8},{1,9},{2,10},{3,11},{4,12},{5,13},{6,14},{7,15},{8,16},{9,17... | collective-permute-start | bytes 1572872 | tf_op jit(solution)/shard_map/ppermute | solution.py:424
  79.7 17.3 %collective-permute-start.14 = (bf16[4,64,1024]{2,1,0:T(8,128)(2,1)}, bf16[4,64,1024]{2,1,0:T(8,128)(2,1)}, u32[]{:S(2)}, u32[]{:S(2)}) collective-permute-start(bf16[4,64,1024]{2,1,0:T(8,128)(2,1)} %column.3.refs_0_.refs_8_), channel_id=1, source_target_pairs={{0,24},{1,25},{2,26},{3,27},{4,28},{5,29},{6,30},{7,31},{8,0},{9,1... | collective-permute-start | bytes 1572872 | tf_op jit(solution)/shard_map/ppermute | solution.py:424
  79.7 20.5 %collective-permute-start.15 = (bf16[4,64,1024]{2,1,0:T(8,128)(2,1)}, bf16[4,64,1024]{2,1,0:T(8,128)(2,1)}, u32[]{:S(2)}, u32[]{:S(2)}) collective-permute-start(bf16[4,64,1024]{2,1,0:T(8,128)(2,1)} %column.3.refs_0_.refs_8_), channel_id=1, source_target_pairs={{0,16},{1,17},{2,18},{3,19},{4,20},{5,21},{6,22},{7,23},{8,24},{9,... | collective-permute-start | bytes 1572872 | tf_op jit(solution)/shard_map/ppermute | solution.py:424
  80.5 19.8 %collective-permute-start.7 = (bf16[4,64,1024]{2,1,0:T(8,128)(2,1)}, bf16[4,64,1024]{2,1,0:T(8,128)(2,1)}, u32[]{:S(2)}, u32[]{:S(2)}) collective-permute-start(bf16[4,64,1024]{2,1,0:T(8,128)(2,1)} %collective-permute-done.3.refs_1_.refs_9_), channel_id=1, source_target_pairs={{0,1},{1,0},{2,3},{3,2},{4,5},{5,4},{6,7},{7,6},{8,9},{9,8},{10,11... | collective-permute-start | bytes 1572872 | tf_op jit(solution)/shard_map/ppermute | solution.py:424
  81.3 19.5 %collective-permute-start.8 = (bf16[4,64,1024]{2,1,0:T(8,128)(2,1)}, bf16[4,64,1024]{2,1,0:T(8,128)(2,1)}, u32[]{:S(2)}, u32[]{:S(2)}) collective-permute-start(bf16[4,64,1024]{2,1,0:T(8,128)(2,1)} %collective-permute-done.4.refs_2_.refs_10_), channel_id=1, source_target_pairs={{0,1},{1,0},{2,3},{3,2},{4,5},{5,4},{6,7},{7,6},{8,9},{9,8},{10,11... | collective-permute-start | bytes 1572872 | tf_op jit(solution)/shard_map/ppermute | solution.py:424
  91.7 9.2 %collective-permute-start.9 = (bf16[4,64,1024]{2,1,0:T(8,128)(2,1)}, bf16[4,64,1024]{2,1,0:T(8,128)(2,1)}, u32[]{:S(2)}, u32[]{:S(2)}) collective-permute-start(bf16[4,64,1024]{2,1,0:T(8,128)(2,1)} %collective-permute-done.5.refs_3_.refs_11_), channel_id=1, source_target_pairs={{0,1},{1,0},{2,3},{3,2},{4,5},{5,4},{6,7},{7,6},{8,9},{9,8},{10,11... | collective-permute-start | bytes 1572872 | tf_op jit(solution)/shard_map/ppermute | solution.py:424
  95.2 5.7 %copy-start.13 = (bf16[4,64,1024]{2,1,0:T(8,128)(2,1)S(1)}, bf16[4,64,1024]{2,1,0:T(8,128)(2,1)}, u32[]{:S(2)}) copy-start(bf16[4,64,1024]{2,1,0:T(8,128)(2,1)} %copy-done.12) | copy-start | bytes 1572868
  96.9 18.7 %collective-permute-start.16 = (bf16[4,64,1024]{2,1,0:T(8,128)(2,1)}, bf16[4,64,1024]{2,1,0:T(8,128)(2,1)S(1)}, u32[]{:S(2)}, u32[]{:S(2)}) collective-permute-start(bf16[4,64,1024]{2,1,0:T(8,128)(2,1)} %column.3.refs_0_.refs_8_), channel_id=1, source_target_pairs={{0,1},{1,0},{2,3},{3,2},{4,5},{5,4},{6,7},{7,6},{8,9},{9,8},{10,11... | collective-permute-start | bytes 1572872 | tf_op jit(solution)/shard_map/ppermute | solution.py:424
  100.2 15.4 %collective-permute-start.17 = (bf16[4,64,1024]{2,1,0:T(8,128)(2,1)S(1)}, bf16[4,64,1024]{2,1,0:T(8,128)(2,1)S(1)}, u32[]{:S(2)}, u32[]{:S(2)}) collective-permute-start(bf16[4,64,1024]{2,1,0:T(8,128)(2,1)S(1)} %copy-done.11), channel_id=1, source_target_pairs={{0,1},{1,0},{2,3},{3,2},{4,5},{5,4},{6,7},{7,6},{8,9},{9,8},{10,11... | collective-permute-start | bytes 1572872 | tf_op jit(solution)/shard_map/ppermute | solution.py:424
  100.2 15.4 %collective-permute-start.18 = (bf16[4,64,1024]{2,1,0:T(8,128)(2,1)}, bf16[4,64,1024]{2,1,0:T(8,128)(2,1)S(1)}, u32[]{:S(2)}, u32[]{:S(2)}) collective-permute-start(bf16[4,64,1024]{2,1,0:T(8,128)(2,1)} %collective-permute-done.14.refs_2_.refs_10_), channel_id=1, source_target_pairs={{0,1},{1,0},{2,3},{3,2},{4,5},{5,4},{6,7},{7,6},{8,9},{9,8},{10,11... | collective-permute-start | bytes 1572872 | tf_op jit(solution)/shard_map/ppermute | solution.py:424
  100.7 14.9 %collective-permute-start.19 = (bf16[4,64,1024]{2,1,0:T(8,128)(2,1)}, bf16[4,64,1024]{2,1,0:T(8,128)(2,1)S(1)}, u32[]{:S(2)}, u32[]{:S(2)}) collective-permute-start(bf16[4,64,1024]{2,1,0:T(8,128)(2,1)} %collective-permute-done.15.refs_3_.refs_11_), channel_id=1, source_target_pairs={{0,1},{1,0},{2,3},{3,2},{4,5},{5,4},{6,7},{7,6},{8,9},{9,8},{10,11... | collective-permute-start | bytes 1572872 | tf_op jit(solution)/shard_map/ppermute | solution.py:424
  165.2 7.0 %collective-permute-start.20 = (bf16[4,104,128]{2,1,0:T(8,128)(2,1)S(1)}, bf16[4,104,128]{2,1,0:T(8,128)(2,1)S(1)}, u32[]{:S(2)}, u32[]{:S(2)}) collective-permute-start(bf16[4,104,128]{2,1,0:T(8,128)(2,1)S(1)} %get-tuple-element.44), channel_id=1, source_target_pairs={{0,64},{32,96},{64,128},{96,160},{128,192},{160,224},{192,0},{224,... | collective-permute-start | bytes 319496 | tf_op jit(solution)/shard_map/ppermute | solution.py:408
  166.8 8.9 %collective-permute-start.21 = (bf16[4,104,128]{2,1,0:T(8,128)(2,1)S(1)}, bf16[4,104,128]{2,1,0:T(8,128)(2,1)S(1)}, u32[]{:S(2)}, u32[]{:S(2)}) collective-permute-start(bf16[4,104,128]{2,1,0:T(8,128)(2,1)S(1)} %get-tuple-element.45), channel_id=1, source_target_pairs={{0,128},{32,160},{64,192},{96,224},{128,0},{160,32},{192,64},{224,... | collective-permute-start | bytes 319496 | tf_op jit(solution)/shard_map/ppermute | solution.py:408
  169.7 6.0 %collective-permute-start.22 = (bf16[4,104,128]{2,1,0:T(8,128)(2,1)S(1)}, bf16[4,104,128]{2,1,0:T(8,128)(2,1)S(1)}, u32[]{:S(2)}, u32[]{:S(2)}) collective-permute-start(bf16[4,104,128]{2,1,0:T(8,128)(2,1)S(1)} %get-tuple-element.46), channel_id=1, source_target_pairs={{0,192},{32,224},{64,0},{96,32},{128,64},{160,96},{192,128},{224,1... | collective-permute-start | bytes 319496 | tf_op jit(solution)/shard_map/ppermute | solution.py:408
  175.8 11.3 %collective-permute-start.23 = (bf16[4,104,128]{2,1,0:T(8,128)(2,1)S(1)}, bf16[4,104,128]{2,1,0:T(8,128)(2,1)S(1)}, u32[]{:S(2)}, u32[]{:S(2)}) collective-permute-start(bf16[4,104,128]{2,1,0:T(8,128)(2,1)S(1)} %shard_map.132.a_ref), channel_id=1, source_target_pairs={{0,32},{32,0},{64,96},{96,64},{128,160},{160,128},{192,224},{224,1... | collective-permute-start | bytes 319496 | tf_op jit(solution)/shard_map/ppermute | solution.py:412
  187.1 7.1 %collective-permute-start.24 = (bf16[4,104,128]{2,1,0:T(8,128)(2,1)S(1)}, bf16[4,104,128]{2,1,0:T(8,128)(2,1)S(1)}, u32[]{:S(2)}, u32[]{:S(2)}) collective-permute-start(bf16[4,104,128]{2,1,0:T(8,128)(2,1)S(1)} %shard_map.133.q0_ref), channel_id=1, source_target_pairs={{0,64},{32,96},{64,128},{96,160},{128,192},{160,224},{192,0},{224,... | collective-permute-start | bytes 319496 | tf_op jit(solution)/shard_map/ppermute | solution.py:408
  188.3 7.1 %collective-permute-start.25 = (bf16[4,104,128]{2,1,0:T(8,128)(2,1)S(1)}, bf16[4,104,128]{2,1,0:T(8,128)(2,1)S(1)}, u32[]{:S(2)}, u32[]{:S(2)}) collective-permute-start(bf16[4,104,128]{2,1,0:T(8,128)(2,1)S(1)} %shard_map.133.q0_ref), channel_id=1, source_target_pairs={{0,128},{32,160},{64,192},{96,224},{128,0},{160,32},{192,64},{224,... | collective-permute-start | bytes 319496 | tf_op jit(solution)/shard_map/ppermute | solution.py:408
  190.9 4.8 %collective-permute-start.26 = (bf16[4,104,128]{2,1,0:T(8,128)(2,1)S(1)}, bf16[4,104,128]{2,1,0:T(8,128)(2,1)S(1)}, u32[]{:S(2)}, u32[]{:S(2)}) collective-permute-start(bf16[4,104,128]{2,1,0:T(8,128)(2,1)S(1)} %shard_map.133.q0_ref), channel_id=1, source_target_pairs={{0,192},{32,224},{64,0},{96,32},{128,64},{160,96},{192,128},{224,1... | collective-permute-start | bytes 319496 | tf_op jit(solution)/shard_map/ppermute | solution.py:408
  (10 other events, 13.6 us)

commit v4 on v3

--- a/solution.py
+++ b/solution.py
@@ -42,27 +42,26 @@
     return pl.BlockSpec(memory_space=pltpu.SMEM)
 
 
-def pack_kernel(ids_ref, end_ref, down_ref, up_ref, pair_ref, out_ref, place_ref):
+def pack_kernel(ids_ref, end_ref, down_ref, up_ref, pair_ref, out_ref, place_ref, joined_ref):
     lane = lax.axis_index("wide")
     group = lax.axis_index("prompt")
     numbers = (lane // 8, lax.rem(lane // 2, 4), lax.rem(lane, 2), end_ref[0, 0])
     for i, value in enumerate(numbers + (group // 2, lax.rem(group, 2))):
         place_ref[i] = value
 
-    def step(n, carry):
+    for a in range(ADAPTERS):
+        pieces = []
+        for p in range(2):
+            pair = pair_ref[a, p].astype(F32)
+            pieces += [pair[:8], pair[8:]]
+        joined_ref[a] = jnp.concatenate(pieces, axis=1)
+    for n in range(WIDE):
         a = ids_ref[0, n]
         for p in range(4):
             out_ref[n, 16 * p : 16 * p + 16, :] = down_ref[a, p]
         for p in range(2):
             out_ref[n, 64 + 16 * p : 80 + 16 * p, :] = up_ref[a, p]
-        pieces = []
-        for p in range(2):
-            pair = pair_ref[a, p].astype(F32)
-            pieces += [pair[:8], pair[8:]]
-        out_ref[n, 96:104, :] = jnp.concatenate(pieces, axis=1).astype(BF16)
-        return carry
-
-    lax.fori_loop(0, WIDE, step, 0)
+        out_ref[n, 96:104, :] = joined_ref[a].astype(BF16)
 
 
 def pack(ids, end, down, up, pairs):
@@ -74,6 +73,7 @@
         ),
         in_specs=[smem(), smem()] + vmem(3),
         out_specs=(pl.BlockSpec(memory_space=pltpu.VMEM), smem()),
+        scratch_shapes=[pltpu.VMEM((ADAPTERS, 8, 128), F32)],
         compiler_params=pltpu.CompilerParams(vmem_limit_bytes=4 << 20),
         name="pack",
     )(ids, end, down, up, pairs)

time: 199 us -> 197 us (0.990)
  Pallas kernels: 40.8 us -> 38.5 us
    pallas_call x1, Pallas kernels: 3.88 us -> 1.59 us  [pack(): pl.pallas_call(pack_kernel, out_shape=(jax.ShapeDtypeStruct((WIDE, ROWS,...]
where the time goes in v4:
time: 197 us; the launch traced here: 195 us
  waiting for transfers between devices  76.5 us (39%)
  starting transfers between devices  39 us (20%)
  Pallas kernels  38.5 us (20%)
  blocking collectives  31.6 us (16%)
  local copies, waits for them, and re-layouts  7.86 us (4%)
    ppermute x20, waiting for transfers between devices, wide_move(): return lax.ppermute(value, 'wide', pairs)  61.8 us
    all_to_all x1, blocking collectives, step(): back = lax.all_to_all(blocks, 'wide', 0, 0, tiled=True)  31.6 us
    pallas_call x2, Pallas kernels, attention_call(): pl.pallas_call(attention_kernel, grid=(4,), out_shape=(jax.ShapeDtypeStru...  29.6 us
    ppermute x20, starting transfers between devices, wide_move(): return lax.ppermute(value, 'wide', pairs)  14 us
    ppermute x6, starting transfers between devices, y_shift(): return lax.ppermute(value, 'prompt', pairs)  11.2 us
    all_to_all x1, starting transfers between devices, step(): mine = lax.all_to_all(sent, 'wide', 0, 0, tiled=True)  9.17 us
    ppermute x6, waiting for transfers between devices, y_shift(): return lax.ppermute(value, 'prompt', pairs)  7.97 us
    unnamed x28, local copies, waits for them, and re-layouts  7.86 us
  transfers between devices with their start and end apart: 28, of which 12 were waited for; matrix products, arithmetic and copies ran while one was open for 0% of the time, Pallas kernels for 9%

profile of v4, /device:TPU:4, one launch (start us, length us, event | category | flops | bytes accessed | tf_op | source)
XLA Modules:
  0.0 195.0 jit_solution(10226913849093496266)
XLA Ops:
  4.1 1.6 pack.1
  5.7 9.2 %all-to-all-start = ((bf16[32,104,128]{2,1,0:T(8,128)(2,1)}), bf16[32,104,128]{2,1,0:T(8,128)(2,1)S(1)}, u32[]{:S(2)}, u32[]{:S(2)}) async-start(bf16[32,104,128]{2,1,0:T(8,128)(2,1)} %get-tuple-element.26), calls=%async_computation | async-start | bytes 1703936 | tf_op jit(solution)/shard_map/all_to_all | solution.py:442
  14.9 1.5 collective-permute-start
  16.4 2.4 %collective-permute-start.1 = (bf16[64,1024]{1,0:T(8,128)(2,1)S(1)}, bf16[64,1024]{1,0:T(8,128)(2,1)S(1)}, u32[]{:S(2)}, u32[]{:S(2)}) collective-permute-start(bf16[64,1024]{1,0:T(8,128)(2,1)S(1)} %get-tuple-element.33.a_ref), channel_id=1, source_target_pairs={{0,4},{1,5},{2,6},{3,7},{4,0},{5,1},{6,2},{7,3},{8,12},{9,13},{10,... | collective-permute-start | bytes 393224 | tf_op jit(solution)/shard_map/ppermute | solution.py:424
  18.8 1.4 collective-permute-start.2
  21.4 14.9 %collective-permute-done.b_ref = bf16[64,1024]{1,0:T(8,128)(2,1)S(1)} collective-permute-done((bf16[64,1024]{1,0:T(8,128)(2,1)S(1)}, bf16[64,1024]{1,0:T(8,128)(2,1)S(1)}, u32[]{:S(2)}, u32[]{:S(2)}) %collective-permute-start) | collective-permute-done | bytes 131104 | tf_op jit(solution)/shard_map/ppermute | solution.py:424
  36.3 14.9 %collective-permute-done.1.c_ref = bf16[64,1024]{1,0:T(8,128)(2,1)S(1)} collective-permute-done((bf16[64,1024]{1,0:T(8,128)(2,1)S(1)}, bf16[64,1024]{1,0:T(8,128)(2,1)S(1)}, u32[]{:S(2)}, u32[]{:S(2)}) %collective-permute-start.1) | collective-permute-done | bytes 131104 | tf_op jit(solution)/shard_map/ppermute | solution.py:424
  51.2 1.3 collective-permute-start.3
  53.3 1.8 collective-permute-start.5
  55.1 1.7 collective-permute-done.11.c_ref
  57.6 1.2 collective-permute-start.13
  58.8 18.5 %collective-permute-done.3.refs_1_.refs_9_ = bf16[4,64,1024]{2,1,0:T(8,128)(2,1)} collective-permute-done((bf16[4,64,1024]{2,1,0:T(8,128)(2,1)S(1)}, bf16[4,64,1024]{2,1,0:T(8,128)(2,1)}, u32[]{:S(2)}, u32[]{:S(2)}) %collective-permute-start.3) | collective-permute-done | bytes 524320 | tf_op jit(solution)/shard_map/ppermute | solution.py:424
  79.5 9.1 %collective-permute-done.13.refs_1_.refs_9_ = bf16[4,64,1024]{2,1,0:T(8,128)(2,1)S(1)} collective-permute-done((bf16[4,64,1024]{2,1,0:T(8,128)(2,1)}, bf16[4,64,1024]{2,1,0:T(8,128)(2,1)S(1)}, u32[]{:S(2)}, u32[]{:S(2)}) %collective-permute-start.13) | collective-permute-done | bytes 524320 | tf_op jit(solution)/shard_map/ppermute | solution.py:424
  89.4 1.2 copy-done.2
  90.6 1.2 copy-done.3
  92.9 1.8 prep.1
  95.2 2.7 %collective-permute-done.15.refs_3_.refs_11_ = bf16[4,64,1024]{2,1,0:T(8,128)(2,1)} collective-permute-done((bf16[4,64,1024]{2,1,0:T(8,128)(2,1)}, bf16[4,64,1024]{2,1,0:T(8,128)(2,1)}, u32[]{:S(2)}, u32[]{:S(2)}) %collective-permute-start.15) | collective-permute-done | bytes 524320 | tf_op jit(solution)/shard_map/ppermute | solution.py:424
  98.5 14.8 %shard_map.130 = (bf16[128,2048]{1,0:T(8,128)(2,1)S(1)}, bf16[128,2048]{1,0:T(8,128)(2,1)S(1)}, bf16[128,512]{1,0:T(8,128)(2,1)S(1)}, bf16[128,512]{1,0:T(8,128)(2,1)S(1)}) custom-call(s32[8]{0:T(128)S(1)} %get-tuple-element.25.limit_ref.lane_ref, bf16[128,4096]{1,0:T(8,128)(2,1)S(1)} %get-tuple-element.30.q_ref, ...), custom_call_target="tpu_custom_call" | custom-call | flops 12000000000 | bytes 8000000 | tf_op jit(solution)/shard_map/pallas_call | solution.py:246
  113.4 14.8 %shard_map.131 = (bf16[128,2048]{1,0:T(8,128)(2,1)S(1)}, bf16[128,2048]{1,0:T(8,128)(2,1)S(1)}, bf16[128,512]{1,0:T(8,128)(2,1)S(1)}, bf16[128,512]{1,0:T(8,128)(2,1)S(1)}) custom-call(s32[8]{0:T(128)S(1)} %get-tuple-element.25.limit_ref.lane_ref, bf16[128,4096]{1,0:T(8,128)(2,1)S(1)} %get-tuple-element.30.q_ref, ...), custom_call_target="tpu_custom_call" | custom-call | flops 12000000000 | bytes 8000000 | tf_op jit(solution)/shard_map/pallas_call | solution.py:246
  128.2 2.1 %grads.1 = bf16[32,104,128]{2,1,0:T(8,128)(2,1)S(1)} custom-call(bf16[32,104,128]{2,1,0:T(8,128)(2,1)S(1)} %all-to-all-done.mine_ref, bf16[1,128,4096]{2,1,0:T(8,128)(2,1)S(1)} %copy-done, bf16[1,128,4096]{2,1,0:T(8,128)(2,1)S(1)} %copy-done.1, bf16[48,128]{1,0:T(8,128)(2,1)S(1)} %get-tuple-element.27.low_ref, ...), custom_call_target="tpu_custom_call" | custom-call | tf_op jit(solution)/shard_map/grads/pallas_call | solution.py:311
  130.3 31.6 %all_to_all.10.back_ref = bf16[32,104,128]{2,1,0:T(8,128)(2,1)S(1)} all-to-all(bf16[32,104,128]{2,1,0:T(8,128)(2,1)S(1)} %grads.1), channel_id=1, replica_groups=mesh['prompt'=8,'wide'=32] {'wide'}, dimensions={0} | all-to-all | bytes 1703936 | tf_op jit(solution)/shard_map/all_to_all | solution.py:455
  162.9 1.6 collective-permute-start.20
  164.5 2.9 %collective-permute-start.21 = (bf16[4,104,128]{2,1,0:T(8,128)(2,1)S(1)}, bf16[4,104,128]{2,1,0:T(8,128)(2,1)S(1)}, u32[]{:S(2)}, u32[]{:S(2)}) collective-permute-start(bf16[4,104,128]{2,1,0:T(8,128)(2,1)S(1)} %get-tuple-element.45), channel_id=1, source_target_pairs={{0,128},{32,160},{64,192},{96,224},{128,0},{160,32},{192,64},{224,... | collective-permute-start | bytes 319496 | tf_op jit(solution)/shard_map/ppermute | solution.py:408
  167.4 1.3 collective-permute-start.22
  169.8 3.6 %collective-permute-done.21.r2_ref = bf16[4,104,128]{2,1,0:T(8,128)(2,1)S(1)} collective-permute-done((bf16[4,104,128]{2,1,0:T(8,128)(2,1)S(1)}, bf16[4,104,128]{2,1,0:T(8,128)(2,1)S(1)}, u32[]{:S(2)}, u32[]{:S(2)}) %collective-permute-start.21) | collective-permute-done | bytes 106528 | tf_op jit(solution)/shard_map/ppermute | solution.py:408
  173.5 4.6 %collective-permute-start.23 = (bf16[4,104,128]{2,1,0:T(8,128)(2,1)S(1)}, bf16[4,104,128]{2,1,0:T(8,128)(2,1)S(1)}, u32[]{:S(2)}, u32[]{:S(2)}) collective-permute-start(bf16[4,104,128]{2,1,0:T(8,128)(2,1)S(1)} %shard_map.132.a_ref), channel_id=1, source_target_pairs={{0,32},{32,0},{64,96},{96,64},{128,160},{160,128},{192,224},{224,1... | collective-permute-start | bytes 319496 | tf_op jit(solution)/shard_map/ppermute | solution.py:412
  178.1 6.7 %collective-permute-done.23.b_ref = bf16[4,104,128]{2,1,0:T(8,128)(2,1)S(1)} collective-permute-done((bf16[4,104,128]{2,1,0:T(8,128)(2,1)S(1)}, bf16[4,104,128]{2,1,0:T(8,128)(2,1)S(1)}, u32[]{:S(2)}, u32[]{:S(2)}) %collective-permute-start.23) | collective-permute-done | bytes 106528 | tf_op jit(solution)/shard_map/ppermute | solution.py:412
  184.8 1.2 collective-permute-start.24
  186.0 2.7 %collective-permute-start.25 = (bf16[4,104,128]{2,1,0:T(8,128)(2,1)S(1)}, bf16[4,104,128]{2,1,0:T(8,128)(2,1)S(1)}, u32[]{:S(2)}, u32[]{:S(2)}) collective-permute-start(bf16[4,104,128]{2,1,0:T(8,128)(2,1)S(1)} %shard_map.133.q0_ref), channel_id=1, source_target_pairs={{0,128},{32,160},{64,192},{96,224},{128,0},{160,32},{192,64},{224,... | collective-permute-start | bytes 319496 | tf_op jit(solution)/shard_map/ppermute | solution.py:408
  188.7 1.4 collective-permute-start.26
  190.1 1.8 collective-permute-done.24.q1_ref
  193.4 1.5 unpack.1
  (65 shorter events, 14.4 us)
Async XLA Ops:
  5.7 9.2 %copy-start.6 = (bf16[1,64,2048]{2,1,0:T(8,128)(2,1)S(1)}, bf16[1,64,2048]{2,1,0:T(8,128)(2,1)}, u32[]{:S(2)}) copy-start(bf16[1,64,2048]{2,1,0:T(8,128)(2,1)} %prompt_ref.1) | copy-start | bytes 786436
  5.7 83.7 %all-to-all-start = ((bf16[32,104,128]{2,1,0:T(8,128)(2,1)}), bf16[32,104,128]{2,1,0:T(8,128)(2,1)S(1)}, u32[]{:S(2)}, u32[]{:S(2)}) async-start(bf16[32,104,128]{2,1,0:T(8,128)(2,1)} %get-tuple-element.26), calls=%async_computation | async-start | bytes 1703936 | tf_op jit(solution)/shard_map/all_to_all | solution.py:442
  14.9 21.4 %collective-permute-start = (bf16[64,1024]{1,0:T(8,128)(2,1)S(1)}, bf16[64,1024]{1,0:T(8,128)(2,1)S(1)}, u32[]{:S(2)}, u32[]{:S(2)}) collective-permute-start(bf16[64,1024]{1,0:T(8,128)(2,1)S(1)} %get-tuple-element.33.a_ref), channel_id=1, source_target_pairs={{0,2},{1,3},{2,4},{3,5},{4,6},{5,7},{6,0},{7,1},{8,10},{9,11},{10,... | collective-permute-start | bytes 393224 | tf_op jit(solution)/shard_map/ppermute | solution.py:424
  16.4 34.7 %collective-permute-start.1 = (bf16[64,1024]{1,0:T(8,128)(2,1)S(1)}, bf16[64,1024]{1,0:T(8,128)(2,1)S(1)}, u32[]{:S(2)}, u32[]{:S(2)}) collective-permute-start(bf16[64,1024]{1,0:T(8,128)(2,1)S(1)} %get-tuple-element.33.a_ref), channel_id=1, source_target_pairs={{0,4},{1,5},{2,6},{3,7},{4,0},{5,1},{6,2},{7,3},{8,12},{9,13},{10,... | collective-permute-start | bytes 393224 | tf_op jit(solution)/shard_map/ppermute | solution.py:424
  18.8 32.3 %collective-permute-start.2 = (bf16[64,1024]{1,0:T(8,128)(2,1)S(1)}, bf16[64,1024]{1,0:T(8,128)(2,1)S(1)}, u32[]{:S(2)}, u32[]{:S(2)}) collective-permute-start(bf16[64,1024]{1,0:T(8,128)(2,1)S(1)} %get-tuple-element.33.a_ref), channel_id=1, source_target_pairs={{0,6},{1,7},{2,0},{3,1},{4,2},{5,3},{6,4},{7,5},{8,14},{9,15},{10,... | collective-permute-start | bytes 393224 | tf_op jit(solution)/shard_map/ppermute | solution.py:424
  20.3 69.1 %copy-start = (bf16[1,128,4096]{2,1,0:T(8,128)(2,1)S(1)}, bf16[1,128,4096]{2,1,0:T(8,128)(2,1)}, u32[]{:S(2)}) copy-start(bf16[1,128,4096]{2,1,0:T(8,128)(2,1)} %x_ref.3) | copy-start | bytes 3145732
  20.3 69.1 %copy-start.1 = (bf16[1,128,4096]{2,1,0:T(8,128)(2,1)S(1)}, bf16[1,128,4096]{2,1,0:T(8,128)(2,1)}, u32[]{:S(2)}) copy-start(bf16[1,128,4096]{2,1,0:T(8,128)(2,1)} %oc_ref.3) | copy-start | bytes 3145732
  20.3 33.0 %collective-permute-start.10 = (bf16[64,1024]{1,0:T(8,128)(2,1)S(1)}, bf16[64,1024]{1,0:T(8,128)(2,1)S(1)}, u32[]{:S(2)}, u32[]{:S(2)}) collective-permute-start(bf16[64,1024]{1,0:T(8,128)(2,1)S(1)} %get-tuple-element.38.a_ref), channel_id=1, source_target_pairs={{0,2},{1,3},{2,4},{3,5},{4,6},{5,7},{6,0},{7,1},{8,10},{9,11},{10,... | collective-permute-start | bytes 393224 | tf_op jit(solution)/shard_map/ppermute | solution.py:424
  20.9 35.9 %collective-permute-start.11 = (bf16[64,1024]{1,0:T(8,128)(2,1)S(1)}, bf16[64,1024]{1,0:T(8,128)(2,1)S(1)}, u32[]{:S(2)}, u32[]{:S(2)}) collective-permute-start(bf16[64,1024]{1,0:T(8,128)(2,1)S(1)} %get-tuple-element.38.a_ref), channel_id=1, source_target_pairs={{0,4},{1,5},{2,6},{3,7},{4,0},{5,1},{6,2},{7,3},{8,12},{9,13},{10,... | collective-permute-start | bytes 393224 | tf_op jit(solution)/shard_map/ppermute | solution.py:424
  36.3 20.5 %collective-permute-start.12 = (bf16[64,1024]{1,0:T(8,128)(2,1)S(1)}, bf16[64,1024]{1,0:T(8,128)(2,1)S(1)}, u32[]{:S(2)}, u32[]{:S(2)}) collective-permute-start(bf16[64,1024]{1,0:T(8,128)(2,1)S(1)} %get-tuple-element.38.a_ref), channel_id=1, source_target_pairs={{0,6},{1,7},{2,0},{3,1},{4,2},{5,3},{6,4},{7,5},{8,14},{9,15},{10,... | collective-permute-start | bytes 393224 | tf_op jit(solution)/shard_map/ppermute | solution.py:424
  51.2 26.2 %collective-permute-start.3 = (bf16[4,64,1024]{2,1,0:T(8,128)(2,1)S(1)}, bf16[4,64,1024]{2,1,0:T(8,128)(2,1)}, u32[]{:S(2)}, u32[]{:S(2)}) collective-permute-start(bf16[4,64,1024]{2,1,0:T(8,128)(2,1)S(1)} %column.2.refs_0_.refs_8_), channel_id=1, source_target_pairs={{0,8},{1,9},{2,10},{3,11},{4,12},{5,13},{6,14},{7,15},{8,16},{9,17... | collective-permute-start | bytes 1572872 | tf_op jit(solution)/shard_map/ppermute | solution.py:424
  52.5 24.9 %collective-permute-start.4 = (bf16[4,64,1024]{2,1,0:T(8,128)(2,1)S(1)}, bf16[4,64,1024]{2,1,0:T(8,128)(2,1)}, u32[]{:S(2)}, u32[]{:S(2)}) collective-permute-start(bf16[4,64,1024]{2,1,0:T(8,128)(2,1)S(1)} %column.2.refs_0_.refs_8_), channel_id=1, source_target_pairs={{0,24},{1,25},{2,26},{3,27},{4,28},{5,29},{6,30},{7,31},{8,0},{9,1... | collective-permute-start | bytes 1572872 | tf_op jit(solution)/shard_map/ppermute | solution.py:424
  53.3 24.8 %collective-permute-start.5 = (bf16[4,64,1024]{2,1,0:T(8,128)(2,1)S(1)}, bf16[4,64,1024]{2,1,0:T(8,128)(2,1)}, u32[]{:S(2)}, u32[]{:S(2)}) collective-permute-start(bf16[4,64,1024]{2,1,0:T(8,128)(2,1)S(1)} %column.2.refs_0_.refs_8_), channel_id=1, source_target_pairs={{0,16},{1,17},{2,18},{3,19},{4,20},{5,21},{6,22},{7,23},{8,24},{9,... | collective-permute-start | bytes 1572872 | tf_op jit(solution)/shard_map/ppermute | solution.py:424
  56.8 21.4 %collective-permute-start.6 = (bf16[4,64,1024]{2,1,0:T(8,128)(2,1)S(1)}, bf16[4,64,1024]{2,1,0:T(8,128)(2,1)S(1)}, u32[]{:S(2)}, u32[]{:S(2)}) collective-permute-start(bf16[4,64,1024]{2,1,0:T(8,128)(2,1)S(1)} %column.2.refs_0_.refs_8_), channel_id=1, source_target_pairs={{0,1},{1,0},{2,3},{3,2},{4,5},{5,4},{6,7},{7,6},{8,9},{9,8},{10,11... | collective-permute-start | bytes 1572872 | tf_op jit(solution)/shard_map/ppermute | solution.py:424
  57.6 30.9 %collective-permute-start.13 = (bf16[4,64,1024]{2,1,0:T(8,128)(2,1)}, bf16[4,64,1024]{2,1,0:T(8,128)(2,1)S(1)}, u32[]{:S(2)}, u32[]{:S(2)}) collective-permute-start(bf16[4,64,1024]{2,1,0:T(8,128)(2,1)} %column.3.refs_0_.refs_8_), channel_id=1, source_target_pairs={{0,8},{1,9},{2,10},{3,11},{4,12},{5,13},{6,14},{7,15},{8,16},{9,17... | collective-permute-start | bytes 1572872 | tf_op jit(solution)/shard_map/ppermute | solution.py:424
  77.4 17.3 %collective-permute-start.14 = (bf16[4,64,1024]{2,1,0:T(8,128)(2,1)}, bf16[4,64,1024]{2,1,0:T(8,128)(2,1)}, u32[]{:S(2)}, u32[]{:S(2)}) collective-permute-start(bf16[4,64,1024]{2,1,0:T(8,128)(2,1)} %column.3.refs_0_.refs_8_), channel_id=1, source_target_pairs={{0,24},{1,25},{2,26},{3,27},{4,28},{5,29},{6,30},{7,31},{8,0},{9,1... | collective-permute-start | bytes 1572872 | tf_op jit(solution)/shard_map/ppermute | solution.py:424
  77.4 20.5 %collective-permute-start.15 = (bf16[4,64,1024]{2,1,0:T(8,128)(2,1)}, bf16[4,64,1024]{2,1,0:T(8,128)(2,1)}, u32[]{:S(2)}, u32[]{:S(2)}) collective-permute-start(bf16[4,64,1024]{2,1,0:T(8,128)(2,1)} %column.3.refs_0_.refs_8_), channel_id=1, source_target_pairs={{0,16},{1,17},{2,18},{3,19},{4,20},{5,21},{6,22},{7,23},{8,24},{9,... | collective-permute-start | bytes 1572872 | tf_op jit(solution)/shard_map/ppermute | solution.py:424
  78.2 19.8 %collective-permute-start.7 = (bf16[4,64,1024]{2,1,0:T(8,128)(2,1)}, bf16[4,64,1024]{2,1,0:T(8,128)(2,1)}, u32[]{:S(2)}, u32[]{:S(2)}) collective-permute-start(bf16[4,64,1024]{2,1,0:T(8,128)(2,1)} %collective-permute-done.3.refs_1_.refs_9_), channel_id=1, source_target_pairs={{0,1},{1,0},{2,3},{3,2},{4,5},{5,4},{6,7},{7,6},{8,9},{9,8},{10,11... | collective-permute-start | bytes 1572872 | tf_op jit(solution)/shard_map/ppermute | solution.py:424
  79.0 19.5 %collective-permute-start.8 = (bf16[4,64,1024]{2,1,0:T(8,128)(2,1)}, bf16[4,64,1024]{2,1,0:T(8,128)(2,1)}, u32[]{:S(2)}, u32[]{:S(2)}) collective-permute-start(bf16[4,64,1024]{2,1,0:T(8,128)(2,1)} %collective-permute-done.4.refs_2_.refs_10_), channel_id=1, source_target_pairs={{0,1},{1,0},{2,3},{3,2},{4,5},{5,4},{6,7},{7,6},{8,9},{9,8},{10,11... | collective-permute-start | bytes 1572872 | tf_op jit(solution)/shard_map/ppermute | solution.py:424
  89.4 9.2 %collective-permute-start.9 = (bf16[4,64,1024]{2,1,0:T(8,128)(2,1)}, bf16[4,64,1024]{2,1,0:T(8,128)(2,1)}, u32[]{:S(2)}, u32[]{:S(2)}) collective-permute-start(bf16[4,64,1024]{2,1,0:T(8,128)(2,1)} %collective-permute-done.5.refs_3_.refs_11_), channel_id=1, source_target_pairs={{0,1},{1,0},{2,3},{3,2},{4,5},{5,4},{6,7},{7,6},{8,9},{9,8},{10,11... | collective-permute-start | bytes 1572872 | tf_op jit(solution)/shard_map/ppermute | solution.py:424
  92.9 5.7 %copy-start.13 = (bf16[4,64,1024]{2,1,0:T(8,128)(2,1)S(1)}, bf16[4,64,1024]{2,1,0:T(8,128)(2,1)}, u32[]{:S(2)}) copy-start(bf16[4,64,1024]{2,1,0:T(8,128)(2,1)} %copy-done.12) | copy-start | bytes 1572868
  94.7 18.7 %collective-permute-start.16 = (bf16[4,64,1024]{2,1,0:T(8,128)(2,1)}, bf16[4,64,1024]{2,1,0:T(8,128)(2,1)S(1)}, u32[]{:S(2)}, u32[]{:S(2)}) collective-permute-start(bf16[4,64,1024]{2,1,0:T(8,128)(2,1)} %column.3.refs_0_.refs_8_), channel_id=1, source_target_pairs={{0,1},{1,0},{2,3},{3,2},{4,5},{5,4},{6,7},{7,6},{8,9},{9,8},{10,11... | collective-permute-start | bytes 1572872 | tf_op jit(solution)/shard_map/ppermute | solution.py:424
  97.9 15.4 %collective-permute-start.17 = (bf16[4,64,1024]{2,1,0:T(8,128)(2,1)S(1)}, bf16[4,64,1024]{2,1,0:T(8,128)(2,1)S(1)}, u32[]{:S(2)}, u32[]{:S(2)}) collective-permute-start(bf16[4,64,1024]{2,1,0:T(8,128)(2,1)S(1)} %copy-done.11), channel_id=1, source_target_pairs={{0,1},{1,0},{2,3},{3,2},{4,5},{5,4},{6,7},{7,6},{8,9},{9,8},{10,11... | collective-permute-start | bytes 1572872 | tf_op jit(solution)/shard_map/ppermute | solution.py:424
  97.9 15.4 %collective-permute-start.18 = (bf16[4,64,1024]{2,1,0:T(8,128)(2,1)}, bf16[4,64,1024]{2,1,0:T(8,128)(2,1)S(1)}, u32[]{:S(2)}, u32[]{:S(2)}) collective-permute-start(bf16[4,64,1024]{2,1,0:T(8,128)(2,1)} %collective-permute-done.14.refs_2_.refs_10_), channel_id=1, source_target_pairs={{0,1},{1,0},{2,3},{3,2},{4,5},{5,4},{6,7},{7,6},{8,9},{9,8},{10,11... | collective-permute-start | bytes 1572872 | tf_op jit(solution)/shard_map/ppermute | solution.py:424
  98.4 14.9 %collective-permute-start.19 = (bf16[4,64,1024]{2,1,0:T(8,128)(2,1)}, bf16[4,64,1024]{2,1,0:T(8,128)(2,1)S(1)}, u32[]{:S(2)}, u32[]{:S(2)}) collective-permute-start(bf16[4,64,1024]{2,1,0:T(8,128)(2,1)} %collective-permute-done.15.refs_3_.refs_11_), channel_id=1, source_target_pairs={{0,1},{1,0},{2,3},{3,2},{4,5},{5,4},{6,7},{7,6},{8,9},{9,8},{10,11... | collective-permute-start | bytes 1572872 | tf_op jit(solution)/shard_map/ppermute | solution.py:424
  162.9 7.0 %collective-permute-start.20 = (bf16[4,104,128]{2,1,0:T(8,128)(2,1)S(1)}, bf16[4,104,128]{2,1,0:T(8,128)(2,1)S(1)}, u32[]{:S(2)}, u32[]{:S(2)}) collective-permute-start(bf16[4,104,128]{2,1,0:T(8,128)(2,1)S(1)} %get-tuple-element.44), channel_id=1, source_target_pairs={{0,64},{32,96},{64,128},{96,160},{128,192},{160,224},{192,0},{224,... | collective-permute-start | bytes 319496 | tf_op jit(solution)/shard_map/ppermute | solution.py:408
  164.5 8.9 %collective-permute-start.21 = (bf16[4,104,128]{2,1,0:T(8,128)(2,1)S(1)}, bf16[4,104,128]{2,1,0:T(8,128)(2,1)S(1)}, u32[]{:S(2)}, u32[]{:S(2)}) collective-permute-start(bf16[4,104,128]{2,1,0:T(8,128)(2,1)S(1)} %get-tuple-element.45), channel_id=1, source_target_pairs={{0,128},{32,160},{64,192},{96,224},{128,0},{160,32},{192,64},{224,... | collective-permute-start | bytes 319496 | tf_op jit(solution)/shard_map/ppermute | solution.py:408
  167.4 6.0 %collective-permute-start.22 = (bf16[4,104,128]{2,1,0:T(8,128)(2,1)S(1)}, bf16[4,104,128]{2,1,0:T(8,128)(2,1)S(1)}, u32[]{:S(2)}, u32[]{:S(2)}) collective-permute-start(bf16[4,104,128]{2,1,0:T(8,128)(2,1)S(1)} %get-tuple-element.46), channel_id=1, source_target_pairs={{0,192},{32,224},{64,0},{96,32},{128,64},{160,96},{192,128},{224,1... | collective-permute-start | bytes 319496 | tf_op jit(solution)/shard_map/ppermute | solution.py:408
  173.5 11.3 %collective-permute-start.23 = (bf16[4,104,128]{2,1,0:T(8,128)(2,1)S(1)}, bf16[4,104,128]{2,1,0:T(8,128)(2,1)S(1)}, u32[]{:S(2)}, u32[]{:S(2)}) collective-permute-start(bf16[4,104,128]{2,1,0:T(8,128)(2,1)S(1)} %shard_map.132.a_ref), channel_id=1, source_target_pairs={{0,32},{32,0},{64,96},{96,64},{128,160},{160,128},{192,224},{224,1... | collective-permute-start | bytes 319496 | tf_op jit(solution)/shard_map/ppermute | solution.py:412
  184.8 7.1 %collective-permute-start.24 = (bf16[4,104,128]{2,1,0:T(8,128)(2,1)S(1)}, bf16[4,104,128]{2,1,0:T(8,128)(2,1)S(1)}, u32[]{:S(2)}, u32[]{:S(2)}) collective-permute-start(bf16[4,104,128]{2,1,0:T(8,128)(2,1)S(1)} %shard_map.133.q0_ref), channel_id=1, source_target_pairs={{0,64},{32,96},{64,128},{96,160},{128,192},{160,224},{192,0},{224,... | collective-permute-start | bytes 319496 | tf_op jit(solution)/shard_map/ppermute | solution.py:408
  186.0 7.1 %collective-permute-start.25 = (bf16[4,104,128]{2,1,0:T(8,128)(2,1)S(1)}, bf16[4,104,128]{2,1,0:T(8,128)(2,1)S(1)}, u32[]{:S(2)}, u32[]{:S(2)}) collective-permute-start(bf16[4,104,128]{2,1,0:T(8,128)(2,1)S(1)} %shard_map.133.q0_ref), channel_id=1, source_target_pairs={{0,128},{32,160},{64,192},{96,224},{128,0},{160,32},{192,64},{224,... | collective-permute-start | bytes 319496 | tf_op jit(solution)/shard_map/ppermute | solution.py:408
  188.7 4.8 %collective-permute-start.26 = (bf16[4,104,128]{2,1,0:T(8,128)(2,1)S(1)}, bf16[4,104,128]{2,1,0:T(8,128)(2,1)S(1)}, u32[]{:S(2)}, u32[]{:S(2)}) collective-permute-start(bf16[4,104,128]{2,1,0:T(8,128)(2,1)S(1)} %shard_map.133.q0_ref), channel_id=1, source_target_pairs={{0,192},{32,224},{64,0},{96,32},{128,64},{160,96},{192,128},{224,1... | collective-permute-start | bytes 319496 | tf_op jit(solution)/shard_map/ppermute | solution.py:408
  (10 other events, 13.6 us)

commit v5 on v4

--- a/solution.py
+++ b/solution.py
@@ -424,9 +424,9 @@
     return lax.ppermute(value, "wide", pairs)
 
 
-def gather_part(mine):
+def gather_part(mine, part):
     moved = [wide_move(mine, 0, s, 0) for s in (1, 2, 3)]
-    column = column_of([mine] + moved)
+    column = jnp.stack([mine] + moved) if part else column_of([mine] + moved)
     return [column] + [wide_move(column, s, 0, 0) for s in (1, 3, 2)]
 
 
@@ -442,7 +442,7 @@
     mine = lax.all_to_all(sent, "wide", 0, 0, tiled=True)
     parts = []
     for part in range(2):
-        pieces = gather_part(prompts[part])
+        pieces = gather_part(prompts[part], part)
         parts.append(pieces + [wide_move(piece, 0, 0, 1) for piece in pieces])
     q, own, cg, low, up_out, pairs = prep(
         mine, candidate_hidden, frozen_query, candidate_key_value, output_cotangent,

time: 197 us -> 197 us (level)
  starting transfers between devices: 39 us -> 52.2 us
  waiting for transfers between devices: 76.5 us -> 63.3 us
    ppermute x20, waiting for transfers between devices: 61.8 us -> 48.6 us  [wide_move(): return lax.ppermute(value, 'wide', pairs)]
    ppermute x20, starting transfers between devices: 14 us -> 27.2 us  [wide_move(): return lax.ppermute(value, 'wide', pairs)]
  transfers between devices with their start and end apart: 28 -> 28, of which waited for: 12 -> 13; matrix products, arithmetic and copies ran while one was open for 0% -> 0% of each run, Pallas kernels for 9% -> 8%
where the time goes in v5:
time: 197 us; the launch traced here: 195 us
  waiting for transfers between devices  63.3 us (32%)
  starting transfers between devices  52.2 us (26%)
  Pallas kernels  37.7 us (19%)
  blocking collectives  31.6 us (16%)
  local copies, waits for them, and re-layouts  7.87 us (4%)
    ppermute x20, waiting for transfers between devices, wide_move(): return lax.ppermute(value, 'wide', pairs)  48.6 us
    all_to_all x1, blocking collectives, step(): back = lax.all_to_all(blocks, 'wide', 0, 0, tiled=True)  31.6 us
    pallas_call x2, Pallas kernels, attention_call(): pl.pallas_call(attention_kernel, grid=(4,), out_shape=(jax.ShapeDtypeStru...  29.6 us
    ppermute x20, starting transfers between devices, wide_move(): return lax.ppermute(value, 'wide', pairs)  27.2 us
    ppermute x6, starting transfers between devices, y_shift(): return lax.ppermute(value, 'prompt', pairs)  11.2 us
    all_to_all x1, starting transfers between devices, step(): mine = lax.all_to_all(sent, 'wide', 0, 0, tiled=True)  9.17 us
    ppermute x6, waiting for transfers between devices, y_shift(): return lax.ppermute(value, 'prompt', pairs)  7.97 us
    unnamed x28, local copies, waits for them, and re-layouts  7.87 us
  transfers between devices with their start and end apart: 28, of which 13 were waited for; matrix products, arithmetic and copies ran while one was open for 0% of the time, Pallas kernels for 8%

profile of v5, /device:TPU:4, one launch (start us, length us, event | category | flops | bytes accessed | tf_op | source)
XLA Modules:
  0.0 195.0 jit_solution(18378445459652669035)
XLA Ops:
  4.1 1.6 pack.1
  5.7 9.2 %all-to-all-start = ((bf16[32,104,128]{2,1,0:T(8,128)(2,1)}), bf16[32,104,128]{2,1,0:T(8,128)(2,1)S(1)}, u32[]{:S(2)}, u32[]{:S(2)}) async-start(bf16[32,104,128]{2,1,0:T(8,128)(2,1)} %get-tuple-element.26), calls=%async_computation | async-start | bytes 1703936 | tf_op jit(solution)/shard_map/all_to_all | solution.py:442
  14.9 1.5 collective-permute-start
  16.4 2.4 %collective-permute-start.1 = (bf16[64,1024]{1,0:T(8,128)(2,1)S(1)}, bf16[64,1024]{1,0:T(8,128)(2,1)S(1)}, u32[]{:S(2)}, u32[]{:S(2)}) collective-permute-start(bf16[64,1024]{1,0:T(8,128)(2,1)S(1)} %get-tuple-element.33.a_ref), channel_id=1, source_target_pairs={{0,4},{1,5},{2,6},{3,7},{4,0},{5,1},{6,2},{7,3},{8,12},{9,13},{10,... | collective-permute-start | bytes 393224 | tf_op jit(solution)/shard_map/ppermute | solution.py:424
  18.8 1.4 collective-permute-start.2
  20.8 1.5 collective-permute-start.11
  22.3 14.0 %collective-permute-done.b_ref = bf16[64,1024]{1,0:T(8,128)(2,1)S(1)} collective-permute-done((bf16[64,1024]{1,0:T(8,128)(2,1)S(1)}, bf16[64,1024]{1,0:T(8,128)(2,1)S(1)}, u32[]{:S(2)}, u32[]{:S(2)}) %collective-permute-start) | collective-permute-done | bytes 131104 | tf_op jit(solution)/shard_map/ppermute | solution.py:424
  36.3 13.0 %collective-permute-start.10 = (bf16[64,1024]{1,0:T(8,128)(2,1)S(1)}, bf16[64,1024]{1,0:T(8,128)(2,1)S(1)}, u32[]{:S(2)}, u32[]{:S(2)}) collective-permute-start(bf16[64,1024]{1,0:T(8,128)(2,1)S(1)} %get-tuple-element.38), channel_id=1, source_target_pairs={{0,2},{1,3},{2,4},{3,5},{4,6},{5,7},{6,0},{7,1},{8,10},{9,11},{10,... | collective-permute-start | bytes 393224 | tf_op jit(solution)/shard_map/ppermute | solution.py:424
  49.3 1.8 collective-permute-done.1.c_ref
  51.2 1.3 collective-permute-start.3
  53.3 1.8 collective-permute-start.5
  55.1 4.0 %collective-permute-done.11 = bf16[64,1024]{1,0:T(8,128)(2,1)S(1)} collective-permute-done((bf16[64,1024]{1,0:T(8,128)(2,1)S(1)}, bf16[64,1024]{1,0:T(8,128)(2,1)S(1)}, u32[]{:S(2)}, u32[]{:S(2)}) %collective-permute-start.11) | collective-permute-done | bytes 131104 | tf_op jit(solution)/shard_map/ppermute | solution.py:424
  59.9 1.2 collective-permute-start.13
  61.1 15.2 %collective-permute-done.3.refs_1_.refs_9_ = bf16[4,64,1024]{2,1,0:T(8,128)(2,1)} collective-permute-done((bf16[4,64,1024]{2,1,0:T(8,128)(2,1)S(1)}, bf16[4,64,1024]{2,1,0:T(8,128)(2,1)}, u32[]{:S(2)}, u32[]{:S(2)}) %collective-permute-start.3) | collective-permute-done | bytes 524320 | tf_op jit(solution)/shard_map/ppermute | solution.py:424
  78.8 9.8 %collective-permute-done.13.refs_1_.refs_9_ = bf16[4,64,1024]{2,1,0:T(8,128)(2,1)S(1)} collective-permute-done((bf16[4,64,1024]{2,1,0:T(8,128)(2,1)}, bf16[4,64,1024]{2,1,0:T(8,128)(2,1)S(1)}, u32[]{:S(2)}, u32[]{:S(2)}) %collective-permute-start.13) | collective-permute-done | bytes 524320 | tf_op jit(solution)/shard_map/ppermute | solution.py:424
  90.6 1.2 copy-done.3
  92.9 1.8 prep.1
  95.2 2.7 %collective-permute-done.15.refs_3_.refs_11_ = bf16[4,64,1024]{2,1,0:T(8,128)(2,1)} collective-permute-done((bf16[4,64,1024]{2,1,0:T(8,128)(2,1)}, bf16[4,64,1024]{2,1,0:T(8,128)(2,1)}, u32[]{:S(2)}, u32[]{:S(2)}) %collective-permute-start.15) | collective-permute-done | bytes 524320 | tf_op jit(solution)/shard_map/ppermute | solution.py:424
  98.5 14.8 %shard_map.130 = (bf16[128,2048]{1,0:T(8,128)(2,1)S(1)}, bf16[128,2048]{1,0:T(8,128)(2,1)S(1)}, bf16[128,512]{1,0:T(8,128)(2,1)S(1)}, bf16[128,512]{1,0:T(8,128)(2,1)S(1)}) custom-call(s32[8]{0:T(128)S(1)} %get-tuple-element.25.limit_ref.lane_ref, bf16[128,4096]{1,0:T(8,128)(2,1)S(1)} %get-tuple-element.30.q_ref, ...), custom_call_target="tpu_custom_call" | custom-call | flops 12000000000 | bytes 8000000 | tf_op jit(solution)/shard_map/pallas_call | solution.py:246
  113.4 14.8 %shard_map.131 = (bf16[128,2048]{1,0:T(8,128)(2,1)S(1)}, bf16[128,2048]{1,0:T(8,128)(2,1)S(1)}, bf16[128,512]{1,0:T(8,128)(2,1)S(1)}, bf16[128,512]{1,0:T(8,128)(2,1)S(1)}) custom-call(s32[8]{0:T(128)S(1)} %get-tuple-element.25.limit_ref.lane_ref, bf16[128,4096]{1,0:T(8,128)(2,1)S(1)} %get-tuple-element.30.q_ref, ...), custom_call_target="tpu_custom_call" | custom-call | flops 12000000000 | bytes 8000000 | tf_op jit(solution)/shard_map/pallas_call | solution.py:246
  128.2 2.1 %grads.1 = bf16[32,104,128]{2,1,0:T(8,128)(2,1)S(1)} custom-call(bf16[32,104,128]{2,1,0:T(8,128)(2,1)S(1)} %all-to-all-done.mine_ref, bf16[1,128,4096]{2,1,0:T(8,128)(2,1)S(1)} %copy-done, bf16[1,128,4096]{2,1,0:T(8,128)(2,1)S(1)} %copy-done.1, bf16[48,128]{1,0:T(8,128)(2,1)S(1)} %get-tuple-element.27.low_ref, ...), custom_call_target="tpu_custom_call" | custom-call | tf_op jit(solution)/shard_map/grads/pallas_call | solution.py:311
  130.3 31.6 %all_to_all.10.back_ref = bf16[32,104,128]{2,1,0:T(8,128)(2,1)S(1)} all-to-all(bf16[32,104,128]{2,1,0:T(8,128)(2,1)S(1)} %grads.1), channel_id=1, replica_groups=mesh['prompt'=8,'wide'=32] {'wide'}, dimensions={0} | all-to-all | bytes 1703936 | tf_op jit(solution)/shard_map/all_to_all | solution.py:455
  162.9 1.6 collective-permute-start.20
  164.5 2.9 %collective-permute-start.21 = (bf16[4,104,128]{2,1,0:T(8,128)(2,1)S(1)}, bf16[4,104,128]{2,1,0:T(8,128)(2,1)S(1)}, u32[]{:S(2)}, u32[]{:S(2)}) collective-permute-start(bf16[4,104,128]{2,1,0:T(8,128)(2,1)S(1)} %get-tuple-element.45), channel_id=1, source_target_pairs={{0,128},{32,160},{64,192},{96,224},{128,0},{160,32},{192,64},{224,... | collective-permute-start | bytes 319496 | tf_op jit(solution)/shard_map/ppermute | solution.py:408
  167.4 1.3 collective-permute-start.22
  169.8 3.6 %collective-permute-done.21.r2_ref = bf16[4,104,128]{2,1,0:T(8,128)(2,1)S(1)} collective-permute-done((bf16[4,104,128]{2,1,0:T(8,128)(2,1)S(1)}, bf16[4,104,128]{2,1,0:T(8,128)(2,1)S(1)}, u32[]{:S(2)}, u32[]{:S(2)}) %collective-permute-start.21) | collective-permute-done | bytes 106528 | tf_op jit(solution)/shard_map/ppermute | solution.py:408
  173.5 4.6 %collective-permute-start.23 = (bf16[4,104,128]{2,1,0:T(8,128)(2,1)S(1)}, bf16[4,104,128]{2,1,0:T(8,128)(2,1)S(1)}, u32[]{:S(2)}, u32[]{:S(2)}) collective-permute-start(bf16[4,104,128]{2,1,0:T(8,128)(2,1)S(1)} %shard_map.132.a_ref), channel_id=1, source_target_pairs={{0,32},{32,0},{64,96},{96,64},{128,160},{160,128},{192,224},{224,1... | collective-permute-start | bytes 319496 | tf_op jit(solution)/shard_map/ppermute | solution.py:412
  178.1 6.7 %collective-permute-done.23.b_ref = bf16[4,104,128]{2,1,0:T(8,128)(2,1)S(1)} collective-permute-done((bf16[4,104,128]{2,1,0:T(8,128)(2,1)S(1)}, bf16[4,104,128]{2,1,0:T(8,128)(2,1)S(1)}, u32[]{:S(2)}, u32[]{:S(2)}) %collective-permute-start.23) | collective-permute-done | bytes 106528 | tf_op jit(solution)/shard_map/ppermute | solution.py:412
  186.0 2.7 %collective-permute-start.25 = (bf16[4,104,128]{2,1,0:T(8,128)(2,1)S(1)}, bf16[4,104,128]{2,1,0:T(8,128)(2,1)S(1)}, u32[]{:S(2)}, u32[]{:S(2)}) collective-permute-start(bf16[4,104,128]{2,1,0:T(8,128)(2,1)S(1)} %shard_map.133.q0_ref), channel_id=1, source_target_pairs={{0,128},{32,160},{64,192},{96,224},{128,0},{160,32},{192,64},{224,... | collective-permute-start | bytes 319496 | tf_op jit(solution)/shard_map/ppermute | solution.py:408
  188.7 1.4 collective-permute-start.26
  190.1 1.8 collective-permute-done.24.q1_ref
  193.4 1.5 unpack.1
  (65 shorter events, 16.6 us)
Async XLA Ops:
  5.7 9.2 %copy-start.6 = (bf16[1,64,2048]{2,1,0:T(8,128)(2,1)S(1)}, bf16[1,64,2048]{2,1,0:T(8,128)(2,1)}, u32[]{:S(2)}) copy-start(bf16[1,64,2048]{2,1,0:T(8,128)(2,1)} %prompt_ref.1) | copy-start | bytes 786436
  5.7 83.7 %all-to-all-start = ((bf16[32,104,128]{2,1,0:T(8,128)(2,1)}), bf16[32,104,128]{2,1,0:T(8,128)(2,1)S(1)}, u32[]{:S(2)}, u32[]{:S(2)}) async-start(bf16[32,104,128]{2,1,0:T(8,128)(2,1)} %get-tuple-element.26), calls=%async_computation | async-start | bytes 1703936 | tf_op jit(solution)/shard_map/all_to_all | solution.py:442
  14.9 21.4 %collective-permute-start = (bf16[64,1024]{1,0:T(8,128)(2,1)S(1)}, bf16[64,1024]{1,0:T(8,128)(2,1)S(1)}, u32[]{:S(2)}, u32[]{:S(2)}) collective-permute-start(bf16[64,1024]{1,0:T(8,128)(2,1)S(1)} %get-tuple-element.33.a_ref), channel_id=1, source_target_pairs={{0,2},{1,3},{2,4},{3,5},{4,6},{5,7},{6,0},{7,1},{8,10},{9,11},{10,... | collective-permute-start | bytes 393224 | tf_op jit(solution)/shard_map/ppermute | solution.py:424
  16.4 34.7 %collective-permute-start.1 = (bf16[64,1024]{1,0:T(8,128)(2,1)S(1)}, bf16[64,1024]{1,0:T(8,128)(2,1)S(1)}, u32[]{:S(2)}, u32[]{:S(2)}) collective-permute-start(bf16[64,1024]{1,0:T(8,128)(2,1)S(1)} %get-tuple-element.33.a_ref), channel_id=1, source_target_pairs={{0,4},{1,5},{2,6},{3,7},{4,0},{5,1},{6,2},{7,3},{8,12},{9,13},{10,... | collective-permute-start | bytes 393224 | tf_op jit(solution)/shard_map/ppermute | solution.py:424
  18.8 32.3 %collective-permute-start.2 = (bf16[64,1024]{1,0:T(8,128)(2,1)S(1)}, bf16[64,1024]{1,0:T(8,128)(2,1)S(1)}, u32[]{:S(2)}, u32[]{:S(2)}) collective-permute-start(bf16[64,1024]{1,0:T(8,128)(2,1)S(1)} %get-tuple-element.33.a_ref), channel_id=1, source_target_pairs={{0,6},{1,7},{2,0},{3,1},{4,2},{5,3},{6,4},{7,5},{8,14},{9,15},{10,... | collective-permute-start | bytes 393224 | tf_op jit(solution)/shard_map/ppermute | solution.py:424
  20.3 69.1 %copy-start = (bf16[1,128,4096]{2,1,0:T(8,128)(2,1)S(1)}, bf16[1,128,4096]{2,1,0:T(8,128)(2,1)}, u32[]{:S(2)}) copy-start(bf16[1,128,4096]{2,1,0:T(8,128)(2,1)} %x_ref.3) | copy-start | bytes 3145732
  20.3 69.1 %copy-start.1 = (bf16[1,128,4096]{2,1,0:T(8,128)(2,1)S(1)}, bf16[1,128,4096]{2,1,0:T(8,128)(2,1)}, u32[]{:S(2)}) copy-start(bf16[1,128,4096]{2,1,0:T(8,128)(2,1)} %oc_ref.3) | copy-start | bytes 3145732
  20.3 33.0 %collective-permute-start.12 = (bf16[64,1024]{1,0:T(8,128)(2,1)S(1)}, bf16[64,1024]{1,0:T(8,128)(2,1)S(1)}, u32[]{:S(2)}, u32[]{:S(2)}) collective-permute-start(bf16[64,1024]{1,0:T(8,128)(2,1)S(1)} %get-tuple-element.38), channel_id=1, source_target_pairs={{0,6},{1,7},{2,0},{3,1},{4,2},{5,3},{6,4},{7,5},{8,14},{9,15},{10,... | collective-permute-start | bytes 393224 | tf_op jit(solution)/shard_map/ppermute | solution.py:424
  20.8 38.2 %collective-permute-start.11 = (bf16[64,1024]{1,0:T(8,128)(2,1)S(1)}, bf16[64,1024]{1,0:T(8,128)(2,1)S(1)}, u32[]{:S(2)}, u32[]{:S(2)}) collective-permute-start(bf16[64,1024]{1,0:T(8,128)(2,1)S(1)} %get-tuple-element.38), channel_id=1, source_target_pairs={{0,4},{1,5},{2,6},{3,7},{4,0},{5,1},{6,2},{7,3},{8,12},{9,13},{10,... | collective-permute-start | bytes 393224 | tf_op jit(solution)/shard_map/ppermute | solution.py:424
  36.3 22.7 %collective-permute-start.10 = (bf16[64,1024]{1,0:T(8,128)(2,1)S(1)}, bf16[64,1024]{1,0:T(8,128)(2,1)S(1)}, u32[]{:S(2)}, u32[]{:S(2)}) collective-permute-start(bf16[64,1024]{1,0:T(8,128)(2,1)S(1)} %get-tuple-element.38), channel_id=1, source_target_pairs={{0,2},{1,3},{2,4},{3,5},{4,6},{5,7},{6,0},{7,1},{8,10},{9,11},{10,... | collective-permute-start | bytes 393224 | tf_op jit(solution)/shard_map/ppermute | solution.py:424
  51.2 25.1 %collective-permute-start.3 = (bf16[4,64,1024]{2,1,0:T(8,128)(2,1)S(1)}, bf16[4,64,1024]{2,1,0:T(8,128)(2,1)}, u32[]{:S(2)}, u32[]{:S(2)}) collective-permute-start(bf16[4,64,1024]{2,1,0:T(8,128)(2,1)S(1)} %column.1.refs_0_.refs_8_), channel_id=1, source_target_pairs={{0,8},{1,9},{2,10},{3,11},{4,12},{5,13},{6,14},{7,15},{8,16},{9,17... | collective-permute-start | bytes 1572872 | tf_op jit(solution)/shard_map/ppermute | solution.py:424
  52.5 23.8 %collective-permute-start.4 = (bf16[4,64,1024]{2,1,0:T(8,128)(2,1)S(1)}, bf16[4,64,1024]{2,1,0:T(8,128)(2,1)}, u32[]{:S(2)}, u32[]{:S(2)}) collective-permute-start(bf16[4,64,1024]{2,1,0:T(8,128)(2,1)S(1)} %column.1.refs_0_.refs_8_), channel_id=1, source_target_pairs={{0,24},{1,25},{2,26},{3,27},{4,28},{5,29},{6,30},{7,31},{8,0},{9,1... | collective-permute-start | bytes 1572872 | tf_op jit(solution)/shard_map/ppermute | solution.py:424
  53.3 24.1 %collective-permute-start.5 = (bf16[4,64,1024]{2,1,0:T(8,128)(2,1)S(1)}, bf16[4,64,1024]{2,1,0:T(8,128)(2,1)}, u32[]{:S(2)}, u32[]{:S(2)}) collective-permute-start(bf16[4,64,1024]{2,1,0:T(8,128)(2,1)S(1)} %column.1.refs_0_.refs_8_), channel_id=1, source_target_pairs={{0,16},{1,17},{2,18},{3,19},{4,20},{5,21},{6,22},{7,23},{8,24},{9,... | collective-permute-start | bytes 1572872 | tf_op jit(solution)/shard_map/ppermute | solution.py:424
  59.0 18.4 %collective-permute-start.6 = (bf16[4,64,1024]{2,1,0:T(8,128)(2,1)S(1)}, bf16[4,64,1024]{2,1,0:T(8,128)(2,1)S(1)}, u32[]{:S(2)}, u32[]{:S(2)}) collective-permute-start(bf16[4,64,1024]{2,1,0:T(8,128)(2,1)S(1)} %column.1.refs_0_.refs_8_), channel_id=1, source_target_pairs={{0,1},{1,0},{2,3},{3,2},{4,5},{5,4},{6,7},{7,6},{8,9},{9,8},{10,11... | collective-permute-start | bytes 1572872 | tf_op jit(solution)/shard_map/ppermute | solution.py:424
  59.9 28.7 %collective-permute-start.13 = (bf16[4,64,1024]{2,1,0:T(8,128)(2,1)}, bf16[4,64,1024]{2,1,0:T(8,128)(2,1)S(1)}, u32[]{:S(2)}, u32[]{:S(2)}) collective-permute-start(bf16[4,64,1024]{2,1,0:T(8,128)(2,1)} %pad_maximum_fusion.refs_0_.refs_8_), channel_id=1, source_target_pairs={{0,8},{1,9},{2,10},{3,11},{4,12},{5,13},{6,14},{7,15},{8,16},{9,17... | collective-permute-start | bytes 1572872 | tf_op jit(solution)/shard_map/ppermute | solution.py:424
  76.3 18.3 %collective-permute-start.14 = (bf16[4,64,1024]{2,1,0:T(8,128)(2,1)}, bf16[4,64,1024]{2,1,0:T(8,128)(2,1)}, u32[]{:S(2)}, u32[]{:S(2)}) collective-permute-start(bf16[4,64,1024]{2,1,0:T(8,128)(2,1)} %pad_maximum_fusion.refs_0_.refs_8_), channel_id=1, source_target_pairs={{0,24},{1,25},{2,26},{3,27},{4,28},{5,29},{6,30},{7,31},{8,0},{9,1... | collective-permute-start | bytes 1572872 | tf_op jit(solution)/shard_map/ppermute | solution.py:424
  76.3 21.6 %collective-permute-start.15 = (bf16[4,64,1024]{2,1,0:T(8,128)(2,1)}, bf16[4,64,1024]{2,1,0:T(8,128)(2,1)}, u32[]{:S(2)}, u32[]{:S(2)}) collective-permute-start(bf16[4,64,1024]{2,1,0:T(8,128)(2,1)} %pad_maximum_fusion.refs_0_.refs_8_), channel_id=1, source_target_pairs={{0,16},{1,17},{2,18},{3,19},{4,20},{5,21},{6,22},{7,23},{8,24},{9,... | collective-permute-start | bytes 1572872 | tf_op jit(solution)/shard_map/ppermute | solution.py:424
  77.5 20.5 %collective-permute-start.7 = (bf16[4,64,1024]{2,1,0:T(8,128)(2,1)}, bf16[4,64,1024]{2,1,0:T(8,128)(2,1)}, u32[]{:S(2)}, u32[]{:S(2)}) collective-permute-start(bf16[4,64,1024]{2,1,0:T(8,128)(2,1)} %collective-permute-done.3.refs_1_.refs_9_), channel_id=1, source_target_pairs={{0,1},{1,0},{2,3},{3,2},{4,5},{5,4},{6,7},{7,6},{8,9},{9,8},{10,11... | collective-permute-start | bytes 1572872 | tf_op jit(solution)/shard_map/ppermute | solution.py:424
  78.3 20.2 %collective-permute-start.8 = (bf16[4,64,1024]{2,1,0:T(8,128)(2,1)}, bf16[4,64,1024]{2,1,0:T(8,128)(2,1)}, u32[]{:S(2)}, u32[]{:S(2)}) collective-permute-start(bf16[4,64,1024]{2,1,0:T(8,128)(2,1)} %collective-permute-done.4.refs_2_.refs_10_), channel_id=1, source_target_pairs={{0,1},{1,0},{2,3},{3,2},{4,5},{5,4},{6,7},{7,6},{8,9},{9,8},{10,11... | collective-permute-start | bytes 1572872 | tf_op jit(solution)/shard_map/ppermute | solution.py:424
  89.4 9.2 %collective-permute-start.9 = (bf16[4,64,1024]{2,1,0:T(8,128)(2,1)}, bf16[4,64,1024]{2,1,0:T(8,128)(2,1)}, u32[]{:S(2)}, u32[]{:S(2)}) collective-permute-start(bf16[4,64,1024]{2,1,0:T(8,128)(2,1)} %collective-permute-done.5.refs_3_.refs_11_), channel_id=1, source_target_pairs={{0,1},{1,0},{2,3},{3,2},{4,5},{5,4},{6,7},{7,6},{8,9},{9,8},{10,11... | collective-permute-start | bytes 1572872 | tf_op jit(solution)/shard_map/ppermute | solution.py:424
  92.9 5.7 %copy-start.13 = (bf16[4,64,1024]{2,1,0:T(8,128)(2,1)S(1)}, bf16[4,64,1024]{2,1,0:T(8,128)(2,1)}, u32[]{:S(2)}) copy-start(bf16[4,64,1024]{2,1,0:T(8,128)(2,1)} %copy-done.12) | copy-start | bytes 1572868
  94.6 18.7 %collective-permute-start.16 = (bf16[4,64,1024]{2,1,0:T(8,128)(2,1)}, bf16[4,64,1024]{2,1,0:T(8,128)(2,1)S(1)}, u32[]{:S(2)}, u32[]{:S(2)}) collective-permute-start(bf16[4,64,1024]{2,1,0:T(8,128)(2,1)} %pad_maximum_fusion.refs_0_.refs_8_), channel_id=1, source_target_pairs={{0,1},{1,0},{2,3},{3,2},{4,5},{5,4},{6,7},{7,6},{8,9},{9,8},{10,11... | collective-permute-start | bytes 1572872 | tf_op jit(solution)/shard_map/ppermute | solution.py:424
  97.9 15.4 %collective-permute-start.17 = (bf16[4,64,1024]{2,1,0:T(8,128)(2,1)S(1)}, bf16[4,64,1024]{2,1,0:T(8,128)(2,1)S(1)}, u32[]{:S(2)}, u32[]{:S(2)}) collective-permute-start(bf16[4,64,1024]{2,1,0:T(8,128)(2,1)S(1)} %copy-done.11), channel_id=1, source_target_pairs={{0,1},{1,0},{2,3},{3,2},{4,5},{5,4},{6,7},{7,6},{8,9},{9,8},{10,11... | collective-permute-start | bytes 1572872 | tf_op jit(solution)/shard_map/ppermute | solution.py:424
  97.9 15.4 %collective-permute-start.18 = (bf16[4,64,1024]{2,1,0:T(8,128)(2,1)}, bf16[4,64,1024]{2,1,0:T(8,128)(2,1)S(1)}, u32[]{:S(2)}, u32[]{:S(2)}) collective-permute-start(bf16[4,64,1024]{2,1,0:T(8,128)(2,1)} %collective-permute-done.14.refs_2_.refs_10_), channel_id=1, source_target_pairs={{0,1},{1,0},{2,3},{3,2},{4,5},{5,4},{6,7},{7,6},{8,9},{9,8},{10,11... | collective-permute-start | bytes 1572872 | tf_op jit(solution)/shard_map/ppermute | solution.py:424
  98.4 14.9 %collective-permute-start.19 = (bf16[4,64,1024]{2,1,0:T(8,128)(2,1)}, bf16[4,64,1024]{2,1,0:T(8,128)(2,1)S(1)}, u32[]{:S(2)}, u32[]{:S(2)}) collective-permute-start(bf16[4,64,1024]{2,1,0:T(8,128)(2,1)} %collective-permute-done.15.refs_3_.refs_11_), channel_id=1, source_target_pairs={{0,1},{1,0},{2,3},{3,2},{4,5},{5,4},{6,7},{7,6},{8,9},{9,8},{10,11... | collective-permute-start | bytes 1572872 | tf_op jit(solution)/shard_map/ppermute | solution.py:424
  162.9 7.0 %collective-permute-start.20 = (bf16[4,104,128]{2,1,0:T(8,128)(2,1)S(1)}, bf16[4,104,128]{2,1,0:T(8,128)(2,1)S(1)}, u32[]{:S(2)}, u32[]{:S(2)}) collective-permute-start(bf16[4,104,128]{2,1,0:T(8,128)(2,1)S(1)} %get-tuple-element.44), channel_id=1, source_target_pairs={{0,64},{32,96},{64,128},{96,160},{128,192},{160,224},{192,0},{224,... | collective-permute-start | bytes 319496 | tf_op jit(solution)/shard_map/ppermute | solution.py:408
  164.5 8.9 %collective-permute-start.21 = (bf16[4,104,128]{2,1,0:T(8,128)(2,1)S(1)}, bf16[4,104,128]{2,1,0:T(8,128)(2,1)S(1)}, u32[]{:S(2)}, u32[]{:S(2)}) collective-permute-start(bf16[4,104,128]{2,1,0:T(8,128)(2,1)S(1)} %get-tuple-element.45), channel_id=1, source_target_pairs={{0,128},{32,160},{64,192},{96,224},{128,0},{160,32},{192,64},{224,... | collective-permute-start | bytes 319496 | tf_op jit(solution)/shard_map/ppermute | solution.py:408
  167.4 6.0 %collective-permute-start.22 = (bf16[4,104,128]{2,1,0:T(8,128)(2,1)S(1)}, bf16[4,104,128]{2,1,0:T(8,128)(2,1)S(1)}, u32[]{:S(2)}, u32[]{:S(2)}) collective-permute-start(bf16[4,104,128]{2,1,0:T(8,128)(2,1)S(1)} %get-tuple-element.46), channel_id=1, source_target_pairs={{0,192},{32,224},{64,0},{96,32},{128,64},{160,96},{192,128},{224,1... | collective-permute-start | bytes 319496 | tf_op jit(solution)/shard_map/ppermute | solution.py:408
  173.5 11.3 %collective-permute-start.23 = (bf16[4,104,128]{2,1,0:T(8,128)(2,1)S(1)}, bf16[4,104,128]{2,1,0:T(8,128)(2,1)S(1)}, u32[]{:S(2)}, u32[]{:S(2)}) collective-permute-start(bf16[4,104,128]{2,1,0:T(8,128)(2,1)S(1)} %shard_map.132.a_ref), channel_id=1, source_target_pairs={{0,32},{32,0},{64,96},{96,64},{128,160},{160,128},{192,224},{224,1... | collective-permute-start | bytes 319496 | tf_op jit(solution)/shard_map/ppermute | solution.py:412
  184.8 7.1 %collective-permute-start.24 = (bf16[4,104,128]{2,1,0:T(8,128)(2,1)S(1)}, bf16[4,104,128]{2,1,0:T(8,128)(2,1)S(1)}, u32[]{:S(2)}, u32[]{:S(2)}) collective-permute-start(bf16[4,104,128]{2,1,0:T(8,128)(2,1)S(1)} %shard_map.133.q0_ref), channel_id=1, source_target_pairs={{0,64},{32,96},{64,128},{96,160},{128,192},{160,224},{192,0},{224,... | collective-permute-start | bytes 319496 | tf_op jit(solution)/shard_map/ppermute | solution.py:408
  186.0 7.1 %collective-permute-start.25 = (bf16[4,104,128]{2,1,0:T(8,128)(2,1)S(1)}, bf16[4,104,128]{2,1,0:T(8,128)(2,1)S(1)}, u32[]{:S(2)}, u32[]{:S(2)}) collective-permute-start(bf16[4,104,128]{2,1,0:T(8,128)(2,1)S(1)} %shard_map.133.q0_ref), channel_id=1, source_target_pairs={{0,128},{32,160},{64,192},{96,224},{128,0},{160,32},{192,64},{224,... | collective-permute-start | bytes 319496 | tf_op jit(solution)/shard_map/ppermute | solution.py:408
  188.7 4.8 %collective-permute-start.26 = (bf16[4,104,128]{2,1,0:T(8,128)(2,1)S(1)}, bf16[4,104,128]{2,1,0:T(8,128)(2,1)S(1)}, u32[]{:S(2)}, u32[]{:S(2)}) collective-permute-start(bf16[4,104,128]{2,1,0:T(8,128)(2,1)S(1)} %shard_map.133.q0_ref), channel_id=1, source_target_pairs={{0,192},{32,224},{64,0},{96,32},{128,64},{160,96},{192,128},{224,1... | collective-permute-start | bytes 319496 | tf_op jit(solution)/shard_map/ppermute | solution.py:408
  (10 other events, 13.6 us)
